TPU v7x, 32 devices: a whole 2x2x4 slice. The times are simulated.
32 devices in a mesh: ctx: 8 (over z, x), heads: 4 (over y, core).
Axes of the slice: x: 2, y: 2, z: 4, core: 2. Of those that a mesh axis runs over, the one named last changes fastest.
Arguments:
- queries: bfloat16 [64, 128, 576], P(None, 'heads'), may hold values from -60 to 60
- latents: bfloat16 [8192, 576], P('ctx'), may hold values from -6 to 6
- index_queries: bfloat16 [64, 64, 128], P(None, 'heads'), may hold values from -24 to 24
- index_keys: bfloat16 [8192, 128], P('ctx'), may hold values from -6 to 6
- index_weights: float32 [64, 64], P(None, 'heads'), may hold values from -15 to 15
- positions: int32 [64], replicated, may hold values from 2048 to 8191, as said below
Outputs:
- grad_index_queries: float32 [64, 64, 128], P(None, 'heads')
- grad_index_keys: float32 [8192, 128], P(('ctx', 'heads'))
Inputs may be any that keep to these rules, and one draw needn't show every extreme that they name: Row q sees keys 0 to positions[q]. One row sits at 8191 and one at 2048.
All inputs are finite; a program needn't handle non-finite values.
Results may differ from a plain program's by a relative error of at most 0.0028.
Values sent between devices are 32-bit elements; how exact they have to be, the bound alone decides.
No kernel may reach another device: no remote copies, remote signals or barrier semaphores. Data moves between devices by JAX's collectives and lax.ppermute only.
A program may use at most 64 MiB of HBM per device.

v0:
```python
import math

import jax
import jax.numpy as jnp
from jax import lax
from jax.sharding import PartitionSpec as P

H = 128
HI = 64
DI = 128


score_scale = 192 ** (-0.5)
negative_fill = -1e30


def joined_2(value, axis, combine):
    everything = jax.tree.map(lambda part: lax.all_gather(part, axis), value)
    leading = jax.tree.map(lambda part: part[0], everything)

    def turn(k, so_far):
        return combine(so_far, jax.tree.map(lambda part: part[k], everything))

    return lax.fori_loop(1, lax.axis_size(axis), turn, leading)


def combine_stats(former, latter):
    joined = jnp.maximum(former[0], latter[0])
    return (
        joined,
        former[1] * jnp.exp(former[0] - joined) + latter[1] * jnp.exp(latter[0] - joined),
    )


def masked_scores(block_queries, latents, block_visible):
    row_count, head_count, width = block_queries.shape
    flattened = block_queries.reshape(row_count * head_count, width)
    products = lax.dot_general(
        flattened, latents, (((1,), (1,)), ((), ())), preferred_element_type=jnp.float32
    )
    products = products.reshape(row_count, head_count, -1) * score_scale
    return jnp.where(block_visible[:, None, :], products, negative_fill)


def local_stats(logits, visible_now):
    masked = jnp.where(visible_now, logits, negative_fill)
    row_peak = jnp.max(masked, axis=1)
    row_mass = jnp.sum(jnp.where(visible_now, jnp.exp(masked - row_peak[:, None]), 0.0), axis=1)
    return (masked, row_peak, row_mass)


def gradient_of(masked, visible_now, row_peak, row_mass, target_sum, loss_scale):
    index_probs = jnp.where(
        visible_now, jnp.exp(masked - row_peak[:, None]) / row_mass[:, None], 0.0
    )
    return loss_scale * (index_probs - target_sum * (1.0 / H))


def body(queries, latents, index_queries, index_keys, index_weights, positions):
    row_count, heads_local, width = queries.shape
    keys_local = latents.shape[0]
    ctx_count = lax.axis_size("ctx")
    loss_scale = float(ctx_count * keys_local // 64)
    key_pos = lax.axis_index("ctx") * keys_local + lax.iota(jnp.int32, keys_local)
    visible = key_pos[None, :] <= positions[:, None]
    block_rows = math.gcd(row_count, max(1, 512 // heads_local))
    nblocks = row_count // block_rows
    query_blocks = queries.reshape(nblocks, block_rows, heads_local, width)
    visible_blocks = visible.reshape(nblocks, block_rows, keys_local)

    def first_pass(inputs):
        scores = masked_scores(inputs[0], latents, inputs[1])
        local_max = jnp.max(scores, axis=2)
        local_total = jnp.sum(
            jnp.where(inputs[1][:, None, :], jnp.exp(scores - local_max[:, :, None]), 0.0), axis=2
        )
        return (scores, local_max, local_total)

    def stats_only(inputs):
        outcome = first_pass(inputs)
        return (outcome[1], outcome[2])

    local_max, local_total = lax.map(stats_only, (query_blocks, visible_blocks))
    local_max = local_max.reshape(row_count, heads_local)
    local_total = local_total.reshape(row_count, heads_local)
    index_local = index_queries.shape[1]
    flat_index = index_queries.reshape(row_count * index_local, -1)
    index_dots = lax.dot_general(
        flat_index, index_keys, (((1,), (1,)), ((), ())), preferred_element_type=jnp.float32
    )
    index_dots = index_dots.reshape(row_count, index_local, keys_local)
    scaled_weights = index_weights * (HI * DI) ** (-0.5)
    logit_part = jnp.sum(scaled_weights[:, :, None] * jnp.maximum(index_dots, 0.0), axis=1)
    row_max = lax.pmax(local_max, "ctx")
    row_total = lax.psum(local_total * jnp.exp(local_max - row_max), "ctx")
    max_blocks = row_max.reshape(nblocks, block_rows, heads_local)
    total_blocks = row_total.reshape(nblocks, block_rows, heads_local)

    def second_pass(inputs):
        source, block_visible, block_max, block_total = inputs
        scores = masked_scores(source, latents, block_visible)
        weights_now = jnp.where(
            block_visible[:, None, :],
            jnp.exp(scores - block_max[:, :, None]) / block_total[:, :, None],
            0.0,
        )
        return jnp.sum(weights_now, axis=1)

    target_part = lax.map(
        second_pass, (query_blocks, visible_blocks, max_blocks, total_blocks)
    ).reshape(row_count, keys_local)
    target_sum, logit_sum = lax.psum((target_part, logit_part), "heads")
    masked, row_peak, row_mass = local_stats(logit_sum, visible)
    row_peak, row_mass = joined_2((row_peak, row_mass), "ctx", combine_stats)
    logit_grad = gradient_of(masked, visible, row_peak, row_mass, target_sum, loss_scale)
    coefficient = jnp.where(
        index_dots > 0.0, logit_grad[:, None, :] * scaled_weights[:, :, None], 0.0
    )
    flat_coefficient = coefficient.astype(jnp.bfloat16).reshape(row_count * index_local, keys_local)
    query_part = jnp.dot(flat_coefficient, index_keys, preferred_element_type=jnp.float32)
    grad_queries = lax.psum(query_part, "ctx").reshape(row_count, index_local, -1)
    grad_keys = lax.psum_scatter(
        lax.dot_general(
            flat_coefficient,
            flat_index,
            (((0,), (0,)), ((), ())),
            preferred_element_type=jnp.float32,
        ),
        "heads",
        scatter_dimension=0,
        tiled=True,
    )
    return (grad_queries, grad_keys)


def solution(mesh):
    placed = (
        P(None, "heads", None),
        P("ctx", None),
        P(None, "heads", None),
        P("ctx", None),
        P(None, "heads"),
        P(),
    )
    return jax.shard_map(
        body,
        mesh=mesh,
        in_specs=placed,
        out_specs=(P(None, "heads", None), P(("ctx", "heads"), None)),
        check_vma=False,
    )
```

profile of v0, /device:TPU:0, one launch (start us, length us, event | category | flops | bytes accessed | tf_op | source)
XLA Modules:
  0.0 257.8 jit_solution(14143279784788766471)
XLA Ops:
  8.1 4.7 %multiply_reduce_fusion = (f32[64,1024]{1,0:T(8,128)}, f32[64,16,1024]{2,1,0:T(8,128)}) fusion(f32[64,16]{1,0:T(8,128)S(1)} %copy.8, bf16[64,16,128]{2,1,0:T(8,128)(2,1)} %param.14, bf16[1024,128]{1,0:T(8,128)(2,1)S(1)} %copy-done), kind=kOutput, calls=%fused_computation.27 | convolution fusion | flops 271515648 | bytes 4984832 | tf_op jit(solution)/shard_map/dot_general | solution.py:88
  13.1 13.0 %while.40 = (s32[]{:T(128)}, f32[4,16,32]{2,1,0:T(8,128)S(1)}, f32[4,16,32]{2,1,0:T(8,128)S(1)}, pred[4,16,1024]{2,1,0:T(8,128)(4,1)S(1)}, bf16[4,16,32,576]{3,2...) while((s32[]{:T(128)}, f32[4,16,32]{2,1,0:T(8,128)S(1)}, f32[4,16,32]{2,1,0:T(8,128)S(1)}, ...), condition=%wide.region_9.10_spmd, body=%wide.region_6.9_spmd.sunk | while | flops 608173056 | bytes 6133857 | solution.py:83
  13.2 2.4 fusion.29
  16.4 2.4 fusion.29
  19.7 2.4 fusion.29
  22.1 0.8 select_reduce_fusion.4
  22.9 2.4 fusion.29
  26.2 38.9 %pmax.7 = f32[64,32]{1,0:T(8,128)S(1)} all-reduce(f32[64,32]{1,0:T(8,128)S(1)} %bitcast.89), channel_id=1, replica_groups=mesh['ctx'=8,'heads'=4] {'ctx'}, use_global_device_ids=true, to_apply=%region_10.11 | all-reduce | flops 2048 | bytes 16384 | tf_op jit(solution)/shard_map/pmax | solution.py:94
  66.2 1.1 fusion.17
  67.6 1.2 fusion.12
  69.1 33.3 %all-reduce.2 = (f32[4,16,32]{2,1,0:T(8,128)S(1)}, f32[512]{0:T(512)S(1)}, f32[512]{0:T(512)S(1)}) all-reduce(f32[4,16,32]{2,1,0:T(8,128)S(1)} %bitcast.90, f32[512]{0:T(512)S(1)} %dynamic-update-slice, f32[512]{0:T(512)S(1)} %dynamic-update-slice.1), channel_id=1, replica_groups=mesh['ctx'=8,'heads'=4] {'ctx'}, use_global_device_ids=true, to_apply=%region_11.12 | all-reduce | flops 3072 | bytes 24576 | tf_op jit(solution)/shard_map/psum | solution.py:95
  102.5 13.5 %while.41 = (s32[]{:T(128)}, f32[4,16,1024]{2,1,0:T(8,128)}, pred[4,16,1024]{2,1,0:T(8,128)(4,1)S(1)}, bf16[4,16,32,576]{3,2,1,0:T(8,128)(2,1)S(1)}, bf16[1024,5...) while((s32[]{:T(128)}, f32[4,16,1024]{2,1,0:T(8,128)}, ...), condition=%wide.region_14.15_spmd, body=%wide.region_12.14_spmd.sunk | while | flops 607109120 | bytes 2105453 | solution.py:109
  102.5 2.8 %select_reduce_fusion.5 = f32[16,1024]{1,0:T(8,128)S(1)} fusion(bf16[1024,576]{0,1:T(8,128)(2,1)} %get-tuple-element.427, f32[16,32]{1,0:T(8,128)S(1)} %get-tuple-element.384, f32[16,32]{1,0:T(8,128)S(1)} %get-tuple-element.385, pred[16,1024]{1,0:T(8,128)(4,1)S(1)} %dynamic-slice_bitcast_fusion.9, ...), kind=kOutput, calls=%fused_computation.17.clone.1 | convolution fusion | flops 607109120 | bytes 1933316 | tf_op jit(solution)/shard_map/while/body/eval_jaxpr/dot_general | solution.py:38
  105.9 2.7 %select_reduce_fusion.5 = f32[16,1024]{1,0:T(8,128)S(1)} fusion(bf16[1024,576]{0,1:T(8,128)(2,1)} %get-tuple-element.427, f32[16,32]{1,0:T(8,128)S(1)} %get-tuple-element.384, f32[16,32]{1,0:T(8,128)S(1)} %get-tuple-element.385, pred[16,1024]{1,0:T(8,128)(4,1)S(1)} %dynamic-slice_bitcast_fusion.9, ...), kind=kOutput, calls=%fused_computation.17.clone.1 | convolution fusion | flops 607109120 | bytes 1933316 | tf_op jit(solution)/shard_map/while/body/eval_jaxpr/dot_general | solution.py:38
  109.3 2.7 %select_reduce_fusion.5 = f32[16,1024]{1,0:T(8,128)S(1)} fusion(bf16[1024,576]{0,1:T(8,128)(2,1)} %get-tuple-element.427, f32[16,32]{1,0:T(8,128)S(1)} %get-tuple-element.384, f32[16,32]{1,0:T(8,128)S(1)} %get-tuple-element.385, pred[16,1024]{1,0:T(8,128)(4,1)S(1)} %dynamic-slice_bitcast_fusion.9, ...), kind=kOutput, calls=%fused_computation.17.clone.1 | convolution fusion | flops 607109120 | bytes 1933316 | tf_op jit(solution)/shard_map/while/body/eval_jaxpr/dot_general | solution.py:38
  112.7 2.7 %select_reduce_fusion.5 = f32[16,1024]{1,0:T(8,128)S(1)} fusion(bf16[1024,576]{0,1:T(8,128)(2,1)} %get-tuple-element.427, f32[16,32]{1,0:T(8,128)S(1)} %get-tuple-element.384, f32[16,32]{1,0:T(8,128)S(1)} %get-tuple-element.385, pred[16,1024]{1,0:T(8,128)(4,1)S(1)} %dynamic-slice_bitcast_fusion.9, ...), kind=kOutput, calls=%fused_computation.17.clone.1 | convolution fusion | flops 607109120 | bytes 1933316 | tf_op jit(solution)/shard_map/while/body/eval_jaxpr/dot_general | solution.py:38
  116.4 30.8 %all-reduce.9.cloned.1.call-done = f32[64,1024]{1,0:T(8,128)} async-done(((f32[64,1024]{1,0:T(8,128)}), f32[64,1024]{1,0:T(8,128)}) %all-reduce.9.cloned.1.call-update) | async-done | bytes 262160 | tf_op jit(solution)/shard_map/psum | solution.py:112
  147.3 1.1 fusion.14
  148.4 2.8 %select_convert_fusion = bf16[64,16,1024]{2,1,0:T(8,128)(2,1)S(1)} fusion(f32[64,16,1024]{2,1,0:T(8,128)} %get-tuple-element.258, f32[64,1024]{1,0:T(8,128)S(1)} %fusion.14, f32[64,16]{1,0:T(8,128)S(1)} %copy.8), kind=kLoop, calls=%fused_computation.26 | loop fusion | flops 4194304 | bytes 6557696 | tf_op jit(solution)/shard_map/convert_element_type | solution.py:119
  151.2 1.5 fusion.18
  152.8 1.6 convolution_bitcast_fusion
  154.3 71.3 %all-reduce.11.cloned.1.call-done = f32[64,16,128]{2,1,0:T(8,128)} async-done(((f32[64,16,128]{2,1,0:T(8,128)}), f32[64,16,128]{2,1,0:T(8,128)}) %all-reduce.11.cloned.1.call-update) | async-done | bytes 524304 | tf_op jit(solution)/shard_map/psum | solution.py:121
  225.6 23.8 %reduce-scatter.2.cloned.1.call-done = f32[256,128]{1,0:T(8,128)} async-done(((f32[1024,128]{1,0:T(8,128)}), f32[256,128]{1,0:T(8,128)}) %reduce-scatter.2.cloned.1.call-update) | async-done | bytes 131088 | tf_op jit(solution)/shard_map/reduce_scatter | solution.py:122
  249.4 1.9 copy.45
  (70 shorter events, 8.1 us)
Async XLA Ops:
  7.2 1.0 copy-start
  7.2 59.0 %all-reduce.7.cloned.1.call-start = ((), (), s32[]{:S(2)}) async-start(), calls=%async_computation.1 | async-start | bytes 524288 | tf_op jit(solution)/shard_map/psum | solution.py:112
  8.1 4.8 %copy-start.3 = (s32[64]{0:T(128)S(1)}, s32[64]{0:T(128)}, u32[]{:S(2)}) copy-start(s32[64]{0:T(128)} %param.17) | copy-start | bytes 772
  8.1 5.0 %copy-start.4 = (bf16[64,32,576]{2,1,0:T(8,128)(2,1)S(1)}, bf16[64,32,576]{2,1,0:T(8,128)(2,1)}, u32[]{:S(2)}) copy-start(bf16[64,32,576]{2,1,0:T(8,128)(2,1)} %param.12) | copy-start | bytes 7077892
  12.8 134.4 %all-reduce.9.cloned.1.call-start = ((), (), s32[]{:S(2)}) async-start(), calls=%async_computation.2 | async-start | bytes 524288 | tf_op jit(solution)/shard_map/psum | solution.py:112
  13.1 51.9 %copy-start.5 = (u32[32]{0:T(128)S(1)}, u32[32]{0:T(128)}, u32[]{:S(2)}) copy-start(u32[32]{0:T(128)} %constant.101) | copy-start | bytes 388
  102.5 44.7 %copy-start.1 = (f32[64,1024]{1,0:T(8,128)S(1)}, f32[64,1024]{1,0:T(8,128)}, u32[]{:S(2)}) copy-start(f32[64,1024]{1,0:T(8,128)} %all-reduce.7.cloned.1.call-done) | copy-start | bytes 786436
  116.1 109.6 %all-reduce.11.cloned.1.call-start = ((), (), s32[]{:S(2)}) async-start(), calls=%async_computation.3 | async-start | bytes 1048576 | tf_op jit(solution)/shard_map/psum | solution.py:121
  151.2 1.6 copy-start.2
  152.7 96.7 %reduce-scatter.2.cloned.1.call-start = ((), (), s32[]{:S(2)}) async-start(), calls=%async_computation.4 | async-start | bytes 655360 | tf_op jit(solution)/shard_map/reduce_scatter | solution.py:122
Sparse Core Ops, SparseCore 0:
  12.9 35.0 all-reduce.6
  116.2 31.0 all-reduce.8
  152.8 72.7 all-reduce.10
  228.5 20.8 reduce-scatter.1
where the time goes:
time: 258 us
  waiting for transfers between devices  126 us (49%)
  blocking collectives  72.2 us (28%)
  matrix products  28.3 us (11%)
  between operations  14.5 us (6%)
  other arithmetic  10.5 us (4%)
  local copies, waits for them, and re-layouts  5.94 us (2%)
    psum x1, waiting for transfers between devices, body(): lax.psum(query_part, 'ctx').reshape(row_count, index_local, -1)  71.3 us
    pmax x1, blocking collectives, body(): row_max = lax.pmax(local_max, 'ctx')  38.9 us
    psum x1, blocking collectives, body(): row_total = lax.psum(local_total * jnp.exp(local_max - row_max), 'ctx')  33.3 us
    psum x2, waiting for transfers between devices, body(): target_sum, logit_sum = lax.psum((target_part, logit_part), 'heads')  30.9 us
    reduce_scatter x1, waiting for transfers between devices, body(): lax.psum_scatter(lax.dot_general(flat_coefficient, flat_index, (((0,), (0...  23.8 us
    dot_general x8, matrix products, masked_scores(): lax.dot_general(flattened, latents, (((1,), (1,)), ((), ())), preferred_e...  20.5 us
  transfers between devices with their start and end apart: 4, of which 3 were waited for; matrix products, arithmetic and copies ran while one was open for 6% of the time, Pallas kernels for 0%

commit v1 on v0

v1 whole, which is shorter than its diff:
```python
import functools
import math

import jax
import jax.numpy as jnp
from jax import lax
from jax.experimental import pallas as pl
from jax.experimental.pallas import tpu as pltpu
from jax.sharding import PartitionSpec as P

F32 = jnp.float32
BF16 = jnp.bfloat16
LOG2E = math.log2(math.e)
SCORE_LOG2 = 192 ** (-0.5) * LOG2E
NEG = -1e30
LANES = 128
VMEM = pl.BlockSpec(memory_space=pltpu.VMEM)
SMEM = pl.BlockSpec(memory_space=pltpu.SMEM)
CONTRACT_LAST = (((1,), (1,)), ((), ()))


def call(kernel, out_shape, n_smem, n_vmem, scratch=(), flops=0, exps=0, nbytes=0):
    outs = jax.tree.map(lambda s: VMEM, out_shape)
    return pl.pallas_call(
        kernel,
        out_shape=out_shape,
        in_specs=[SMEM] * n_smem + [VMEM] * n_vmem,
        out_specs=outs,
        scratch_shapes=list(scratch),
        compiler_params=pltpu.CompilerParams(vmem_limit_bytes=40 << 20),
        cost_estimate=pl.CostEstimate(flops=flops, transcendentals=exps, bytes_accessed=nbytes),
    )


def columns(ref_rows, count):
    padded = jnp.concatenate(
        [ref_rows, jnp.zeros((LANES - count, LANES), F32)], axis=0
    )
    return jnp.transpose(padded)


def logits_kernel(n_rows, n_heads, who_ref, iq_ref, ik_ref, iw_ref, keep_ref, send_ref, part):
    half = keep_ref.shape[1]
    wcol = columns(iw_ref[...], iw_ref.shape[0])
    rows = LANES
    per = rows // n_heads
    for b in range(n_rows * n_heads // rows):
        dots = lax.dot_general(
            iq_ref[b * rows : (b + 1) * rows, :], ik_ref[...], CONTRACT_LAST, preferred_element_type=F32
        )
        weighted = jnp.maximum(dots, 0.0) * wcol[:, b : b + 1]
        for i in range(per):
            part[b * per + i : b * per + i + 1, :] = jnp.sum(
                weighted[i * n_heads : (i + 1) * n_heads, :], axis=0, keepdims=True
            )
    core = who_ref[1]
    keep_ref[...] = part[:, pl.ds(pl.multiple_of(core * half, LANES), half)]
    send_ref[...] = part[:, pl.ds(pl.multiple_of((1 - core) * half, LANES), half)]


def scores_kernel(n_rows, n_heads, who_ref, pos_ref, q_ref, lat_ref, p_ref, stat_ref, s_even, s_odd, col):
    keys = lat_ref.shape[0]
    place = who_ref[0] + lax.broadcasted_iota(jnp.int32, (1, keys), 1)
    block = 256
    per = block // n_heads
    in_col = LANES // n_heads
    blocks = n_rows * n_heads // LANES
    col[...] = jnp.zeros_like(col)
    for b in range(n_rows * n_heads // block):
        held = s_even if b % 2 == 0 else s_odd
        held[...] = lax.dot_general(
            q_ref[b * block : (b + 1) * block, :], lat_ref[...], CONTRACT_LAST, preferred_element_type=F32
        )
        for i in range(per):
            row = b * per + i
            bias = jnp.where(place <= pos_ref[row], 0.0, NEG)
            x = held[i * n_heads : (i + 1) * n_heads, :] + bias
            top = jnp.max(x, axis=1, keepdims=True)
            e = jnp.exp2((x - top) * SCORE_LOG2)
            p_ref[row * n_heads : (row + 1) * n_heads, :] = e
            total = jnp.sum(e, axis=1, keepdims=True)
            lane = row // in_col
            at = (row % in_col) * n_heads
            col[at : at + n_heads, lane : lane + 1] = top
            col[at : at + n_heads, blocks + lane : blocks + lane + 1] = total
    stat_ref[...] = jnp.transpose(col[...])[: stat_ref.shape[0], :]


def index_stats_kernel(who_ref, pos_ref, mine_ref, other_ref, stat_ref, logit_ref, out_ref, col):
    n_rows, half = mine_ref.shape
    first = who_ref[0] + who_ref[1] * half
    place = first + lax.broadcasted_iota(jnp.int32, (1, half), 1)
    rows = lax.broadcasted_iota(jnp.int32, (n_rows, 1), 0)
    pos = jnp.zeros((n_rows, 1), jnp.int32)
    for r in range(n_rows):
        pos = jnp.where(rows == r, pos_ref[r], pos)
    x = jnp.where(place <= pos, (mine_ref[...] + other_ref[...]) * LOG2E, NEG)
    logit_ref[...] = x
    top = jnp.max(x, axis=1, keepdims=True)
    col[...] = jnp.zeros_like(col)
    col[:n_rows, 0:1] = top
    col[:n_rows, 1:2] = jnp.sum(jnp.exp2(x - top), axis=1, keepdims=True)
    n = stat_ref.shape[0]
    out_ref[:n, :] = stat_ref[...]
    out_ref[n:, :] = jnp.transpose(col[...])[: out_ref.shape[0] - n, :]


def joined(tops, totals, unit):
    top = tops[0]
    for t in tops[1:]:
        top = jnp.maximum(top, t)
    total = totals[0] * jnp.exp2((tops[0] - top) * unit)
    for t, l in zip(tops[1:], totals[1:]):
        total = total + l * jnp.exp2((t - top) * unit)
    return top, total


def target_kernel(n_rows, n_heads, who_ref, all_ref, own_ref, p_ref, keep_ref, send_ref, part):
    half = keep_ref.shape[1]
    n = all_ref.shape[0]
    blocks = n_rows * n_heads // LANES
    top, total = joined(
        [all_ref[k, :blocks, :] for k in range(n)],
        [all_ref[k, blocks : 2 * blocks, :] for k in range(n)],
        SCORE_LOG2,
    )
    weight = jnp.exp2((own_ref[:blocks, :] - top) * SCORE_LOG2) / total
    wcol = columns(weight, blocks)
    in_col = LANES // n_heads
    for row in range(n_rows):
        at = (row % in_col) * n_heads
        lane = row // in_col
        part[row : row + 1, :] = jnp.sum(
            p_ref[row * n_heads : (row + 1) * n_heads, :] * wcol[at : at + n_heads, lane : lane + 1],
            axis=0,
            keepdims=True,
        )
    peak, mass = joined(
        [all_ref[k, 2 * blocks : 2 * blocks + 1, :] for k in range(n)],
        [all_ref[k, 2 * blocks + 1 : 2 * blocks + 2, :] for k in range(n)],
        1.0,
    )
    core = who_ref[1]
    keep_ref[:n_rows, :] = part[:, pl.ds(pl.multiple_of(core * half, LANES), half)]
    send_ref[:n_rows, :] = part[:, pl.ds(pl.multiple_of((1 - core) * half, LANES), half)]
    stats = jnp.concatenate([peak, mass, jnp.zeros((6, LANES), F32)], axis=0)
    for ref in (keep_ref, send_ref):
        ref[n_rows:, :LANES] = stats
        ref[n_rows:, LANES:] = jnp.zeros((8, half - LANES), F32)


def probs_kernel(mine_ref, other_ref, logit_ref, prob_ref):
    n_rows = logit_ref.shape[0]
    peak, mass = joined(
        [mine_ref[n_rows : n_rows + 1, :LANES], other_ref[n_rows : n_rows + 1, :LANES]],
        [mine_ref[n_rows + 1 : n_rows + 2, :LANES], other_ref[n_rows + 1 : n_rows + 2, :LANES]],
        1.0,
    )
    stats = columns(jnp.concatenate([peak, 1.0 / mass], axis=0), 2)
    prob_ref[...] = jnp.exp2(logit_ref[...] - stats[:n_rows, 0:1]) * stats[:n_rows, 1:2]


def grads_kernel(n_rows, n_heads, who_ref, mine_ref, other_ref, iq_ref, ik_ref, iw_ref, gq_ref, *rest):
    *gk_refs, g_full, gk_t = rest
    half = mine_ref.shape[1]
    core = who_ref[1]
    g_full[:, pl.ds(pl.multiple_of(core * half, LANES), half)] = mine_ref[...]
    g_full[:, pl.ds(pl.multiple_of((1 - core) * half, LANES), half)] = other_ref[...]
    wcol = columns(iw_ref[...], iw_ref.shape[0])
    rows = LANES
    per = rows // n_heads
    blocks = n_rows * n_heads // rows
    for b in range(blocks):
        iq = iq_ref[b * rows : (b + 1) * rows, :]
        dots = lax.dot_general(iq, ik_ref[...], CONTRACT_LAST, preferred_element_type=F32)
        g = jnp.concatenate(
            [
                jnp.broadcast_to(g_full[b * per + i : b * per + i + 1, :], (n_heads, 2 * half))
                for i in range(per)
            ],
            axis=0,
        )
        coef = jnp.where(dots > 0.0, g * wcol[:, b : b + 1], 0.0).astype(BF16)
        gq_ref[b * rows : (b + 1) * rows, :] = jnp.dot(coef, ik_ref[...], preferred_element_type=F32)
        term = jnp.dot(jnp.transpose(iq), coef, preferred_element_type=F32)
        if b == 0:
            gk_t[...] = term
        else:
            gk_t[...] += term
    me = who_ref[2]
    size = gk_refs[0].shape[0]
    for k, ref in enumerate(gk_refs):
        at = pl.multiple_of((me ^ k) * size, LANES)
        ref[...] = jnp.transpose(gk_t[:, pl.ds(at, size)])


def body(queries, latents, index_queries, index_keys, index_weights, positions):
    n_rows, heads_local, width = queries.shape
    keys = latents.shape[0]
    index_local, depth = index_queries.shape[1:]
    n_ctx = lax.axis_size("ctx")
    n_heads = lax.axis_size("heads")
    half = keys // 2
    loss_scale = float(n_ctx * keys // 64)
    me = lax.axis_index("heads")
    who = jnp.stack([lax.axis_index("ctx") * keys, me % 2, me]).astype(jnp.int32)
    partner = [[(i, i ^ k) for i in range(n_heads)] for k in range(n_heads)]
    shape = jax.ShapeDtypeStruct
    iq = index_queries.reshape(n_rows * index_local, depth)
    weights = (index_weights * (index_local * n_heads * depth) ** (-0.5)).reshape(-1, LANES)

    def over_rest(value):
        k = 2
        while k < n_heads:
            value = value + lax.ppermute(value, "heads", partner[k])
            k *= 2
        return value

    keep, send = call(
        functools.partial(logits_kernel, n_rows, index_local),
        (shape((n_rows, half), F32),) * 2,
        1,
        3,
        [pltpu.VMEM((n_rows, keys), F32)],
        flops=2 * iq.size * keys,
        nbytes=keys * depth * 4,
    )(who, iq, index_keys, weights)
    logit_mine = keep + lax.ppermute(send, "heads", partner[1])
    logit_other = lax.ppermute(logit_mine, "heads", partner[2])

    stat_rows = 2 * n_rows * heads_local // LANES
    probs, stats = call(
        functools.partial(scores_kernel, n_rows, heads_local),
        (shape((n_rows * heads_local, keys), F32), shape((stat_rows, LANES), F32)),
        2,
        2,
        [pltpu.VMEM((256, keys), F32)] * 2 + [pltpu.VMEM((LANES, LANES), F32)],
        flops=2 * queries.size * keys,
        exps=n_rows * heads_local * keys,
        nbytes=queries.size * 2,
    )(who, positions, queries.reshape(n_rows * heads_local, width), latents)
    logits, stats = call(
        index_stats_kernel,
        (shape((n_rows, half), F32), shape((stat_rows + 8, LANES), F32)),
        2,
        3,
        [pltpu.VMEM((LANES, LANES), F32)],
    )(who, positions, logit_mine, logit_other, stats)
    everyone = lax.all_to_all(
        jnp.broadcast_to(stats, (n_ctx,) + stats.shape), "ctx", 0, 0
    )
    keep, send = call(
        functools.partial(target_kernel, n_rows, heads_local),
        (shape((n_rows + 8, half), F32),) * 2,
        1,
        3,
        [pltpu.VMEM((n_rows, keys), F32)],
    )(who, everyone, stats, probs)
    got = lax.ppermute(send, "heads", partner[1])
    index_probs = call(probs_kernel, shape((n_rows, half), F32), 0, 3)(keep, got, logits)
    target = over_rest(keep[:n_rows] + got[:n_rows])
    grad = loss_scale * (index_probs - target * (1.0 / (heads_local * n_heads)))
    grad_other = lax.ppermute(grad, "heads", partner[1])
    owned = keys // n_heads
    query_part, *key_parts = call(
        functools.partial(grads_kernel, n_rows, index_local),
        (shape((n_rows * index_local, depth), F32),) + (shape((owned, depth), F32),) * n_heads,
        1,
        5,
        [pltpu.VMEM((n_rows, keys), F32), pltpu.VMEM((depth, keys), F32)],
    )(who, grad, grad_other, iq, index_keys, weights)
    grad_keys = key_parts[0]
    for k in range(1, n_heads):
        grad_keys = grad_keys + lax.ppermute(key_parts[k], "heads", partner[k])
    blocks = query_part.reshape(n_ctx, -1, depth)
    mine = jnp.sum(lax.all_to_all(blocks, "ctx", 0, 0), axis=0)
    grad_queries = lax.all_to_all(jnp.broadcast_to(mine, blocks.shape), "ctx", 0, 0)
    return grad_queries.reshape(n_rows, index_local, depth), grad_keys


def solution(mesh):
    placed = (
        P(None, "heads", None),
        P("ctx", None),
        P(None, "heads", None),
        P("ctx", None),
        P(None, "heads"),
        P(),
    )
    return jax.shard_map(
        body,
        mesh=mesh,
        in_specs=placed,
        out_specs=(P(None, "heads", None), P(("ctx", "heads"), None)),
        check_vma=False,
    )
```

time: 258 us -> 81.7 us (0.32)
  waiting for transfers between devices: 126 us -> 19.2 us
  blocking collectives: 72.2 us -> 31 us
  matrix products: 28.3 us -> 0 us
  between operations: 14.5 us -> 0.76 us
  Pallas kernels: 0 us -> 12.3 us
  starting transfers between devices: 0.16 us -> 9.35 us
  other arithmetic: 10.5 us -> 1.58 us
    psum x3 -> x0, waiting for transfers between devices: 102 us -> none  [the longest x1 71.3 us: body(): lax.psum(query_part, 'ctx').reshape(row_count, index_local, -1)]
    pmax x1 -> x0, blocking collectives: 38.9 us -> none  [body(): row_max = lax.pmax(local_max, 'ctx')]
    psum x1 -> x0, blocking collectives: 33.3 us -> none  [body(): row_total = lax.psum(local_total * jnp.exp(local_max - row_max), 'ctx')]
    all_to_all x0 -> x2, blocking collectives: none -> 31 us  [the longest x1 17.5 us: body(): mine = jnp.sum(lax.all_to_all(blocks, 'ctx', 0, 0), axis=0)]
    dot_general x11 -> x0, matrix products: 28.3 us -> none  [the longest x8 20.5 us: masked_scores(): lax.dot_general(flattened, latents, (((1,), (1,)), ((), ())), preferred_e...]
    reduce_scatter x1 -> x0, waiting for transfers between devices: 23.8 us -> none  [body(): lax.psum_scatter(lax.dot_general(flat_coefficient, flat_index, (((0,), (0...]
    ppermute x0 -> x8, waiting for transfers between devices: none -> 13.9 us  [the longest x3 6.32 us: body(): grad_keys = grad_keys + lax.ppermute(key_parts[k], 'heads', partner[k])]
    pallas_call x0 -> x6, Pallas kernels: none -> 12.3 us  [the longest x1 4.44 us: body(): call(functools.partial(scores_kernel, n_rows, heads_local), (shape((n_row...]
  transfers between devices with their start and end apart: 4 -> 9, of which waited for: 3 -> 6; matrix products, arithmetic and copies ran while one was open for 6% -> 3% of each run, Pallas kernels for 0% -> 6%
where the time goes in v1:
time: 81.7 us; the launch traced here: 81.2 us
  blocking collectives  31 us (38%)
  waiting for transfers between devices  19.2 us (24%)
  Pallas kernels  12.3 us (15%)
  starting transfers between devices  9.35 us (11%)
  local copies, waits for them, and re-layouts  7.14 us (9%)
  other arithmetic  1.58 us (2%)
    all_to_all x1, blocking collectives, body(): mine = jnp.sum(lax.all_to_all(blocks, 'ctx', 0, 0), axis=0)  17.5 us
    all_to_all x1, blocking collectives, body(): lax.all_to_all(jnp.broadcast_to(stats, (n_ctx,) + stats.shape), 'ctx', 0, 0)  13.5 us
    ppermute x3, waiting for transfers between devices, body(): grad_keys = grad_keys + lax.ppermute(key_parts[k], 'heads', partner[k])  6.32 us
    unnamed x14, local copies, waits for them, and re-layouts  6.13 us
    all_to_all x1, waiting for transfers between devices, body(): lax.all_to_all(jnp.broadcast_to(mine, blocks.shape), 'ctx', 0, 0)  5.3 us
    ppermute x1, waiting for transfers between devices, over_rest(): value = value + lax.ppermute(value, 'heads', partner[k])  4.85 us
    pallas_call x1, Pallas kernels, body(): call(functools.partial(scores_kernel, n_rows, heads_local), (shape((n_row...  4.44 us
    all_to_all x1, starting transfers between devices, body(): lax.all_to_all(jnp.broadcast_to(mine, blocks.shape), 'ctx', 0, 0)  3.64 us
  transfers between devices with their start and end apart: 9, of which 6 were waited for; matrix products, arithmetic and copies ran while one was open for 3% of the time, Pallas kernels for 6%

profile of v1, /device:TPU:0, one launch (start us, length us, event | category | flops | bytes accessed | tf_op | source)
XLA Modules:
  0.0 81.2 jit_solution(8963818713490000548)
XLA Ops:
  0.6 0.7 broadcast_multiply_fusion
  1.6 1.0 %copy-done = bf16[64,16,128]{2,1,0:T(8,128)(2,1)S(1)} copy-done((bf16[64,16,128]{2,1,0:T(8,128)(2,1)S(1)}, bf16[64,16,128]{2,1,0:T(8,128)(2,1)}, u32[]{:S(2)}) %copy-start) | copy-done | bytes 262168
  2.5 0.9 %copy-done.2 = bf16[1024,128]{1,0:T(8,128)(2,1)S(1)} copy-done((bf16[1024,128]{1,0:T(8,128)(2,1)S(1)}, bf16[1024,128]{1,0:T(8,128)(2,1)}, u32[]{:S(2)}) %copy-start.2) | copy-done | bytes 262168
  3.5 1.7 %shard_map.77 = (f32[64,512]{1,0:T(8,128)S(1)}, f32[64,512]{1,0:T(8,128)S(1)}) custom-call(s32[3]{0:T(128)S(1)} %pad_add_fusion.who_ref, bf16[1024,128]{1,0:T(8,128)(2,1)S(1)} %bitcast.8, bf16[1024,128]{1,0:T(8,128)(2,1)S(1)} %copy-done.2, f32[8,128]{1,0:T(8,128)S(1)} %reshape.20.iw_ref), custom_call_target="tpu_custom_call" | custom-call | flops 268435456 | bytes 524288 | tf_op jit(solution)/shard_map/pallas_call | solution.py:219
  5.8 1.7 %copy.11.lat_ref = bf16[1024,576]{1,0:T(8,128)(2,1)S(1)} copy(bf16[1024,576]{0,1:T(8,128)(2,1)} %param.7) | data formatting | bytes 2359296 | tf_op args[1]
  7.5 2.6 %collective-permute-start.1 = (f32[64,512]{1,0:T(8,128)S(1)}, f32[64,512]{1,0:T(8,128)S(1)}, u32[]{:S(2)}, u32[]{:S(2)}) collective-permute-start(f32[64,512]{1,0:T(8,128)S(1)} %add.23.mine_ref), channel_id=1, source_target_pairs={{0,2},{1,3},{2,0},{3,1},{4,6},{5,7},{6,4},{7,5},{8,10},{9,11},{10,... | collective-permute-start | bytes 393224 | tf_op jit(solution)/shard_map/ppermute | solution.py:229
  10.1 1.7 %copy-done.5 = bf16[64,32,576]{2,1,0:T(8,128)(2,1)S(1)} copy-done((bf16[64,32,576]{2,1,0:T(8,128)(2,1)S(1)}, bf16[64,32,576]{2,1,0:T(8,128)(2,1)}, u32[]{:S(2)}) %copy-start.5) | copy-done | bytes 2359320
  11.9 4.4 %shard_map.78 = (f32[2048,1024]{1,0:T(8,128)S(1)}, f32[32,128]{1,0:T(8,128)S(1)}) custom-call(s32[3]{0:T(128)S(1)} %pad_add_fusion.who_ref, s32[64]{0:T(128)S(1)} %copy-done.4, bf16[2048,576]{1,0:T(8,128)(2,1)S(1)} %bitcast.10, bf16[1024,576]{1,0:T(8,128)(2,1)S(1)} %copy.11.lat_ref), custom_call_target="tpu_custom_call" | custom-call | flops 2415919104 | bytes 2359296 | tf_op jit(solution)/shard_map/pallas_call | solution.py:232
  16.3 0.8 %shard_map.79 = (f32[64,512]{1,0:T(8,128)S(1)}, f32[40,128]{1,0:T(8,128)S(1)}) custom-call(s32[3]{0:T(128)S(1)} %pad_add_fusion.who_ref, s32[64]{0:T(128)S(1)} %copy-done.4, f32[64,512]{1,0:T(8,128)S(1)} %add.23.mine_ref, f32[64,512]{1,0:T(8,128)S(1)} %collective-permute-done.1.other_ref, f32[32,128]{1,0:T(8,128)S(1)} %get-tuple-element.17.stat_ref), custom_call_target="tpu_custom_call" | custom-call | tf_op jit(solution)/shard_map/pallas_call | solution.py:242
  17.2 13.5 %all_to_all.15.all_ref = f32[8,40,128]{2,1,0:T(8,128)S(1)} all-to-all(f32[8,40,128]{2,1,0:T(8,128)S(1)} %broadcast_in_dim.6), channel_id=1, replica_groups=mesh['ctx'=8,'heads'=4] {'ctx'}, dimensions={0} | all-to-all | bytes 327680 | tf_op jit(solution)/shard_map/all_to_all | solution.py:249
  30.6 1.9 %shard_map.80 = (f32[72,512]{1,0:T(8,128)S(1)}, f32[72,512]{1,0:T(8,128)S(1)}) custom-call(s32[3]{0:T(128)S(1)} %pad_add_fusion.who_ref, f32[8,40,128]{2,1,0:T(8,128)S(1)} %all_to_all.15.all_ref, f32[40,128]{1,0:T(8,128)S(1)} %get-tuple-element.18.own_ref, f32[2048,1024]{1,0:T(8,128)S(1)} %get-tuple-element.19.p_ref), custom_call_target="tpu_custom_call" | custom-call | tf_op jit(solution)/shard_map/pallas_call | solution.py:252
  32.6 1.4 %collective-permute-done.2.other_ref = f32[72,512]{1,0:T(8,128)S(1)} collective-permute-done((f32[72,512]{1,0:T(8,128)S(1)}, f32[72,512]{1,0:T(8,128)S(1)}, u32[]{:S(2)}, u32[]{:S(2)}) %collective-permute-start.2) | collective-permute-done | bytes 147488 | tf_op jit(solution)/shard_map/ppermute | solution.py:259
  34.7 4.8 %collective-permute-done.3 = f32[64,512]{1,0:T(8,128)S(1)} collective-permute-done((f32[64,512]{1,0:T(8,128)S(1)}, f32[64,512]{1,0:T(8,128)S(1)}, u32[]{:S(2)}, u32[]{:S(2)}) %collective-permute-start.3) | collective-permute-done | bytes 131104 | tf_op jit(solution)/shard_map/ppermute | solution.py:215
  39.7 1.3 %collective-permute-done.4.other_ref = f32[64,512]{1,0:T(8,128)S(1)} collective-permute-done((f32[64,512]{1,0:T(8,128)S(1)}, f32[64,512]{1,0:T(8,128)S(1)}, u32[]{:S(2)}, u32[]{:S(2)}) %collective-permute-start.4) | collective-permute-done | bytes 131104 | tf_op jit(solution)/shard_map/ppermute | solution.py:263
  41.0 3.2 %shard_map.82 = (f32[1024,128]{1,0:T(8,128)S(1)}, f32[256,128]{1,0:T(8,128)S(1)}, f32[256,128]{1,0:T(8,128)S(1)}, f32[256,128]{1,0:T(8,128)S(1)}, f32[256,128]{1,0:T(8,128)S(1)}) custom-call(s32[3]{0:T(128)S(1)} %pad_add_fusion.who_ref, f32[64,512]{1,0:T(8,128)S(1)} %subtract_multiply_fusion.mine_ref, f32[64,512]{1,0:T(8,128)S(1)} %collective-permute-done.4.other_ref, ...), custom_call_target="tpu_custom_call" | custom-call | tf_op jit(solution)/shard_map/pallas_call | solution.py:265
  44.2 17.5 %all_to_all.16 = f32[8,128,128]{2,1,0:T(8,128)S(1)} all-to-all(f32[8,128,128]{2,1,0:T(8,128)S(1)} %bitcast.7), channel_id=1, replica_groups=mesh['ctx'=8,'heads'=4] {'ctx'}, dimensions={0} | all-to-all | bytes 1048576 | tf_op jit(solution)/shard_map/all_to_all | solution.py:276
  61.8 0.8 %broadcast_in_dim.7 = f32[8,128,128]{2,1,0:T(8,128)} broadcast(f32[128,128]{1,0:T(8,128)S(1)} %reduce_sum.9), dimensions={1,2} | broadcast | bytes 589824 | tf_op jit(solution)/shard_map/broadcast_in_dim | solution.py:277
  62.6 3.6 %all-to-all-start.2 = ((f32[8,128,128]{2,1,0:T(8,128)}), f32[8,128,128]{2,1,0:T(8,128)S(1)}, u32[]{:S(2)}, u32[]{:S(2)}) async-start(f32[8,128,128]{2,1,0:T(8,128)} %broadcast_in_dim.7), calls=%async_computation.2 | async-start | bytes 1048576 | tf_op jit(solution)/shard_map/all_to_all | solution.py:277
  66.9 1.3 %collective-permute-start.7 = (f32[256,128]{1,0:T(8,128)S(1)}, f32[256,128]{1,0:T(8,128)S(1)}, u32[]{:S(2)}, u32[]{:S(2)}) collective-permute-start(f32[256,128]{1,0:T(8,128)S(1)} %get-tuple-element.27), channel_id=1, source_target_pairs={{0,3},{1,2},{2,1},{3,0},{4,7},{5,6},{6,5},{7,4},{8,11},{9,10},{10,... | collective-permute-start | bytes 393224 | tf_op jit(solution)/shard_map/ppermute | solution.py:274
  68.1 4.6 %collective-permute-done.6 = f32[256,128]{1,0:T(8,128)S(1)} collective-permute-done((f32[256,128]{1,0:T(8,128)S(1)}, f32[256,128]{1,0:T(8,128)S(1)}, u32[]{:S(2)}, u32[]{:S(2)}) %collective-permute-start.6) | collective-permute-done | bytes 131104 | tf_op jit(solution)/shard_map/ppermute | solution.py:274
  72.7 1.7 %collective-permute-done.7 = f32[256,128]{1,0:T(8,128)S(1)} collective-permute-done((f32[256,128]{1,0:T(8,128)S(1)}, f32[256,128]{1,0:T(8,128)S(1)}, u32[]{:S(2)}, u32[]{:S(2)}) %collective-permute-start.7) | collective-permute-done | bytes 131104 | tf_op jit(solution)/shard_map/ppermute | solution.py:274
  74.4 0.7 add_add_fusion
  75.1 5.3 %all-to-all-done.2 = f32[8,128,128]{2,1,0:T(8,128)S(1)} async-done(((f32[8,128,128]{2,1,0:T(8,128)}), f32[8,128,128]{2,1,0:T(8,128)S(1)}, u32[]{:S(2)}, u32[]{:S(2)}) %all-to-all-start.2) | async-done | bytes 524320 | tf_op jit(solution)/shard_map/all_to_all | solution.py:277
  80.4 0.8 copy.13
  (27 shorter events, 2.4 us)
Async XLA Ops:
  0.6 9.5 %copy-start.4 = (s32[64]{0:T(128)S(1)}, s32[64]{0:T(128)}, u32[]{:S(2)}) copy-start(s32[64]{0:T(128)} %pos_ref.3) | copy-start | bytes 772
  1.6 1.0 %copy-start = (bf16[64,16,128]{2,1,0:T(8,128)(2,1)S(1)}, bf16[64,16,128]{2,1,0:T(8,128)(2,1)}, u32[]{:S(2)}) copy-start(bf16[64,16,128]{2,1,0:T(8,128)(2,1)} %param.8) | copy-start | bytes 786436
  2.5 0.9 %copy-start.2 = (bf16[1024,128]{1,0:T(8,128)(2,1)S(1)}, bf16[1024,128]{1,0:T(8,128)(2,1)}, u32[]{:S(2)}) copy-start(bf16[1024,128]{1,0:T(8,128)(2,1)} %ik_ref.3) | copy-start | bytes 786436
  5.3 2.2 %collective-permute-start = (f32[64,512]{1,0:T(8,128)S(1)}, f32[64,512]{1,0:T(8,128)S(1)}, u32[]{:S(2)}, u32[]{:S(2)}) collective-permute-start(f32[64,512]{1,0:T(8,128)S(1)} %get-tuple-element.16), channel_id=1, source_target_pairs={{0,1},{1,0},{2,3},{3,2},{4,5},{5,4},{6,7},{7,6},{8,9},{9,8},{10,11... | collective-permute-start | bytes 393224 | tf_op jit(solution)/shard_map/ppermute | solution.py:228
  7.5 8.8 %collective-permute-start.1 = (f32[64,512]{1,0:T(8,128)S(1)}, f32[64,512]{1,0:T(8,128)S(1)}, u32[]{:S(2)}, u32[]{:S(2)}) collective-permute-start(f32[64,512]{1,0:T(8,128)S(1)} %add.23.mine_ref), channel_id=1, source_target_pairs={{0,2},{1,3},{2,0},{3,1},{4,6},{5,7},{6,4},{7,5},{8,10},{9,11},{10,... | collective-permute-start | bytes 393224 | tf_op jit(solution)/shard_map/ppermute | solution.py:229
  10.1 1.7 %copy-start.5 = (bf16[64,32,576]{2,1,0:T(8,128)(2,1)S(1)}, bf16[64,32,576]{2,1,0:T(8,128)(2,1)}, u32[]{:S(2)}) copy-start(bf16[64,32,576]{2,1,0:T(8,128)(2,1)} %param.6) | copy-start | bytes 7077892
  30.6 10.4 %copy-start.1 = (bf16[64,16,128]{2,1,0:T(8,128)(2,1)S(1)}, bf16[64,16,128]{2,1,0:T(8,128)(2,1)}, u32[]{:S(2)}) copy-start(bf16[64,16,128]{2,1,0:T(8,128)(2,1)} %param.8) | copy-start | bytes 786436
  30.6 10.4 %copy-start.3 = (bf16[1024,128]{1,0:T(8,128)(2,1)S(1)}, bf16[1024,128]{1,0:T(8,128)(2,1)}, u32[]{:S(2)}) copy-start(bf16[1024,128]{1,0:T(8,128)(2,1)} %ik_ref.3) | copy-start | bytes 786436
  32.5 1.4 %collective-permute-start.2 = (f32[72,512]{1,0:T(8,128)S(1)}, f32[72,512]{1,0:T(8,128)S(1)}, u32[]{:S(2)}, u32[]{:S(2)}) collective-permute-start(f32[72,512]{1,0:T(8,128)S(1)} %get-tuple-element.21), channel_id=1, source_target_pairs={{0,1},{1,0},{2,3},{3,2},{4,5},{5,4},{6,7},{7,6},{8,9},{9,8},{10,11... | collective-permute-start | bytes 442376 | tf_op jit(solution)/shard_map/ppermute | solution.py:259
  34.0 5.6 %collective-permute-start.3 = (f32[64,512]{1,0:T(8,128)S(1)}, f32[64,512]{1,0:T(8,128)S(1)}, u32[]{:S(2)}, u32[]{:S(2)}) collective-permute-start(f32[64,512]{1,0:T(8,128)S(1)} %slice_add_fusion), channel_id=1, source_target_pairs={{0,2},{1,3},{2,0},{3,1},{4,6},{5,7},{6,4},{7,5},{8,10},{9,11},{10,... | collective-permute-start | bytes 393224 | tf_op jit(solution)/shard_map/ppermute | solution.py:215
  39.6 1.4 %collective-permute-start.4 = (f32[64,512]{1,0:T(8,128)S(1)}, f32[64,512]{1,0:T(8,128)S(1)}, u32[]{:S(2)}, u32[]{:S(2)}) collective-permute-start(f32[64,512]{1,0:T(8,128)S(1)} %subtract_multiply_fusion.mine_ref), channel_id=1, source_target_pairs={{0,1},{1,0},{2,3},{3,2},{4,5},{5,4},{6,7},{7,6},{8,9},{9,8},{10,11... | collective-permute-start | bytes 393224 | tf_op jit(solution)/shard_map/ppermute | solution.py:263
  62.6 17.8 %all-to-all-start.2 = ((f32[8,128,128]{2,1,0:T(8,128)}), f32[8,128,128]{2,1,0:T(8,128)S(1)}, u32[]{:S(2)}, u32[]{:S(2)}) async-start(f32[8,128,128]{2,1,0:T(8,128)} %broadcast_in_dim.7), calls=%async_computation.2 | async-start | bytes 1048576 | tf_op jit(solution)/shard_map/all_to_all | solution.py:277
  66.3 1.9 %collective-permute-start.5 = (f32[256,128]{1,0:T(8,128)S(1)}, f32[256,128]{1,0:T(8,128)S(1)}, u32[]{:S(2)}, u32[]{:S(2)}) collective-permute-start(f32[256,128]{1,0:T(8,128)S(1)} %get-tuple-element.25), channel_id=1, source_target_pairs={{0,1},{1,0},{2,3},{3,2},{4,5},{5,4},{6,7},{7,6},{8,9},{9,8},{10,11... | collective-permute-start | bytes 393224 | tf_op jit(solution)/shard_map/ppermute | solution.py:274
  66.3 6.4 %collective-permute-start.6 = (f32[256,128]{1,0:T(8,128)S(1)}, f32[256,128]{1,0:T(8,128)S(1)}, u32[]{:S(2)}, u32[]{:S(2)}) collective-permute-start(f32[256,128]{1,0:T(8,128)S(1)} %get-tuple-element.26), channel_id=1, source_target_pairs={{0,2},{1,3},{2,0},{3,1},{4,6},{5,7},{6,4},{7,5},{8,10},{9,11},{10,... | collective-permute-start | bytes 393224 | tf_op jit(solution)/shard_map/ppermute | solution.py:274
  66.9 7.6 %collective-permute-start.7 = (f32[256,128]{1,0:T(8,128)S(1)}, f32[256,128]{1,0:T(8,128)S(1)}, u32[]{:S(2)}, u32[]{:S(2)}) collective-permute-start(f32[256,128]{1,0:T(8,128)S(1)} %get-tuple-element.27), channel_id=1, source_target_pairs={{0,3},{1,2},{2,1},{3,0},{4,7},{5,6},{6,5},{7,4},{8,11},{9,10},{10,... | collective-permute-start | bytes 393224 | tf_op jit(solution)/shard_map/ppermute | solution.py:274

commit v2 on v1

v2 whole, which is shorter than its diff:
```python
import functools
import math

import jax
import jax.numpy as jnp
from jax import lax
from jax.experimental import pallas as pl
from jax.experimental.pallas import tpu as pltpu
from jax.sharding import PartitionSpec as P

F32 = jnp.float32
BF16 = jnp.bfloat16
LOG2E = math.log2(math.e)
SCORE_LOG2 = 192 ** (-0.5) * LOG2E
NEG = -1e30
LANES = 128
VMEM = pl.BlockSpec(memory_space=pltpu.VMEM)
SMEM = pl.BlockSpec(memory_space=pltpu.SMEM)
HBM = pl.BlockSpec(memory_space=pl.ANY)
CONTRACT_LAST = (((1,), (1,)), ((), ()))
QUAD = 4


def call(kernel, out_shape, in_specs, out_specs=None, scratch=(), flops=0, exps=0, nbytes=0):
    if out_specs is None:
        out_specs = jax.tree.map(lambda s: VMEM, out_shape)
    return pl.pallas_call(
        kernel,
        out_shape=out_shape,
        in_specs=in_specs,
        out_specs=out_specs,
        scratch_shapes=list(scratch),
        compiler_params=pltpu.CompilerParams(vmem_limit_bytes=40 << 20),
        cost_estimate=pl.CostEstimate(flops=flops, transcendentals=exps, bytes_accessed=nbytes),
    )


def half_at(core, half):
    return pl.ds(pl.multiple_of(core * half, LANES), half)


def logits_kernel(
    n_rows, n_heads, scale,
    pos_ref, iq_hbm, ik_hbm, iw_hbm, q_hbm, lat_hbm,
    keep_ref, send_ref, bias_ref, iq_ref, ik_ref, iw_ref, q_ref, lat_ref,
    part, sems,
):
    half = keep_ref.shape[1]
    copies = [
        pltpu.make_async_copy(a, b, sems.at[i])
        for i, (a, b) in enumerate(
            ((ik_hbm, ik_ref), (iq_hbm, iq_ref), (iw_hbm, iw_ref), (lat_hbm, lat_ref), (q_hbm, q_ref))
        )
    ]
    for copy in copies:
        copy.start()
    place = lax.axis_index("ctx") * 2 * half + lax.broadcasted_iota(jnp.int32, (1, 2 * half), 1)
    for row in range(n_rows):
        bias_ref[row : row + 1, :] = jnp.where(place <= pos_ref[row], 0.0, NEG)
    for copy in copies[:3]:
        copy.wait()
    iw_ref[...] = iw_ref[...] * scale
    rows = LANES
    per = rows // n_heads
    for b in range(n_rows * n_heads // rows):
        dots = lax.dot_general(
            iq_ref[b * rows : (b + 1) * rows, :], ik_ref[...], CONTRACT_LAST, preferred_element_type=F32
        )
        for i in range(per):
            row = b * per + i
            part[row : row + 1, :] = jnp.sum(
                jnp.maximum(dots[i * n_heads : (i + 1) * n_heads, :], 0.0) * iw_ref[:, row : row + 1],
                axis=0,
                keepdims=True,
            )
    core = lax.axis_index("heads") & 1
    mine, other = half_at(core, half), half_at(1 - core, half)
    keep_ref[...] = part[:, mine] + bias_ref[:, mine]
    send_ref[...] = part[:, other]
    for copy in copies[3:]:
        copy.wait()


def scores_kernel(n_rows, n_heads, bias_ref, q_ref, lat_ref, p_ref, stat_ref, s_even, s_odd):
    block = 256
    per = block // n_heads
    for b in range(n_rows * n_heads // block):
        held = s_even if b % 2 == 0 else s_odd
        held[...] = jnp.dot(
            q_ref[b * block : (b + 1) * block, :], lat_ref[...], preferred_element_type=F32
        )
        for i in range(per):
            row = b * per + i
            x = held[i * n_heads : (i + 1) * n_heads, :] + bias_ref[row : row + 1, :]
            top = jnp.max(x, axis=1, keepdims=True)
            e = jnp.exp2((x - top) * SCORE_LOG2)
            p_ref[row * n_heads : (row + 1) * n_heads, :] = e
            stat_ref[:, row : row + 1] = top
            stat_ref[:, n_rows + row : n_rows + row + 1] = jnp.sum(e, axis=1, keepdims=True)


def index_stats_kernel(mine_ref, other_ref, stat_ref, e_ref, out_ref, col):
    n_rows = mine_ref.shape[0]
    x = (mine_ref[...] + other_ref[...]) * LOG2E
    top = jnp.max(x, axis=1, keepdims=True)
    e = jnp.exp2(x - top)
    e_ref[...] = e
    col[:n_rows, 0:1] = top
    col[n_rows:, 0:1] = jnp.sum(e, axis=1, keepdims=True)
    n = stat_ref.shape[0]
    out_ref[:n, :] = stat_ref[...]
    out_ref[n:, :] = jnp.transpose(col[...])[: out_ref.shape[0] - n, :]


def joined(stats, unit):
    n = stats[0].shape[1] // 2
    tops = [s[:, :n] for s in stats]
    top = functools.reduce(jnp.maximum, tops)
    total = sum(s[:, n:] * jnp.exp2((t - top) * unit) for s, t in zip(stats, tops))
    return top, total


def target_kernel(n_rows, n_heads, all_ref, own_ref, p_ref, keep_ref, send_ref, part):
    half = keep_ref.shape[1]
    n = all_ref.shape[0]
    top, total = joined([all_ref[k, :n_heads, :] for k in range(n)], SCORE_LOG2)
    weight = jnp.exp2((own_ref[:n_heads, :n_rows] - top) * SCORE_LOG2) / total
    for row in range(n_rows):
        part[row : row + 1, :] = jnp.sum(
            p_ref[row * n_heads : (row + 1) * n_heads, :] * weight[:, row : row + 1],
            axis=0,
            keepdims=True,
        )
    peak, mass = joined([all_ref[k, n_heads:, :] for k in range(n)], 1.0)
    core = lax.axis_index("heads") & 1
    keep_ref[:n_rows, :] = part[:, half_at(core, half)]
    send_ref[:n_rows, :] = part[:, half_at(1 - core, half)]
    for ref in (keep_ref, send_ref):
        ref[n_rows:, :n_rows] = peak
        ref[n_rows:, n_rows : 2 * n_rows] = mass


def probs_kernel(mine_ref, other_ref, own_ref, e_ref, prob_ref, col):
    n_rows = e_ref.shape[0]
    peak, mass = joined([ref[n_rows:, : 2 * n_rows] for ref in (mine_ref, other_ref)], 1.0)
    factor = jnp.exp2(own_ref[own_ref.shape[0] - 8 :, :n_rows] - peak) / mass
    col[:8, :n_rows] = factor
    prob_ref[...] = e_ref[...] * jnp.transpose(col[...])[:n_rows, 0:1]


def grads_kernel(n_rows, n_heads, mine_ref, other_ref, iq_ref, ik_ref, iw_ref, *rest):
    *out_refs, g_full, gk_t, w_cols = rest
    gq_refs, gk_refs = out_refs[:QUAD], out_refs[QUAD:]
    half = mine_ref.shape[1]
    me = lax.axis_index("heads")
    core = me & 1
    g_full[:, half_at(core, half)] = mine_ref[...]
    g_full[:, half_at(1 - core, half)] = other_ref[...]
    for row in range(n_rows):
        w_cols[row * n_heads : (row + 1) * n_heads, :] = jnp.broadcast_to(
            iw_ref[:, row : row + 1], (n_heads, LANES)
        )
    slot = lax.axis_index("ctx") & (QUAD - 1)
    rows = LANES
    per = rows // n_heads
    size = n_rows // QUAD
    for k in range(QUAD):
        for b in range(size // per):
            first = pl.multiple_of((slot ^ k) * size, size) + b * per
            at = pl.ds(pl.multiple_of(first * n_heads, rows), rows)
            iq = iq_ref[at, :]
            dots = lax.dot_general(iq, ik_ref[...], CONTRACT_LAST, preferred_element_type=F32)
            g_rows = g_full[pl.ds(pl.multiple_of(first, per), per), :]
            g = jnp.concatenate(
                [jnp.broadcast_to(g_rows[i : i + 1, :], (n_heads, 2 * half)) for i in range(per)], axis=0
            )
            coef = jnp.where(dots > 0.0, g * w_cols[at, 0:1], 0.0).astype(BF16)
            gq_refs[k][b * rows : (b + 1) * rows, :] = jnp.dot(
                coef, ik_ref[...], preferred_element_type=F32
            )
            term = jnp.dot(jnp.transpose(iq), coef, preferred_element_type=F32)
            if k == 0 and b == 0:
                gk_t[...] = term
            else:
                gk_t[...] += term
    size = gk_refs[0].shape[0]
    for k, ref in enumerate(gk_refs):
        at = pl.multiple_of((me ^ k) * size, LANES)
        ref[...] = jnp.transpose(gk_t[:, pl.ds(at, size)])


def outputs_kernel(n_quad, *refs):
    *in_refs, gq_hbm, gk_hbm, total, sems = refs
    blocks, parts = in_refs[:n_quad], in_refs[n_quad:]
    size = blocks[0].shape[0]
    slot = lax.axis_index("ctx") & (n_quad - 1)
    copies = [
        pltpu.make_async_copy(
            ref, gq_hbm.at[pl.ds(pl.multiple_of((slot ^ k) * size, size), size), :], sems.at[k]
        )
        for k, ref in enumerate(blocks)
    ]
    for copy in copies:
        copy.start()
    total[...] = sum(ref[...] for ref in parts)
    last = pltpu.make_async_copy(total, gk_hbm, sems.at[n_quad])
    last.start()
    for copy in copies + [last]:
        copy.wait()


def body(queries, latents, index_queries, index_keys, index_weights, positions):
    n_rows, heads_local, width = queries.shape
    keys = latents.shape[0]
    index_local, depth = index_queries.shape[1:]
    n_ctx = lax.axis_size("ctx")
    n_heads = lax.axis_size("heads")
    half = keys // 2
    loss_scale = float(n_ctx * keys // 64)
    shape = jax.ShapeDtypeStruct

    def swapped(value, axis, k):
        n = lax.axis_size(axis)
        return lax.ppermute(value, axis, [(i, i ^ k) for i in range(n)])

    flat = (n_rows * index_local, depth)
    keep, send, bias, iq, ik, iw, q, lat = call(
        functools.partial(
            logits_kernel, n_rows, index_local, (index_local * n_heads * depth) ** (-0.5)
        ),
        (
            shape((n_rows, half), F32),
            shape((n_rows, half), F32),
            shape((n_rows, keys), F32),
            shape(flat, BF16),
            shape((keys, depth), BF16),
            shape((index_local, n_rows), F32),
            shape((n_rows * heads_local, width), BF16),
            shape((width, keys), BF16),
        ),
        [SMEM] + [HBM] * 5,
        scratch=[pltpu.VMEM((n_rows, keys), F32), pltpu.SemaphoreType.DMA((5,))],
        flops=2 * flat[0] * depth * keys,
        nbytes=queries.size * 2 + latents.size * 2,
    )(
        positions,
        index_queries.reshape(flat),
        index_keys,
        index_weights.T,
        queries.reshape(n_rows * heads_local, width),
        latents.T,
    )
    logit_mine = keep + swapped(send, "heads", 1)
    logit_other = swapped(logit_mine, "heads", 2)
    probs, stats = call(
        functools.partial(scores_kernel, n_rows, heads_local),
        (shape((n_rows * heads_local, keys), F32), shape((heads_local, 2 * n_rows), F32)),
        [VMEM] * 3,
        scratch=[pltpu.VMEM((256, keys), F32)] * 2,
        flops=2 * queries.size * keys,
        exps=n_rows * heads_local * keys,
        nbytes=queries.size * 2,
    )(bias, q, lat)
    exps, stats = call(
        index_stats_kernel,
        (shape((n_rows, half), F32), shape((heads_local + 8, 2 * n_rows), F32)),
        [VMEM] * 3,
        scratch=[pltpu.VMEM((LANES, LANES), F32)],
    )(logit_mine, logit_other, stats)
    everyone = lax.all_to_all(jnp.broadcast_to(stats, (n_ctx,) + stats.shape), "ctx", 0, 0)
    keep, send = call(
        functools.partial(target_kernel, n_rows, heads_local),
        (shape((n_rows + 8, half), F32),) * 2,
        [VMEM] * 3,
        scratch=[pltpu.VMEM((n_rows, keys), F32)],
    )(everyone, stats, probs)
    got = swapped(send, "heads", 1)
    index_probs = call(
        probs_kernel,
        shape((n_rows, half), F32),
        [VMEM] * 4,
        scratch=[pltpu.VMEM((LANES, LANES), F32)],
    )(keep, got, stats, exps)
    target = keep[:n_rows] + got[:n_rows]
    target = target + swapped(target, "heads", 2)
    grad = loss_scale * (index_probs - target * (1.0 / (heads_local * n_heads)))
    grad_other = swapped(grad, "heads", 1)
    owned = keys // n_heads
    block = (flat[0] // QUAD, depth)
    parts = call(
        functools.partial(grads_kernel, n_rows, index_local),
        (shape(block, F32),) * QUAD + (shape((owned, depth), F32),) * n_heads,
        [VMEM] * 5,
        scratch=[
            pltpu.VMEM((n_rows, keys), F32),
            pltpu.VMEM((depth, keys), F32),
            pltpu.VMEM((flat[0], LANES), F32),
        ],
    )(grad, grad_other, iq, ik, iw)
    query_parts, key_parts = parts[:QUAD], parts[QUAD:]
    mine = query_parts[0] + sum(swapped(query_parts[k], "ctx", k) for k in range(1, QUAD))
    key_parts = [key_parts[0]] + [swapped(key_parts[k], "heads", k) for k in range(1, n_heads)]
    k = QUAD
    while k < n_ctx:
        mine = mine + swapped(mine, "ctx", k)
        k *= 2
    blocks = [mine] + [swapped(mine, "ctx", k) for k in range(1, QUAD)]
    grad_queries, grad_keys = call(
        functools.partial(outputs_kernel, QUAD),
        (shape(flat, F32), shape((owned, depth), F32)),
        [VMEM] * (QUAD + n_heads),
        out_specs=(HBM, HBM),
        scratch=[pltpu.VMEM((owned, depth), F32), pltpu.SemaphoreType.DMA((QUAD + 1,))],
    )(*blocks, *key_parts)
    return grad_queries.reshape(n_rows, index_local, depth), grad_keys


def solution(mesh):
    placed = (
        P(None, "heads", None),
        P("ctx", None),
        P(None, "heads", None),
        P("ctx", None),
        P(None, "heads"),
        P(),
    )
    return jax.shard_map(
        body,
        mesh=mesh,
        in_specs=placed,
        out_specs=(P(None, "heads", None), P(("ctx", "heads"), None)),
        check_vma=False,
    )
```

time: 81.7 us -> 72 us (0.88)
  blocking collectives: 31 us -> 13.2 us
  waiting for transfers between devices: 19.2 us -> 24.6 us
  starting transfers between devices: 9.35 us -> 14.5 us
  other arithmetic: 1.58 us -> 0.13 us
  local copies, waits for them, and re-layouts: 7.14 us -> 6.28 us
    all_to_all x1 -> x0, blocking collectives: 17.5 us -> none  [body(): mine = jnp.sum(lax.all_to_all(blocks, 'ctx', 0, 0), axis=0)]
    ppermute x8 -> x15, waiting for transfers between devices: 13.9 us -> 24.6 us  [swapped(): return lax.ppermute(value, axis, [(i, i ^ k) for i in range(n)])]
    ppermute x8 -> x15, starting transfers between devices: 5.71 us -> 14.5 us  [swapped(): return lax.ppermute(value, axis, [(i, i ^ k) for i in range(n)])]
    all_to_all x1 -> x0, waiting for transfers between devices: 5.3 us -> none  [body(): lax.all_to_all(jnp.broadcast_to(mine, blocks.shape), 'ctx', 0, 0)]
    all_to_all x1 -> x0, starting transfers between devices: 3.64 us -> none  [body(): lax.all_to_all(jnp.broadcast_to(mine, blocks.shape), 'ctx', 0, 0)]
    broadcast_in_dim x1 -> x0, local copies, waits for them, and re-layouts: 0.83 us -> none  [body(): jnp.broadcast_to(mine, blocks.shape)]
    pallas_call x4 -> x5, Pallas kernels: 5.95 us -> 6.61 us  [the longest x1 2.7 us: body(): call(functools.partial(grads_kernel, n_rows, index_local), (shape(block,...]
    unnamed x14 -> x12, local copies, waits for them, and re-layouts: 6.13 us -> 6.25 us
  transfers between devices with their start and end apart: 9 -> 15, of which waited for: 6 -> 11; matrix products, arithmetic and copies ran while one was open for 3% -> 0% of each run, Pallas kernels for 6% -> 6%
where the time goes in v2:
time: 72 us; the launch traced here: 71.7 us
  waiting for transfers between devices  24.6 us (34%)
  starting transfers between devices  14.5 us (20%)
  blocking collectives  13.2 us (18%)
  Pallas kernels  12.3 us (17%)
  local copies, waits for them, and re-layouts  6.28 us (9%)
  between operations  0.73 us (1%)
    ppermute x15, waiting for transfers between devices, swapped(): return lax.ppermute(value, axis, [(i, i ^ k) for i in range(n)])  24.6 us
    ppermute x15, starting transfers between devices, swapped(): return lax.ppermute(value, axis, [(i, i ^ k) for i in range(n)])  14.5 us
    all_to_all x1, blocking collectives, body(): lax.all_to_all(jnp.broadcast_to(stats, (n_ctx,) + stats.shape), 'ctx', 0, 0)  13.2 us
    unnamed x12, local copies, waits for them, and re-layouts  6.25 us
    pallas_call x1, Pallas kernels, body(): call(functools.partial(scores_kernel, n_rows, heads_local), (shape((n_row...  4.33 us
    pallas_call x1, Pallas kernels, body(): call(functools.partial(grads_kernel, n_rows, index_local), (shape(block,...  2.7 us
    pallas_call x1, Pallas kernels, body(): call(functools.partial(logits_kernel, n_rows, index_local, (index_local *...  2.5 us
  transfers between devices with their start and end apart: 15, of which 11 were waited for; matrix products, arithmetic and copies ran while one was open for 0% of the time, Pallas kernels for 6%

profile of v2, /device:TPU:0, one launch (start us, length us, event | category | flops | bytes accessed | tf_op | source)
XLA Modules:
  0.0 71.7 jit_solution(10041917521463866481)
XLA Ops:
  0.6 1.7 %copy-done = bf16[64,32,576]{2,1,0:T(8,128)(2,1)S(1)} copy-done((bf16[64,32,576]{2,1,0:T(8,128)(2,1)S(1)}, bf16[64,32,576]{2,1,0:T(8,128)(2,1)}, u32[]{:S(2)}) %copy-start) | copy-done | bytes 2359320
  2.4 1.3 %copy-done.1 = bf16[1024,576]{0,1:T(8,128)(2,1)S(1)} copy-done((bf16[1024,576]{0,1:T(8,128)(2,1)S(1)}, bf16[1024,576]{0,1:T(8,128)(2,1)}, u32[]{:S(2)}) %copy-start.1) | copy-done | bytes 1179672
  3.6 0.9 %copy-done.2 = bf16[64,16,128]{2,1,0:T(8,128)(2,1)S(1)} copy-done((bf16[64,16,128]{2,1,0:T(8,128)(2,1)S(1)}, bf16[64,16,128]{2,1,0:T(8,128)(2,1)}, u32[]{:S(2)}) %copy-start.2) | copy-done | bytes 262168
  6.9 2.5 %shard_map.77 = (f32[64,512]{1,0:T(8,128)S(1)}, f32[64,512]{1,0:T(8,128)S(1)}, f32[64,1024]{1,0:T(8,128)S(1)}, bf16[1024,128]{1,0:T(8,128)(2,1)S(1)}, bf16[1024,...) custom-call(s32[64]{0:T(128)S(1)} %copy-done.5, ...), custom_call_target="tpu_custom_call" | custom-call | flops 268435456 | bytes 3538944 | tf_op jit(solution)/shard_map/pallas_call | solution.py:227
  10.0 1.0 %collective-permute-done = f32[64,512]{1,0:T(8,128)S(1)} collective-permute-done((f32[64,512]{1,0:T(8,128)S(1)}, f32[64,512]{1,0:T(8,128)S(1)}, u32[]{:S(2)}, u32[]{:S(2)}) %collective-permute-start) | collective-permute-done | bytes 131104 | tf_op jit(solution)/shard_map/ppermute | solution.py:224
  11.0 2.9 %collective-permute-start.1 = (f32[64,512]{1,0:T(8,128)S(1)}, f32[64,512]{1,0:T(8,128)S(1)}, u32[]{:S(2)}, u32[]{:S(2)}) collective-permute-start(f32[64,512]{1,0:T(8,128)S(1)} %add.21.mine_ref), channel_id=1, source_target_pairs={{0,2},{1,3},{2,0},{3,1},{4,6},{5,7},{6,4},{7,5},{8,10},{9,11},{10,... | collective-permute-start | bytes 393224 | tf_op jit(solution)/shard_map/ppermute | solution.py:224
  13.9 4.3 %shard_map.78 = (f32[2048,1024]{1,0:T(8,128)S(1)}, f32[32,128]{1,0:T(8,128)S(1)}) custom-call(f32[64,1024]{1,0:T(8,128)S(1)} %get-tuple-element.28.bias_ref, bf16[2048,576]{1,0:T(8,128)(2,1)S(1)} %get-tuple-element.29.q_ref, bf16[576,1024]{1,0:T(8,128)(2,1)S(1)} %get-tuple-element.30.lat_ref), custom_call_target="tpu_custom_call" | custom-call | flops 2415919104 | bytes 2359296 | tf_op jit(solution)/shard_map/pallas_call | solution.py:255
  18.5 13.2 %all_to_all.5.all_ref = f32[8,40,128]{2,1,0:T(8,128)S(1)} all-to-all(f32[8,40,128]{2,1,0:T(8,128)S(1)} %broadcast_in_dim.3), channel_id=1, replica_groups=mesh['ctx'=8,'heads'=4] {'ctx'}, dimensions={0} | all-to-all | bytes 327680 | tf_op jit(solution)/shard_map/all_to_all | solution.py:270
  31.7 1.3 %shard_map.80 = (f32[72,512]{1,0:T(8,128)S(1)}, f32[72,512]{1,0:T(8,128)S(1)}) custom-call(f32[8,40,128]{2,1,0:T(8,128)S(1)} %all_to_all.5.all_ref, f32[40,128]{1,0:T(8,128)S(1)} %get-tuple-element.32.own_ref, f32[2048,1024]{1,0:T(8,128)S(1)} %get-tuple-element.33.p_ref), custom_call_target="tpu_custom_call" | custom-call | tf_op jit(solution)/shard_map/pallas_call | solution.py:271
  33.1 1.4 %collective-permute-done.2.other_ref = f32[72,512]{1,0:T(8,128)S(1)} collective-permute-done((f32[72,512]{1,0:T(8,128)S(1)}, f32[72,512]{1,0:T(8,128)S(1)}, u32[]{:S(2)}, u32[]{:S(2)}) %collective-permute-start.2) | collective-permute-done | bytes 147488 | tf_op jit(solution)/shard_map/ppermute | solution.py:224
  34.4 1.3 %collective-permute-start.3 = (f32[64,512]{1,0:T(8,128)S(1)}, f32[64,512]{1,0:T(8,128)S(1)}, u32[]{:S(2)}, u32[]{:S(2)}) collective-permute-start(f32[64,512]{1,0:T(8,128)S(1)} %slice_add_fusion), channel_id=1, source_target_pairs={{0,2},{1,3},{2,0},{3,1},{4,6},{5,7},{6,4},{7,5},{8,10},{9,11},{10,... | collective-permute-start | bytes 393224 | tf_op jit(solution)/shard_map/ppermute | solution.py:224
  36.0 4.0 %collective-permute-done.3 = f32[64,512]{1,0:T(8,128)S(1)} collective-permute-done((f32[64,512]{1,0:T(8,128)S(1)}, f32[64,512]{1,0:T(8,128)S(1)}, u32[]{:S(2)}, u32[]{:S(2)}) %collective-permute-start.3) | collective-permute-done | bytes 131104 | tf_op jit(solution)/shard_map/ppermute | solution.py:224
  40.2 1.3 %collective-permute-done.4.other_ref = f32[64,512]{1,0:T(8,128)S(1)} collective-permute-done((f32[64,512]{1,0:T(8,128)S(1)}, f32[64,512]{1,0:T(8,128)S(1)}, u32[]{:S(2)}, u32[]{:S(2)}) %collective-permute-start.4) | collective-permute-done | bytes 131104 | tf_op jit(solution)/shard_map/ppermute | solution.py:224
  41.5 2.7 %shard_map.82 = (f32[256,128]{1,0:T(8,128)S(1)}, f32[256,128]{1,0:T(8,128)S(1)}, f32[256,128]{1,0:T(8,128)S(1)}, f32[256,128]{1,0:T(8,128)S(1)}, f32[256,128]{1,...) custom-call(f32[64,512]{1,0:T(8,128)S(1)} %subtract_multiply_fusion.mine_ref, ...), custom_call_target="tpu_custom_call" | custom-call | tf_op jit(solution)/shard_map/pallas_call | solution.py:290
  44.2 1.0 %collective-permute-start.5 = (f32[256,128]{1,0:T(8,128)S(1)}, f32[256,128]{1,0:T(8,128)S(1)}, u32[]{:S(2)}, u32[]{:S(2)}) collective-permute-start(f32[256,128]{1,0:T(8,128)S(1)} %get-tuple-element.41), channel_id=1, source_target_pairs={{0,4},{4,0},{8,12},{12,8},{16,20},{20,16},{24,28},{28,24},{1,5},{5... | collective-permute-start | bytes 393224 | tf_op jit(solution)/shard_map/ppermute | solution.py:224
  45.6 2.1 %collective-permute-start.7 = (f32[256,128]{1,0:T(8,128)S(1)}, f32[256,128]{1,0:T(8,128)S(1)}, u32[]{:S(2)}, u32[]{:S(2)}) collective-permute-start(f32[256,128]{1,0:T(8,128)S(1)} %get-tuple-element.43), channel_id=1, source_target_pairs={{0,12},{4,8},{8,4},{12,0},{16,28},{20,24},{24,20},{28,16},{1,13},{... | collective-permute-start | bytes 393224 | tf_op jit(solution)/shard_map/ppermute | solution.py:224
  47.8 2.1 %collective-permute-done.5 = f32[256,128]{1,0:T(8,128)S(1)} collective-permute-done((f32[256,128]{1,0:T(8,128)S(1)}, f32[256,128]{1,0:T(8,128)S(1)}, u32[]{:S(2)}, u32[]{:S(2)}) %collective-permute-start.5) | collective-permute-done | bytes 131104 | tf_op jit(solution)/shard_map/ppermute | solution.py:224
  49.8 1.8 %collective-permute-done.6 = f32[256,128]{1,0:T(8,128)S(1)} collective-permute-done((f32[256,128]{1,0:T(8,128)S(1)}, f32[256,128]{1,0:T(8,128)S(1)}, u32[]{:S(2)}, u32[]{:S(2)}) %collective-permute-start.6) | collective-permute-done | bytes 131104 | tf_op jit(solution)/shard_map/ppermute | solution.py:224
  51.6 2.2 %collective-permute-done.7 = f32[256,128]{1,0:T(8,128)S(1)} collective-permute-done((f32[256,128]{1,0:T(8,128)S(1)}, f32[256,128]{1,0:T(8,128)S(1)}, u32[]{:S(2)}, u32[]{:S(2)}) %collective-permute-start.7) | collective-permute-done | bytes 131104 | tf_op jit(solution)/shard_map/ppermute | solution.py:224
  54.5 1.0 %collective-permute-start.13 = (f32[256,128]{1,0:T(8,128)S(1)}, f32[256,128]{1,0:T(8,128)S(1)}, u32[]{:S(2)}, u32[]{:S(2)}) collective-permute-start(f32[256,128]{1,0:T(8,128)S(1)} %get-tuple-element.46), channel_id=1, source_target_pairs={{0,2},{1,3},{2,0},{3,1},{4,6},{5,7},{6,4},{7,5},{8,10},{9,11},{10,... | collective-permute-start | bytes 393224 | tf_op jit(solution)/shard_map/ppermute | solution.py:224
  56.3 5.6 %collective-permute-done.8 = f32[256,128]{1,0:T(8,128)S(1)} collective-permute-done((f32[256,128]{1,0:T(8,128)S(1)}, f32[256,128]{1,0:T(8,128)S(1)}, u32[]{:S(2)}, u32[]{:S(2)}) %collective-permute-start.8) | collective-permute-done | bytes 131104 | tf_op jit(solution)/shard_map/ppermute | solution.py:224
  62.0 2.5 %collective-permute-start.10 = (f32[256,128]{1,0:T(8,128)S(1)}, f32[256,128]{1,0:T(8,128)S(1)}, u32[]{:S(2)}, u32[]{:S(2)}) collective-permute-start(f32[256,128]{1,0:T(8,128)S(1)} %add.27.refs_0_), channel_id=1, source_target_pairs={{0,8},{4,12},{8,0},{12,4},{16,24},{20,28},{24,16},{28,20},{1,9},{5... | collective-permute-start | bytes 393224 | tf_op jit(solution)/shard_map/ppermute | solution.py:224
  65.5 3.8 %collective-permute-done.11.refs_3_ = f32[256,128]{1,0:T(8,128)S(1)} collective-permute-done((f32[256,128]{1,0:T(8,128)S(1)}, f32[256,128]{1,0:T(8,128)S(1)}, u32[]{:S(2)}, u32[]{:S(2)}) %collective-permute-start.11) | collective-permute-done | bytes 131104 | tf_op jit(solution)/shard_map/ppermute | solution.py:224
  69.2 1.2 %collective-permute-done.10.refs_2_ = f32[256,128]{1,0:T(8,128)S(1)} collective-permute-done((f32[256,128]{1,0:T(8,128)S(1)}, f32[256,128]{1,0:T(8,128)S(1)}, u32[]{:S(2)}, u32[]{:S(2)}) %collective-permute-start.10) | collective-permute-done | bytes 131104 | tf_op jit(solution)/shard_map/ppermute | solution.py:224
  (32 shorter events, 7.9 us)
Async XLA Ops:
  0.6 1.7 %copy-start = (bf16[64,32,576]{2,1,0:T(8,128)(2,1)S(1)}, bf16[64,32,576]{2,1,0:T(8,128)(2,1)}, u32[]{:S(2)}) copy-start(bf16[64,32,576]{2,1,0:T(8,128)(2,1)} %param.6) | copy-start | bytes 7077892
  2.4 1.3 %copy-start.1 = (bf16[1024,576]{0,1:T(8,128)(2,1)S(1)}, bf16[1024,576]{0,1:T(8,128)(2,1)}, u32[]{:S(2)}) copy-start(bf16[1024,576]{0,1:T(8,128)(2,1)} %param.7) | copy-start | bytes 3538948
  3.6 0.9 %copy-start.2 = (bf16[64,16,128]{2,1,0:T(8,128)(2,1)S(1)}, bf16[64,16,128]{2,1,0:T(8,128)(2,1)}, u32[]{:S(2)}) copy-start(bf16[64,16,128]{2,1,0:T(8,128)(2,1)} %param.8) | copy-start | bytes 786436
  4.6 0.9 %copy-start.3 = (bf16[1024,128]{1,0:T(8,128)(2,1)S(1)}, bf16[1024,128]{1,0:T(8,128)(2,1)}, u32[]{:S(2)}) copy-start(bf16[1024,128]{1,0:T(8,128)(2,1)} %ik_hbm.1) | copy-start | bytes 786436
  5.5 0.7 copy-start.4
  6.2 0.7 copy-start.5
  9.4 1.6 %collective-permute-start = (f32[64,512]{1,0:T(8,128)S(1)}, f32[64,512]{1,0:T(8,128)S(1)}, u32[]{:S(2)}, u32[]{:S(2)}) collective-permute-start(f32[64,512]{1,0:T(8,128)S(1)} %get-tuple-element.27), channel_id=1, source_target_pairs={{0,1},{1,0},{2,3},{3,2},{4,5},{5,4},{6,7},{7,6},{8,9},{9,8},{10,11... | collective-permute-start | bytes 393224 | tf_op jit(solution)/shard_map/ppermute | solution.py:224
  11.0 7.3 %collective-permute-start.1 = (f32[64,512]{1,0:T(8,128)S(1)}, f32[64,512]{1,0:T(8,128)S(1)}, u32[]{:S(2)}, u32[]{:S(2)}) collective-permute-start(f32[64,512]{1,0:T(8,128)S(1)} %add.21.mine_ref), channel_id=1, source_target_pairs={{0,2},{1,3},{2,0},{3,1},{4,6},{5,7},{6,4},{7,5},{8,10},{9,11},{10,... | collective-permute-start | bytes 393224 | tf_op jit(solution)/shard_map/ppermute | solution.py:224
  33.0 1.4 %collective-permute-start.2 = (f32[72,512]{1,0:T(8,128)S(1)}, f32[72,512]{1,0:T(8,128)S(1)}, u32[]{:S(2)}, u32[]{:S(2)}) collective-permute-start(f32[72,512]{1,0:T(8,128)S(1)} %get-tuple-element.35), channel_id=1, source_target_pairs={{0,1},{1,0},{2,3},{3,2},{4,5},{5,4},{6,7},{7,6},{8,9},{9,8},{10,11... | collective-permute-start | bytes 442376 | tf_op jit(solution)/shard_map/ppermute | solution.py:224
  34.4 5.6 %collective-permute-start.3 = (f32[64,512]{1,0:T(8,128)S(1)}, f32[64,512]{1,0:T(8,128)S(1)}, u32[]{:S(2)}, u32[]{:S(2)}) collective-permute-start(f32[64,512]{1,0:T(8,128)S(1)} %slice_add_fusion), channel_id=1, source_target_pairs={{0,2},{1,3},{2,0},{3,1},{4,6},{5,7},{6,4},{7,5},{8,10},{9,11},{10,... | collective-permute-start | bytes 393224 | tf_op jit(solution)/shard_map/ppermute | solution.py:224
  40.1 1.4 %collective-permute-start.4 = (f32[64,512]{1,0:T(8,128)S(1)}, f32[64,512]{1,0:T(8,128)S(1)}, u32[]{:S(2)}, u32[]{:S(2)}) collective-permute-start(f32[64,512]{1,0:T(8,128)S(1)} %subtract_multiply_fusion.mine_ref), channel_id=1, source_target_pairs={{0,1},{1,0},{2,3},{3,2},{4,5},{5,4},{6,7},{7,6},{8,9},{9,8},{10,11... | collective-permute-start | bytes 393224 | tf_op jit(solution)/shard_map/ppermute | solution.py:224
  44.2 5.6 %collective-permute-start.5 = (f32[256,128]{1,0:T(8,128)S(1)}, f32[256,128]{1,0:T(8,128)S(1)}, u32[]{:S(2)}, u32[]{:S(2)}) collective-permute-start(f32[256,128]{1,0:T(8,128)S(1)} %get-tuple-element.41), channel_id=1, source_target_pairs={{0,4},{4,0},{8,12},{12,8},{16,20},{20,16},{24,28},{28,24},{1,5},{5... | collective-permute-start | bytes 393224 | tf_op jit(solution)/shard_map/ppermute | solution.py:224
  45.2 6.4 %collective-permute-start.6 = (f32[256,128]{1,0:T(8,128)S(1)}, f32[256,128]{1,0:T(8,128)S(1)}, u32[]{:S(2)}, u32[]{:S(2)}) collective-permute-start(f32[256,128]{1,0:T(8,128)S(1)} %get-tuple-element.42), channel_id=1, source_target_pairs={{0,8},{4,12},{8,0},{12,4},{16,24},{20,28},{24,16},{28,20},{1,9},{5... | collective-permute-start | bytes 393224 | tf_op jit(solution)/shard_map/ppermute | solution.py:224
  45.6 8.2 %collective-permute-start.7 = (f32[256,128]{1,0:T(8,128)S(1)}, f32[256,128]{1,0:T(8,128)S(1)}, u32[]{:S(2)}, u32[]{:S(2)}) collective-permute-start(f32[256,128]{1,0:T(8,128)S(1)} %get-tuple-element.43), channel_id=1, source_target_pairs={{0,12},{4,8},{8,4},{12,0},{16,28},{20,24},{24,20},{28,16},{1,13},{... | collective-permute-start | bytes 393224 | tf_op jit(solution)/shard_map/ppermute | solution.py:224
  53.9 8.0 %collective-permute-start.8 = (f32[256,128]{1,0:T(8,128)S(1)}, f32[256,128]{1,0:T(8,128)S(1)}, u32[]{:S(2)}, u32[]{:S(2)}) collective-permute-start(f32[256,128]{1,0:T(8,128)S(1)} %add_add_fusion), channel_id=1, source_target_pairs={{0,16},{4,20},{8,24},{12,28},{16,0},{20,4},{24,8},{28,12},{1,17},{... | collective-permute-start | bytes 393224 | tf_op jit(solution)/shard_map/ppermute | solution.py:224
  54.5 10.1 %collective-permute-start.12 = (f32[256,128]{1,0:T(8,128)S(1)}, f32[256,128]{1,0:T(8,128)S(1)}, u32[]{:S(2)}, u32[]{:S(2)}) collective-permute-start(f32[256,128]{1,0:T(8,128)S(1)} %get-tuple-element.45), channel_id=1, source_target_pairs={{0,1},{1,0},{2,3},{3,2},{4,5},{5,4},{6,7},{7,6},{8,9},{9,8},{10,11... | collective-permute-start | bytes 393224 | tf_op jit(solution)/shard_map/ppermute | solution.py:224
  54.5 11.0 %collective-permute-start.13 = (f32[256,128]{1,0:T(8,128)S(1)}, f32[256,128]{1,0:T(8,128)S(1)}, u32[]{:S(2)}, u32[]{:S(2)}) collective-permute-start(f32[256,128]{1,0:T(8,128)S(1)} %get-tuple-element.46), channel_id=1, source_target_pairs={{0,2},{1,3},{2,0},{3,1},{4,6},{5,7},{6,4},{7,5},{8,10},{9,11},{10,... | collective-permute-start | bytes 393224 | tf_op jit(solution)/shard_map/ppermute | solution.py:224
  55.5 10.0 %collective-permute-start.14 = (f32[256,128]{1,0:T(8,128)S(1)}, f32[256,128]{1,0:T(8,128)S(1)}, u32[]{:S(2)}, u32[]{:S(2)}) collective-permute-start(f32[256,128]{1,0:T(8,128)S(1)} %get-tuple-element.47), channel_id=1, source_target_pairs={{0,3},{1,2},{2,1},{3,0},{4,7},{5,6},{6,5},{7,4},{8,11},{9,10},{10,... | collective-permute-start | bytes 393224 | tf_op jit(solution)/shard_map/ppermute | solution.py:224
  61.9 7.3 %collective-permute-start.11 = (f32[256,128]{1,0:T(8,128)S(1)}, f32[256,128]{1,0:T(8,128)S(1)}, u32[]{:S(2)}, u32[]{:S(2)}) collective-permute-start(f32[256,128]{1,0:T(8,128)S(1)} %add.27.refs_0_), channel_id=1, source_target_pairs={{0,12},{4,8},{8,4},{12,0},{16,28},{20,24},{24,20},{28,16},{1,13},{... | collective-permute-start | bytes 393224 | tf_op jit(solution)/shard_map/ppermute | solution.py:224
  62.0 8.4 %collective-permute-start.10 = (f32[256,128]{1,0:T(8,128)S(1)}, f32[256,128]{1,0:T(8,128)S(1)}, u32[]{:S(2)}, u32[]{:S(2)}) collective-permute-start(f32[256,128]{1,0:T(8,128)S(1)} %add.27.refs_0_), channel_id=1, source_target_pairs={{0,8},{4,12},{8,0},{12,4},{16,24},{20,28},{24,16},{28,20},{1,9},{5... | collective-permute-start | bytes 393224 | tf_op jit(solution)/shard_map/ppermute | solution.py:224
  64.5 6.3 %collective-permute-start.9 = (f32[256,128]{1,0:T(8,128)S(1)}, f32[256,128]{1,0:T(8,128)S(1)}, u32[]{:S(2)}, u32[]{:S(2)}) collective-permute-start(f32[256,128]{1,0:T(8,128)S(1)} %add.27.refs_0_), channel_id=1, source_target_pairs={{0,4},{4,0},{8,12},{12,8},{16,20},{20,16},{24,28},{28,24},{1,5},{5... | collective-permute-start | bytes 393224 | tf_op jit(solution)/shard_map/ppermute | solution.py:224

commit v3 on v2

--- a/solution.py
+++ b/solution.py
@@ -15,9 +15,9 @@
 NEG = -1e30
 LANES = 128
 VMEM = pl.BlockSpec(memory_space=pltpu.VMEM)
-SMEM = pl.BlockSpec(memory_space=pltpu.SMEM)
-HBM = pl.BlockSpec(memory_space=pl.ANY)
+HBM = pl.BlockSpec(memory_space=pltpu.HBM)
 CONTRACT_LAST = (((1,), (1,)), ((), ()))
+COLUMNS = 256
 QUAD = 4
 
 
@@ -41,23 +41,31 @@
 
 def logits_kernel(
     n_rows, n_heads, scale,
-    pos_ref, iq_hbm, ik_hbm, iw_hbm, q_hbm, lat_hbm,
+    pos_hbm, iq_hbm, ik_hbm, iw_hbm, q_hbm, lat_hbm,
     keep_ref, send_ref, bias_ref, iq_ref, ik_ref, iw_ref, q_ref, lat_ref,
-    part, sems,
+    part, pos_ref, sems,
 ):
     half = keep_ref.shape[1]
     copies = [
         pltpu.make_async_copy(a, b, sems.at[i])
         for i, (a, b) in enumerate(
-            ((ik_hbm, ik_ref), (iq_hbm, iq_ref), (iw_hbm, iw_ref), (lat_hbm, lat_ref), (q_hbm, q_ref))
+            (
+                (pos_hbm, pos_ref),
+                (ik_hbm, ik_ref),
+                (iq_hbm, iq_ref),
+                (iw_hbm, iw_ref),
+                (lat_hbm, lat_ref),
+                (q_hbm, q_ref),
+            )
         )
     ]
     for copy in copies:
         copy.start()
+    copies[0].wait()
     place = lax.axis_index("ctx") * 2 * half + lax.broadcasted_iota(jnp.int32, (1, 2 * half), 1)
     for row in range(n_rows):
         bias_ref[row : row + 1, :] = jnp.where(place <= pos_ref[row], 0.0, NEG)
-    for copy in copies[:3]:
+    for copy in copies[1:4]:
         copy.wait()
     iw_ref[...] = iw_ref[...] * scale
     rows = LANES
@@ -77,26 +85,36 @@
     mine, other = half_at(core, half), half_at(1 - core, half)
     keep_ref[...] = part[:, mine] + bias_ref[:, mine]
     send_ref[...] = part[:, other]
-    for copy in copies[3:]:
+    for copy in copies[4:]:
         copy.wait()
 
 
 def scores_kernel(n_rows, n_heads, bias_ref, q_ref, lat_ref, p_ref, stat_ref, s_even, s_odd):
-    block = 256
-    per = block // n_heads
-    for b in range(n_rows * n_heads // block):
-        held = s_even if b % 2 == 0 else s_odd
-        held[...] = jnp.dot(
-            q_ref[b * block : (b + 1) * block, :], lat_ref[...], preferred_element_type=F32
-        )
-        for i in range(per):
-            row = b * per + i
-            x = held[i * n_heads : (i + 1) * n_heads, :] + bias_ref[row : row + 1, :]
-            top = jnp.max(x, axis=1, keepdims=True)
-            e = jnp.exp2((x - top) * SCORE_LOG2)
-            p_ref[row * n_heads : (row + 1) * n_heads, :] = e
-            stat_ref[:, row : row + 1] = top
-            stat_ref[:, n_rows + row : n_rows + row + 1] = jnp.sum(e, axis=1, keepdims=True)
+    block = s_even.shape[0]
+    keys = lat_ref.shape[1]
+    steps = keys // COLUMNS
+    per = block // n_heads // steps
+    strips = n_rows * n_heads // block * steps
+    for step in range(strips + steps):
+        if step < strips:
+            b, n = divmod(step, steps)
+            held = s_even if b % 2 == 0 else s_odd
+            held[:, n * COLUMNS : (n + 1) * COLUMNS] = jnp.dot(
+                q_ref[b * block : (b + 1) * block, :],
+                lat_ref[:, n * COLUMNS : (n + 1) * COLUMNS],
+                preferred_element_type=F32,
+            )
+        if step >= steps:
+            b, n = divmod(step - steps, steps)
+            held = s_even if b % 2 == 0 else s_odd
+            for i in range(n * per, (n + 1) * per):
+                row = b * (block // n_heads) + i
+                x = held[i * n_heads : (i + 1) * n_heads, :] + bias_ref[row : row + 1, :]
+                top = jnp.max(x, axis=1, keepdims=True)
+                e = jnp.exp2((x - top) * SCORE_LOG2)
+                p_ref[row * n_heads : (row + 1) * n_heads, :] = e
+                stat_ref[:, row : row + 1] = top
+                stat_ref[:, n_rows + row : n_rows + row + 1] = jnp.sum(e, axis=1, keepdims=True)
 
 
 def index_stats_kernel(mine_ref, other_ref, stat_ref, e_ref, out_ref, col):
@@ -238,17 +256,26 @@
             shape((n_rows * heads_local, width), BF16),
             shape((width, keys), BF16),
         ),
-        [SMEM] + [HBM] * 5,
-        scratch=[pltpu.VMEM((n_rows, keys), F32), pltpu.SemaphoreType.DMA((5,))],
+        [HBM] * 6,
+        scratch=[
+            pltpu.VMEM((n_rows, keys), F32),
+            pltpu.SMEM((n_rows,), jnp.int32),
+            pltpu.SemaphoreType.DMA((6,)),
+        ],
         flops=2 * flat[0] * depth * keys,
         nbytes=queries.size * 2 + latents.size * 2,
     )(
-        positions,
-        index_queries.reshape(flat),
-        index_keys,
-        index_weights.T,
-        queries.reshape(n_rows * heads_local, width),
-        latents.T,
+        *(
+            pltpu.with_memory_space_constraint(x, pltpu.HBM)
+            for x in (
+                positions,
+                index_queries.reshape(flat),
+                index_keys,
+                index_weights.T,
+                queries.reshape(n_rows * heads_local, width),
+                latents.T,
+            )
+        ),
     )
     logit_mine = keep + swapped(send, "heads", 1)
     logit_other = swapped(logit_mine, "heads", 2)

time: 72 us -> 65.3 us (0.907)
  local copies, waits for them, and re-layouts: 6.28 us -> 0.03 us
    unnamed x12 -> x0, local copies, waits for them, and re-layouts: 6.25 us -> none
  transfers between devices with their start and end apart: 15 -> 15, of which waited for: 11 -> 11; matrix products, arithmetic and copies ran while one was open for 0% -> 0% of each run, Pallas kernels for 6% -> 7%
where the time goes in v3:
time: 65.3 us; the launch traced here: 65.1 us
  waiting for transfers between devices  24.5 us (38%)
  starting transfers between devices  14.6 us (22%)
  blocking collectives  13.2 us (20%)
  Pallas kernels  12 us (18%)
  between operations  0.71 us (1%)
    ppermute x15, waiting for transfers between devices, swapped(): return lax.ppermute(value, axis, [(i, i ^ k) for i in range(n)])  24.5 us
    ppermute x15, starting transfers between devices, swapped(): return lax.ppermute(value, axis, [(i, i ^ k) for i in range(n)])  14.6 us
    all_to_all x1, blocking collectives, body(): lax.all_to_all(jnp.broadcast_to(stats, (n_ctx,) + stats.shape), 'ctx', 0, 0)  13.2 us
    pallas_call x1, Pallas kernels, body(): call(functools.partial(scores_kernel, n_rows, heads_local), (shape((n_row...  4.21 us
    pallas_call x1, Pallas kernels, body(): call(functools.partial(grads_kernel, n_rows, index_local), (shape(block,...  2.7 us
    pallas_call x1, Pallas kernels, body(): call(functools.partial(logits_kernel, n_rows, index_local, (index_local *...  2.34 us
    pallas_call x1, Pallas kernels, body(): call(functools.partial(target_kernel, n_rows, heads_local), (shape((n_row...  1.32 us
  transfers between devices with their start and end apart: 15, of which 11 were waited for; matrix products, arithmetic and copies ran while one was open for 0% of the time, Pallas kernels for 7%

profile of v3, /device:TPU:0, one launch (start us, length us, event | category | flops | bytes accessed | tf_op | source)
XLA Modules:
  0.0 65.1 jit_solution(16280708713133419475)
XLA Ops:
  0.6 2.3 %shard_map.77 = (f32[64,512]{1,0:T(8,128)S(1)}, f32[64,512]{1,0:T(8,128)S(1)}, f32[64,1024]{1,0:T(8,128)S(1)}, bf16[1024,128]{1,0:T(8,128)(2,1)S(1)}, bf16[1024,...) custom-call(s32[64]{0:T(128)} %pos_hbm.1, ...), custom_call_target="tpu_custom_call" | custom-call | flops 268435456 | bytes 3538944 | tf_op jit(solution)/shard_map/pallas_call | solution.py:245
  3.5 1.0 %collective-permute-done = f32[64,512]{1,0:T(8,128)S(1)} collective-permute-done((f32[64,512]{1,0:T(8,128)S(1)}, f32[64,512]{1,0:T(8,128)S(1)}, u32[]{:S(2)}, u32[]{:S(2)}) %collective-permute-start) | collective-permute-done | bytes 131104 | tf_op jit(solution)/shard_map/ppermute | solution.py:242
  4.6 2.9 %collective-permute-start.1 = (f32[64,512]{1,0:T(8,128)S(1)}, f32[64,512]{1,0:T(8,128)S(1)}, u32[]{:S(2)}, u32[]{:S(2)}) collective-permute-start(f32[64,512]{1,0:T(8,128)S(1)} %add.21.mine_ref), channel_id=1, source_target_pairs={{0,2},{1,3},{2,0},{3,1},{4,6},{5,7},{6,4},{7,5},{8,10},{9,11},{10,... | collective-permute-start | bytes 393224 | tf_op jit(solution)/shard_map/ppermute | solution.py:242
  7.5 4.2 %shard_map.78 = (f32[2048,1024]{1,0:T(8,128)S(1)}, f32[32,128]{1,0:T(8,128)S(1)}) custom-call(f32[64,1024]{1,0:T(8,128)S(1)} %get-tuple-element.28.bias_ref, bf16[2048,576]{1,0:T(8,128)(2,1)S(1)} %get-tuple-element.29.q_ref, bf16[576,1024]{1,0:T(8,128)(2,1)S(1)} %get-tuple-element.30.lat_ref), custom_call_target="tpu_custom_call" | custom-call | flops 2415919104 | bytes 2359296 | tf_op jit(solution)/shard_map/pallas_call | solution.py:282
  11.9 13.2 %all_to_all.5.all_ref = f32[8,40,128]{2,1,0:T(8,128)S(1)} all-to-all(f32[8,40,128]{2,1,0:T(8,128)S(1)} %broadcast_in_dim.3), channel_id=1, replica_groups=mesh['ctx'=8,'heads'=4] {'ctx'}, dimensions={0} | all-to-all | bytes 327680 | tf_op jit(solution)/shard_map/all_to_all | solution.py:297
  25.1 1.3 %shard_map.80 = (f32[72,512]{1,0:T(8,128)S(1)}, f32[72,512]{1,0:T(8,128)S(1)}) custom-call(f32[8,40,128]{2,1,0:T(8,128)S(1)} %all_to_all.5.all_ref, f32[40,128]{1,0:T(8,128)S(1)} %get-tuple-element.32.own_ref, f32[2048,1024]{1,0:T(8,128)S(1)} %get-tuple-element.33.p_ref), custom_call_target="tpu_custom_call" | custom-call | tf_op jit(solution)/shard_map/pallas_call | solution.py:298
  26.5 1.4 %collective-permute-done.2.other_ref = f32[72,512]{1,0:T(8,128)S(1)} collective-permute-done((f32[72,512]{1,0:T(8,128)S(1)}, f32[72,512]{1,0:T(8,128)S(1)}, u32[]{:S(2)}, u32[]{:S(2)}) %collective-permute-start.2) | collective-permute-done | bytes 147488 | tf_op jit(solution)/shard_map/ppermute | solution.py:242
  27.9 1.4 %collective-permute-start.3 = (f32[64,512]{1,0:T(8,128)S(1)}, f32[64,512]{1,0:T(8,128)S(1)}, u32[]{:S(2)}, u32[]{:S(2)}) collective-permute-start(f32[64,512]{1,0:T(8,128)S(1)} %slice_add_fusion), channel_id=1, source_target_pairs={{0,2},{1,3},{2,0},{3,1},{4,6},{5,7},{6,4},{7,5},{8,10},{9,11},{10,... | collective-permute-start | bytes 393224 | tf_op jit(solution)/shard_map/ppermute | solution.py:242
  29.6 3.9 %collective-permute-done.3 = f32[64,512]{1,0:T(8,128)S(1)} collective-permute-done((f32[64,512]{1,0:T(8,128)S(1)}, f32[64,512]{1,0:T(8,128)S(1)}, u32[]{:S(2)}, u32[]{:S(2)}) %collective-permute-start.3) | collective-permute-done | bytes 131104 | tf_op jit(solution)/shard_map/ppermute | solution.py:242
  33.6 1.3 %collective-permute-done.4.other_ref = f32[64,512]{1,0:T(8,128)S(1)} collective-permute-done((f32[64,512]{1,0:T(8,128)S(1)}, f32[64,512]{1,0:T(8,128)S(1)}, u32[]{:S(2)}, u32[]{:S(2)}) %collective-permute-start.4) | collective-permute-done | bytes 131104 | tf_op jit(solution)/shard_map/ppermute | solution.py:242
  34.9 2.7 %shard_map.82 = (f32[256,128]{1,0:T(8,128)S(1)}, f32[256,128]{1,0:T(8,128)S(1)}, f32[256,128]{1,0:T(8,128)S(1)}, f32[256,128]{1,0:T(8,128)S(1)}, f32[256,128]{1,...) custom-call(f32[64,512]{1,0:T(8,128)S(1)} %subtract_multiply_fusion.mine_ref, ...), custom_call_target="tpu_custom_call" | custom-call | tf_op jit(solution)/shard_map/pallas_call | solution.py:317
  37.7 1.0 %collective-permute-start.5 = (f32[256,128]{1,0:T(8,128)S(1)}, f32[256,128]{1,0:T(8,128)S(1)}, u32[]{:S(2)}, u32[]{:S(2)}) collective-permute-start(f32[256,128]{1,0:T(8,128)S(1)} %get-tuple-element.41), channel_id=1, source_target_pairs={{0,4},{4,0},{8,12},{12,8},{16,20},{20,16},{24,28},{28,24},{1,5},{5... | collective-permute-start | bytes 393224 | tf_op jit(solution)/shard_map/ppermute | solution.py:242
  39.1 2.2 %collective-permute-start.7 = (f32[256,128]{1,0:T(8,128)S(1)}, f32[256,128]{1,0:T(8,128)S(1)}, u32[]{:S(2)}, u32[]{:S(2)}) collective-permute-start(f32[256,128]{1,0:T(8,128)S(1)} %get-tuple-element.43), channel_id=1, source_target_pairs={{0,12},{4,8},{8,4},{12,0},{16,28},{20,24},{24,20},{28,16},{1,13},{... | collective-permute-start | bytes 393224 | tf_op jit(solution)/shard_map/ppermute | solution.py:242
  41.2 2.1 %collective-permute-done.5 = f32[256,128]{1,0:T(8,128)S(1)} collective-permute-done((f32[256,128]{1,0:T(8,128)S(1)}, f32[256,128]{1,0:T(8,128)S(1)}, u32[]{:S(2)}, u32[]{:S(2)}) %collective-permute-start.5) | collective-permute-done | bytes 131104 | tf_op jit(solution)/shard_map/ppermute | solution.py:242
  43.3 1.8 %collective-permute-done.6 = f32[256,128]{1,0:T(8,128)S(1)} collective-permute-done((f32[256,128]{1,0:T(8,128)S(1)}, f32[256,128]{1,0:T(8,128)S(1)}, u32[]{:S(2)}, u32[]{:S(2)}) %collective-permute-start.6) | collective-permute-done | bytes 131104 | tf_op jit(solution)/shard_map/ppermute | solution.py:242
  45.0 2.2 %collective-permute-done.7 = f32[256,128]{1,0:T(8,128)S(1)} collective-permute-done((f32[256,128]{1,0:T(8,128)S(1)}, f32[256,128]{1,0:T(8,128)S(1)}, u32[]{:S(2)}, u32[]{:S(2)}) %collective-permute-start.7) | collective-permute-done | bytes 131104 | tf_op jit(solution)/shard_map/ppermute | solution.py:242
  47.9 1.1 %collective-permute-start.13 = (f32[256,128]{1,0:T(8,128)S(1)}, f32[256,128]{1,0:T(8,128)S(1)}, u32[]{:S(2)}, u32[]{:S(2)}) collective-permute-start(f32[256,128]{1,0:T(8,128)S(1)} %get-tuple-element.46), channel_id=1, source_target_pairs={{0,2},{1,3},{2,0},{3,1},{4,6},{5,7},{6,4},{7,5},{8,10},{9,11},{10,... | collective-permute-start | bytes 393224 | tf_op jit(solution)/shard_map/ppermute | solution.py:242
  49.1 0.7 %collective-permute-start.14 = (f32[256,128]{1,0:T(8,128)S(1)}, f32[256,128]{1,0:T(8,128)S(1)}, u32[]{:S(2)}, u32[]{:S(2)}) collective-permute-start(f32[256,128]{1,0:T(8,128)S(1)} %get-tuple-element.47), channel_id=1, source_target_pairs={{0,3},{1,2},{2,1},{3,0},{4,7},{5,6},{6,5},{7,4},{8,11},{9,10},{10,... | collective-permute-start | bytes 393224 | tf_op jit(solution)/shard_map/ppermute | solution.py:242
  49.8 5.6 %collective-permute-done.8 = f32[256,128]{1,0:T(8,128)S(1)} collective-permute-done((f32[256,128]{1,0:T(8,128)S(1)}, f32[256,128]{1,0:T(8,128)S(1)}, u32[]{:S(2)}, u32[]{:S(2)}) %collective-permute-start.8) | collective-permute-done | bytes 131104 | tf_op jit(solution)/shard_map/ppermute | solution.py:242
  55.5 2.5 %collective-permute-start.10 = (f32[256,128]{1,0:T(8,128)S(1)}, f32[256,128]{1,0:T(8,128)S(1)}, u32[]{:S(2)}, u32[]{:S(2)}) collective-permute-start(f32[256,128]{1,0:T(8,128)S(1)} %add.27.refs_0_), channel_id=1, source_target_pairs={{0,8},{4,12},{8,0},{12,4},{16,24},{20,28},{24,16},{28,20},{1,9},{5... | collective-permute-start | bytes 393224 | tf_op jit(solution)/shard_map/ppermute | solution.py:242
  58.0 1.0 %collective-permute-start.9 = (f32[256,128]{1,0:T(8,128)S(1)}, f32[256,128]{1,0:T(8,128)S(1)}, u32[]{:S(2)}, u32[]{:S(2)}) collective-permute-start(f32[256,128]{1,0:T(8,128)S(1)} %add.27.refs_0_), channel_id=1, source_target_pairs={{0,4},{4,0},{8,12},{12,8},{16,20},{20,16},{24,28},{28,24},{1,5},{5... | collective-permute-start | bytes 393224 | tf_op jit(solution)/shard_map/ppermute | solution.py:242
  58.9 3.8 %collective-permute-done.11.refs_3_ = f32[256,128]{1,0:T(8,128)S(1)} collective-permute-done((f32[256,128]{1,0:T(8,128)S(1)}, f32[256,128]{1,0:T(8,128)S(1)}, u32[]{:S(2)}, u32[]{:S(2)}) %collective-permute-start.11) | collective-permute-done | bytes 131104 | tf_op jit(solution)/shard_map/ppermute | solution.py:242
  62.7 1.2 %collective-permute-done.10.refs_2_ = f32[256,128]{1,0:T(8,128)S(1)} collective-permute-done((f32[256,128]{1,0:T(8,128)S(1)}, f32[256,128]{1,0:T(8,128)S(1)}, u32[]{:S(2)}, u32[]{:S(2)}) %collective-permute-start.10) | collective-permute-done | bytes 131104 | tf_op jit(solution)/shard_map/ppermute | solution.py:242
  64.3 0.9 %shard_map.83 = (f32[1024,128]{1,0:T(8,128)}, f32[256,128]{1,0:T(8,128)}) custom-call(f32[256,128]{1,0:T(8,128)S(1)} %add.27.refs_0_, f32[256,128]{1,0:T(8,128)S(1)} %collective-permute-done.9.refs_1_, f32[256,128]{1,0:T(8,128)S(1)} %collective-permute-done.10.refs_2_, f32[256,128]{1,0:T(8,128)S(1)} %collective-permute-done.11.refs_3_, ...), custom_call_target="tpu_custom_call" | custom-call | tf_op jit(solution)/shard_map/pallas_call | solution.py:335
  (20 shorter events, 2.8 us)
Async XLA Ops:
  3.0 1.5 %collective-permute-start = (f32[64,512]{1,0:T(8,128)S(1)}, f32[64,512]{1,0:T(8,128)S(1)}, u32[]{:S(2)}, u32[]{:S(2)}) collective-permute-start(f32[64,512]{1,0:T(8,128)S(1)} %get-tuple-element.27), channel_id=1, source_target_pairs={{0,1},{1,0},{2,3},{3,2},{4,5},{5,4},{6,7},{7,6},{8,9},{9,8},{10,11... | collective-permute-start | bytes 393224 | tf_op jit(solution)/shard_map/ppermute | solution.py:242
  4.6 7.1 %collective-permute-start.1 = (f32[64,512]{1,0:T(8,128)S(1)}, f32[64,512]{1,0:T(8,128)S(1)}, u32[]{:S(2)}, u32[]{:S(2)}) collective-permute-start(f32[64,512]{1,0:T(8,128)S(1)} %add.21.mine_ref), channel_id=1, source_target_pairs={{0,2},{1,3},{2,0},{3,1},{4,6},{5,7},{6,4},{7,5},{8,10},{9,11},{10,... | collective-permute-start | bytes 393224 | tf_op jit(solution)/shard_map/ppermute | solution.py:242
  26.4 1.4 %collective-permute-start.2 = (f32[72,512]{1,0:T(8,128)S(1)}, f32[72,512]{1,0:T(8,128)S(1)}, u32[]{:S(2)}, u32[]{:S(2)}) collective-permute-start(f32[72,512]{1,0:T(8,128)S(1)} %get-tuple-element.35), channel_id=1, source_target_pairs={{0,1},{1,0},{2,3},{3,2},{4,5},{5,4},{6,7},{7,6},{8,9},{9,8},{10,11... | collective-permute-start | bytes 442376 | tf_op jit(solution)/shard_map/ppermute | solution.py:242
  27.9 5.6 %collective-permute-start.3 = (f32[64,512]{1,0:T(8,128)S(1)}, f32[64,512]{1,0:T(8,128)S(1)}, u32[]{:S(2)}, u32[]{:S(2)}) collective-permute-start(f32[64,512]{1,0:T(8,128)S(1)} %slice_add_fusion), channel_id=1, source_target_pairs={{0,2},{1,3},{2,0},{3,1},{4,6},{5,7},{6,4},{7,5},{8,10},{9,11},{10,... | collective-permute-start | bytes 393224 | tf_op jit(solution)/shard_map/ppermute | solution.py:242
  33.5 1.4 %collective-permute-start.4 = (f32[64,512]{1,0:T(8,128)S(1)}, f32[64,512]{1,0:T(8,128)S(1)}, u32[]{:S(2)}, u32[]{:S(2)}) collective-permute-start(f32[64,512]{1,0:T(8,128)S(1)} %subtract_multiply_fusion.mine_ref), channel_id=1, source_target_pairs={{0,1},{1,0},{2,3},{3,2},{4,5},{5,4},{6,7},{7,6},{8,9},{9,8},{10,11... | collective-permute-start | bytes 393224 | tf_op jit(solution)/shard_map/ppermute | solution.py:242
  37.7 5.6 %collective-permute-start.5 = (f32[256,128]{1,0:T(8,128)S(1)}, f32[256,128]{1,0:T(8,128)S(1)}, u32[]{:S(2)}, u32[]{:S(2)}) collective-permute-start(f32[256,128]{1,0:T(8,128)S(1)} %get-tuple-element.41), channel_id=1, source_target_pairs={{0,4},{4,0},{8,12},{12,8},{16,20},{20,16},{24,28},{28,24},{1,5},{5... | collective-permute-start | bytes 393224 | tf_op jit(solution)/shard_map/ppermute | solution.py:242
  38.7 6.4 %collective-permute-start.6 = (f32[256,128]{1,0:T(8,128)S(1)}, f32[256,128]{1,0:T(8,128)S(1)}, u32[]{:S(2)}, u32[]{:S(2)}) collective-permute-start(f32[256,128]{1,0:T(8,128)S(1)} %get-tuple-element.42), channel_id=1, source_target_pairs={{0,8},{4,12},{8,0},{12,4},{16,24},{20,28},{24,16},{28,20},{1,9},{5... | collective-permute-start | bytes 393224 | tf_op jit(solution)/shard_map/ppermute | solution.py:242
  39.1 8.2 %collective-permute-start.7 = (f32[256,128]{1,0:T(8,128)S(1)}, f32[256,128]{1,0:T(8,128)S(1)}, u32[]{:S(2)}, u32[]{:S(2)}) collective-permute-start(f32[256,128]{1,0:T(8,128)S(1)} %get-tuple-element.43), channel_id=1, source_target_pairs={{0,12},{4,8},{8,4},{12,0},{16,28},{20,24},{24,20},{28,16},{1,13},{... | collective-permute-start | bytes 393224 | tf_op jit(solution)/shard_map/ppermute | solution.py:242
  47.3 8.0 %collective-permute-start.8 = (f32[256,128]{1,0:T(8,128)S(1)}, f32[256,128]{1,0:T(8,128)S(1)}, u32[]{:S(2)}, u32[]{:S(2)}) collective-permute-start(f32[256,128]{1,0:T(8,128)S(1)} %add_add_fusion), channel_id=1, source_target_pairs={{0,16},{4,20},{8,24},{12,28},{16,0},{20,4},{24,8},{28,12},{1,17},{... | collective-permute-start | bytes 393224 | tf_op jit(solution)/shard_map/ppermute | solution.py:242
  47.9 10.1 %collective-permute-start.12 = (f32[256,128]{1,0:T(8,128)S(1)}, f32[256,128]{1,0:T(8,128)S(1)}, u32[]{:S(2)}, u32[]{:S(2)}) collective-permute-start(f32[256,128]{1,0:T(8,128)S(1)} %get-tuple-element.45), channel_id=1, source_target_pairs={{0,1},{1,0},{2,3},{3,2},{4,5},{5,4},{6,7},{7,6},{8,9},{9,8},{10,11... | collective-permute-start | bytes 393224 | tf_op jit(solution)/shard_map/ppermute | solution.py:242
  47.9 11.0 %collective-permute-start.13 = (f32[256,128]{1,0:T(8,128)S(1)}, f32[256,128]{1,0:T(8,128)S(1)}, u32[]{:S(2)}, u32[]{:S(2)}) collective-permute-start(f32[256,128]{1,0:T(8,128)S(1)} %get-tuple-element.46), channel_id=1, source_target_pairs={{0,2},{1,3},{2,0},{3,1},{4,6},{5,7},{6,4},{7,5},{8,10},{9,11},{10,... | collective-permute-start | bytes 393224 | tf_op jit(solution)/shard_map/ppermute | solution.py:242
  49.1 9.9 %collective-permute-start.14 = (f32[256,128]{1,0:T(8,128)S(1)}, f32[256,128]{1,0:T(8,128)S(1)}, u32[]{:S(2)}, u32[]{:S(2)}) collective-permute-start(f32[256,128]{1,0:T(8,128)S(1)} %get-tuple-element.47), channel_id=1, source_target_pairs={{0,3},{1,2},{2,1},{3,0},{4,7},{5,6},{6,5},{7,4},{8,11},{9,10},{10,... | collective-permute-start | bytes 393224 | tf_op jit(solution)/shard_map/ppermute | solution.py:242
  55.4 7.3 %collective-permute-start.11 = (f32[256,128]{1,0:T(8,128)S(1)}, f32[256,128]{1,0:T(8,128)S(1)}, u32[]{:S(2)}, u32[]{:S(2)}) collective-permute-start(f32[256,128]{1,0:T(8,128)S(1)} %add.27.refs_0_), channel_id=1, source_target_pairs={{0,12},{4,8},{8,4},{12,0},{16,28},{20,24},{24,20},{28,16},{1,13},{... | collective-permute-start | bytes 393224 | tf_op jit(solution)/shard_map/ppermute | solution.py:242
  55.5 8.4 %collective-permute-start.10 = (f32[256,128]{1,0:T(8,128)S(1)}, f32[256,128]{1,0:T(8,128)S(1)}, u32[]{:S(2)}, u32[]{:S(2)}) collective-permute-start(f32[256,128]{1,0:T(8,128)S(1)} %add.27.refs_0_), channel_id=1, source_target_pairs={{0,8},{4,12},{8,0},{12,4},{16,24},{20,28},{24,16},{28,20},{1,9},{5... | collective-permute-start | bytes 393224 | tf_op jit(solution)/shard_map/ppermute | solution.py:242
  58.0 6.3 %collective-permute-start.9 = (f32[256,128]{1,0:T(8,128)S(1)}, f32[256,128]{1,0:T(8,128)S(1)}, u32[]{:S(2)}, u32[]{:S(2)}) collective-permute-start(f32[256,128]{1,0:T(8,128)S(1)} %add.27.refs_0_), channel_id=1, source_target_pairs={{0,4},{4,0},{8,12},{12,8},{16,20},{20,16},{24,28},{28,24},{1,5},{5... | collective-permute-start | bytes 393224 | tf_op jit(solution)/shard_map/ppermute | solution.py:242

commit v4 on v3

--- a/solution.py
+++ b/solution.py
@@ -7,6 +7,7 @@
 from jax.experimental import pallas as pl
 from jax.experimental.pallas import tpu as pltpu
 from jax.sharding import PartitionSpec as P
+
 
 F32 = jnp.float32
 BF16 = jnp.bfloat16
@@ -39,21 +40,38 @@
     return pl.ds(pl.multiple_of(core * half, LANES), half)
 
 
+def head_sums(n_rows, n_heads, iq_ref, keys, w_ref, out_ref):
+    rows = 256
+    per = rows // n_heads
+    for b in range(n_rows * n_heads // rows):
+        dots = lax.dot_general(
+            iq_ref[b * rows : (b + 1) * rows, :], keys, CONTRACT_LAST, preferred_element_type=F32
+        )
+        for i in range(per):
+            row = b * per + i
+            at = slice(row * n_heads, (row + 1) * n_heads)
+            out_ref[row : row + 1, :] = jnp.sum(
+                jnp.maximum(dots[i * n_heads : (i + 1) * n_heads, :], 0.0) * w_ref[at, 0:1],
+                axis=0,
+                keepdims=True,
+            )
+
+
 def logits_kernel(
     n_rows, n_heads, scale,
     pos_hbm, iq_hbm, ik_hbm, iw_hbm, q_hbm, lat_hbm,
-    keep_ref, send_ref, bias_ref, iq_ref, ik_ref, iw_ref, q_ref, lat_ref,
-    part, pos_ref, sems,
+    send_ref, bias_ref, iq_ref, ik_ref, w_ref, q_ref, lat_ref,
+    iw_ref, pos_ref, sems,
 ):
-    half = keep_ref.shape[1]
+    half = send_ref.shape[1]
     copies = [
         pltpu.make_async_copy(a, b, sems.at[i])
         for i, (a, b) in enumerate(
             (
                 (pos_hbm, pos_ref),
+                (iw_hbm, iw_ref),
                 (ik_hbm, ik_ref),
                 (iq_hbm, iq_ref),
-                (iw_hbm, iw_ref),
                 (lat_hbm, lat_ref),
                 (q_hbm, q_ref),
             )
@@ -62,31 +80,31 @@
     for copy in copies:
         copy.start()
     copies[0].wait()
-    place = lax.axis_index("ctx") * 2 * half + lax.broadcasted_iota(jnp.int32, (1, 2 * half), 1)
+    place = lax.axis_index("ctx") * 2 * half + lax.broadcasted_iota(jnp.int32, (8, 2 * half), 1)
+    sublane = lax.broadcasted_iota(jnp.int32, (8, 1), 0)
+    for first in range(0, n_rows, 8):
+        pos = jnp.zeros((8, 1), jnp.int32)
+        for i in range(8):
+            pos = jnp.where(sublane == i, pos_ref[first + i], pos)
+        bias_ref[first : first + 8, :] = jnp.where(place <= pos, 0.0, NEG)
+    copies[1].wait()
     for row in range(n_rows):
-        bias_ref[row : row + 1, :] = jnp.where(place <= pos_ref[row], 0.0, NEG)
-    for copy in copies[1:4]:
-        copy.wait()
-    iw_ref[...] = iw_ref[...] * scale
-    rows = LANES
-    per = rows // n_heads
-    for b in range(n_rows * n_heads // rows):
-        dots = lax.dot_general(
-            iq_ref[b * rows : (b + 1) * rows, :], ik_ref[...], CONTRACT_LAST, preferred_element_type=F32
+        w_ref[row * n_heads : (row + 1) * n_heads, :] = jnp.broadcast_to(
+            iw_ref[:, row : row + 1] * scale, (n_heads, LANES)
         )
-        for i in range(per):
-            row = b * per + i
-            part[row : row + 1, :] = jnp.sum(
-                jnp.maximum(dots[i * n_heads : (i + 1) * n_heads, :], 0.0) * iw_ref[:, row : row + 1],
-                axis=0,
-                keepdims=True,
-            )
+    copies[2].wait()
+    copies[3].wait()
     core = lax.axis_index("heads") & 1
-    mine, other = half_at(core, half), half_at(1 - core, half)
-    keep_ref[...] = part[:, mine] + bias_ref[:, mine]
-    send_ref[...] = part[:, other]
-    for copy in copies[4:]:
-        copy.wait()
+    head_sums(n_rows, n_heads, iq_ref, ik_ref[half_at(1 - core, half), :], w_ref, send_ref)
+    copies[4].wait()
+    copies[5].wait()
+
+
+def kept_logits_kernel(n_rows, n_heads, bias_ref, iq_ref, ik_ref, w_ref, keep_ref):
+    half = keep_ref.shape[1]
+    core = lax.axis_index("heads") & 1
+    head_sums(n_rows, n_heads, iq_ref, ik_ref[half_at(core, half), :], w_ref, keep_ref)
+    keep_ref[...] += bias_ref[:, half_at(core, half)]
 
 
 def scores_kernel(n_rows, n_heads, bias_ref, q_ref, lat_ref, p_ref, stat_ref, s_even, s_odd):
@@ -138,69 +156,99 @@
     return top, total
 
 
-def target_kernel(n_rows, n_heads, all_ref, own_ref, p_ref, keep_ref, send_ref, part):
-    half = keep_ref.shape[1]
+def target_sums(n_rows, n_heads, p_ref, weight, at, out_ref):
+    for row in range(n_rows):
+        out_ref[row : row + 1, :] = jnp.sum(
+            p_ref[row * n_heads : (row + 1) * n_heads, at] * weight[:, row : row + 1],
+            axis=0,
+            keepdims=True,
+        )
+
+
+def target_kernel(n_rows, n_heads, all_ref, own_ref, p_ref, send_ref, weight_ref):
+    half = send_ref.shape[1]
     n = all_ref.shape[0]
     top, total = joined([all_ref[k, :n_heads, :] for k in range(n)], SCORE_LOG2)
     weight = jnp.exp2((own_ref[:n_heads, :n_rows] - top) * SCORE_LOG2) / total
-    for row in range(n_rows):
-        part[row : row + 1, :] = jnp.sum(
-            p_ref[row * n_heads : (row + 1) * n_heads, :] * weight[:, row : row + 1],
-            axis=0,
-            keepdims=True,
-        )
     peak, mass = joined([all_ref[k, n_heads:, :] for k in range(n)], 1.0)
+    weight_ref[:n_heads, :n_rows] = weight
+    for ref, first in ((weight_ref, n_heads), (send_ref, n_rows)):
+        ref[first:, :n_rows] = peak
+        ref[first:, n_rows : 2 * n_rows] = mass
     core = lax.axis_index("heads") & 1
-    keep_ref[:n_rows, :] = part[:, half_at(core, half)]
-    send_ref[:n_rows, :] = part[:, half_at(1 - core, half)]
-    for ref in (keep_ref, send_ref):
-        ref[n_rows:, :n_rows] = peak
-        ref[n_rows:, n_rows : 2 * n_rows] = mass
+    target_sums(n_rows, n_heads, p_ref, weight, half_at(1 - core, half), send_ref)
+
+
+def kept_target_kernel(n_rows, n_heads, weight_ref, p_ref, keep_ref):
+    core = lax.axis_index("heads") & 1
+    at = half_at(core, keep_ref.shape[1])
+    target_sums(n_rows, n_heads, p_ref, weight_ref[:n_heads, :n_rows], at, keep_ref)
 
 
 def probs_kernel(mine_ref, other_ref, own_ref, e_ref, prob_ref, col):
     n_rows = e_ref.shape[0]
-    peak, mass = joined([ref[n_rows:, : 2 * n_rows] for ref in (mine_ref, other_ref)], 1.0)
+    first = mine_ref.shape[0] - 8
+    peak, mass = joined([mine_ref[first:, :], other_ref[n_rows:, : 2 * n_rows]], 1.0)
     factor = jnp.exp2(own_ref[own_ref.shape[0] - 8 :, :n_rows] - peak) / mass
     col[:8, :n_rows] = factor
     prob_ref[...] = e_ref[...] * jnp.transpose(col[...])[:n_rows, 0:1]
 
 
-def grads_kernel(n_rows, n_heads, mine_ref, other_ref, iq_ref, ik_ref, iw_ref, *rest):
-    *out_refs, g_full, gk_t, w_cols = rest
-    gq_refs, gk_refs = out_refs[:QUAD], out_refs[QUAD:]
+def mask_kernel(iq_ref, ik_ref, w_ref, wm_ref, iqt_ref):
+    rows = 256
+    for b in range(iq_ref.shape[0] // rows):
+        at = slice(b * rows, (b + 1) * rows)
+        dots = lax.dot_general(iq_ref[at, :], ik_ref[...], CONTRACT_LAST, preferred_element_type=F32)
+        wm_ref[at, :] = jnp.where(dots > 0.0, w_ref[at, 0:1], 0.0)
+        iqt_ref[:, at] = jnp.transpose(iq_ref[at, :])
+
+
+def coefficients(n_heads, g_rows, wm):
+    n = g_rows.shape[1]
+    g = jnp.concatenate(
+        [jnp.broadcast_to(g_rows[i : i + 1, :], (n_heads, n)) for i in range(g_rows.shape[0])], axis=0
+    )
+    return (g * wm).astype(BF16)
+
+
+def own_grads_kernel(n_heads, g_ref, wm_ref, iqt_ref, ik_ref, gq_ref, gkt_ref):
+    half = g_ref.shape[1]
+    at = half_at(lax.axis_index("heads") & 1, half)
+    rows = 256
+    per = rows // n_heads
+    for b in range(wm_ref.shape[0] // rows):
+        row = slice(b * rows, (b + 1) * rows)
+        coef = coefficients(n_heads, g_ref[b * per : (b + 1) * per, :], wm_ref[row, at])
+        gq_ref[row, :] = jnp.dot(coef, ik_ref[at, :], preferred_element_type=F32)
+        term = jnp.dot(iqt_ref[:, row], coef, preferred_element_type=F32)
+        if b == 0:
+            gkt_ref[...] = term
+        else:
+            gkt_ref[...] += term
+
+
+def other_grads_kernel(n_heads, k, g_ref, wm_ref, iqt_ref, ik_ref, gq_ref, *rest):
+    *acc_ref, out_ref, gkt_ref = rest
+    half = g_ref.shape[1]
+    at = half_at(1 - (lax.axis_index("heads") & 1), half)
+    rows = out_ref.shape[0]
+    per = rows // n_heads
+    block = (lax.axis_index("ctx") & (QUAD - 1)) ^ k
+    row = pl.ds(pl.multiple_of(block * rows, rows), rows)
+    coef = coefficients(
+        n_heads, g_ref[pl.ds(pl.multiple_of(block * per, per), per), :], wm_ref[row, at]
+    )
+    out_ref[...] = gq_ref[row, :] + jnp.dot(coef, ik_ref[at, :], preferred_element_type=F32)
+    term = jnp.dot(iqt_ref[:, row], coef, preferred_element_type=F32)
+    gkt_ref[...] = acc_ref[0][...] + term if acc_ref else term
+
+
+def key_grads_kernel(mine_ref, other_ref, *rest):
+    *gk_refs, gk_t = rest
     half = mine_ref.shape[1]
     me = lax.axis_index("heads")
-    core = me & 1
-    g_full[:, half_at(core, half)] = mine_ref[...]
-    g_full[:, half_at(1 - core, half)] = other_ref[...]
-    for row in range(n_rows):
-        w_cols[row * n_heads : (row + 1) * n_heads, :] = jnp.broadcast_to(
-            iw_ref[:, row : row + 1], (n_heads, LANES)
-        )
-    slot = lax.axis_index("ctx") & (QUAD - 1)
-    rows = LANES
-    per = rows // n_heads
-    size = n_rows // QUAD
-    for k in range(QUAD):
-        for b in range(size // per):
-            first = pl.multiple_of((slot ^ k) * size, size) + b * per
-            at = pl.ds(pl.multiple_of(first * n_heads, rows), rows)
-            iq = iq_ref[at, :]
-            dots = lax.dot_general(iq, ik_ref[...], CONTRACT_LAST, preferred_element_type=F32)
-            g_rows = g_full[pl.ds(pl.multiple_of(first, per), per), :]
-            g = jnp.concatenate(
-                [jnp.broadcast_to(g_rows[i : i + 1, :], (n_heads, 2 * half)) for i in range(per)], axis=0
-            )
-            coef = jnp.where(dots > 0.0, g * w_cols[at, 0:1], 0.0).astype(BF16)
-            gq_refs[k][b * rows : (b + 1) * rows, :] = jnp.dot(
-                coef, ik_ref[...], preferred_element_type=F32
-            )
-            term = jnp.dot(jnp.transpose(iq), coef, preferred_element_type=F32)
-            if k == 0 and b == 0:
-                gk_t[...] = term
-            else:
-                gk_t[...] += term
+    gk_t[:, half_at(me & 1, half)] = mine_ref[...]
+    gk_t[:, half_at(1 - (me & 1), half)] = other_ref[...]
     size = gk_refs[0].shape[0]
     for k, ref in enumerate(gk_refs):
         at = pl.multiple_of((me ^ k) * size, LANES)
@@ -242,27 +290,26 @@
         return lax.ppermute(value, axis, [(i, i ^ k) for i in range(n)])
 
     flat = (n_rows * index_local, depth)
-    keep, send, bias, iq, ik, iw, q, lat = call(
+    send, bias, iq, ik, w, q, lat = call(
         functools.partial(
             logits_kernel, n_rows, index_local, (index_local * n_heads * depth) ** (-0.5)
         ),
         (
             shape((n_rows, half), F32),
-            shape((n_rows, half), F32),
             shape((n_rows, keys), F32),
             shape(flat, BF16),
             shape((keys, depth), BF16),
-            shape((index_local, n_rows), F32),
+            shape((flat[0], LANES), F32),
             shape((n_rows * heads_local, width), BF16),
             shape((width, keys), BF16),
         ),
         [HBM] * 6,
         scratch=[
-            pltpu.VMEM((n_rows, keys), F32),
+            pltpu.VMEM((index_local, n_rows), F32),
             pltpu.SMEM((n_rows,), jnp.int32),
             pltpu.SemaphoreType.DMA((6,)),
         ],
-        flops=2 * flat[0] * depth * keys,
+        flops=flat[0] * depth * keys,
         nbytes=queries.size * 2 + latents.size * 2,
     )(
         *(
@@ -277,7 +324,14 @@
             )
         ),
     )
-    logit_mine = keep + swapped(send, "heads", 1)
+    got = swapped(send, "heads", 1)
+    keep = call(
+        functools.partial(kept_logits_kernel, n_rows, index_local),
+        shape((n_rows, half), F32),
+        [VMEM] * 4,
+        flops=flat[0] * depth * keys,
+    )(bias, iq, ik, w)
+    logit_mine = keep + got
     logit_other = swapped(logit_mine, "heads", 2)
     probs, stats = call(
         functools.partial(scores_kernel, n_rows, heads_local),
@@ -295,43 +349,70 @@
         scratch=[pltpu.VMEM((LANES, LANES), F32)],
     )(logit_mine, logit_other, stats)
     everyone = lax.all_to_all(jnp.broadcast_to(stats, (n_ctx,) + stats.shape), "ctx", 0, 0)
-    keep, send = call(
+    send, weight = call(
         functools.partial(target_kernel, n_rows, heads_local),
-        (shape((n_rows + 8, half), F32),) * 2,
+        (shape((n_rows + 8, half), F32), shape((heads_local + 8, 2 * n_rows), F32)),
         [VMEM] * 3,
-        scratch=[pltpu.VMEM((n_rows, keys), F32)],
+        flops=n_rows * heads_local * keys,
     )(everyone, stats, probs)
     got = swapped(send, "heads", 1)
+    keep = call(
+        functools.partial(kept_target_kernel, n_rows, heads_local),
+        shape((n_rows, half), F32),
+        [VMEM] * 2,
+        flops=n_rows * heads_local * keys,
+    )(weight, probs)
     index_probs = call(
         probs_kernel,
         shape((n_rows, half), F32),
         [VMEM] * 4,
         scratch=[pltpu.VMEM((LANES, LANES), F32)],
-    )(keep, got, stats, exps)
-    target = keep[:n_rows] + got[:n_rows]
-    target = target + swapped(target, "heads", 2)
+    )(weight, got, stats, exps)
+    target = keep + got[:n_rows]
+    masked, iq_t = call(
+        mask_kernel,
+        (shape((flat[0], keys), F32), shape(flat[::-1], BF16)),
+        [VMEM] * 3,
+        flops=2 * flat[0] * depth * keys,
+    )(iq, ik, w)
+    rest, masked, iq_t = lax.optimization_barrier((swapped(target, "heads", 2), masked, iq_t))
+    target = target + rest
     grad = loss_scale * (index_probs - target * (1.0 / (heads_local * n_heads)))
     grad_other = swapped(grad, "heads", 1)
+    query_sums, key_sums = call(
+        functools.partial(own_grads_kernel, index_local),
+        (shape(flat, F32), shape((depth, half), F32)),
+        [VMEM] * 4,
+        flops=2 * flat[0] * depth * keys,
+    )(grad, masked, iq_t, ik)
+    query_parts = [None] * QUAD
+    sums = ()
+    for k in range(QUAD - 1, -1, -1):
+        query_parts[k], more = call(
+            functools.partial(other_grads_kernel, index_local, k),
+            (shape((flat[0] // QUAD, depth), F32), shape((depth, half), F32)),
+            [VMEM] * (5 + len(sums)),
+            flops=2 * flat[0] * depth * keys // QUAD,
+        )(grad_other, masked, iq_t, ik, query_sums, *sums)
+        sums = (more,)
+        if k:
+            query_parts[k] = swapped(query_parts[k], "ctx", k)
     owned = keys // n_heads
-    block = (flat[0] // QUAD, depth)
-    parts = call(
-        functools.partial(grads_kernel, n_rows, index_local),
-        (shape(block, F32),) * QUAD + (shape((owned, depth), F32),) * n_heads,
-        [VMEM] * 5,
-        scratch=[
-            pltpu.VMEM((n_rows, keys), F32),
-            pltpu.VMEM((depth, keys), F32),
-            pltpu.VMEM((flat[0], LANES), F32),
-        ],
-    )(grad, grad_other, iq, ik, iw)
-    query_parts, key_parts = parts[:QUAD], parts[QUAD:]
-    mine = query_parts[0] + sum(swapped(query_parts[k], "ctx", k) for k in range(1, QUAD))
+    key_parts = call(
+        key_grads_kernel,
+        (shape((owned, depth), F32),) * n_heads,
+        [VMEM] * 2,
+        scratch=[pltpu.VMEM((depth, keys), F32)],
+    )(key_sums, *sums)
+    mine = sum(query_parts)
     key_parts = [key_parts[0]] + [swapped(key_parts[k], "heads", k) for k in range(1, n_heads)]
     k = QUAD
     while k < n_ctx:
         mine = mine + swapped(mine, "ctx", k)
         k *= 2
-    blocks = [mine] + [swapped(mine, "ctx", k) for k in range(1, QUAD)]
+    blocks = [mine]
+    for k in range(1, QUAD):
+        blocks.append(swapped(mine, "ctx", k))
     grad_queries, grad_keys = call(
         functools.partial(outputs_kernel, QUAD),
         (shape(flat, F32), shape((owned, depth), F32)),

time: 65.3 us -> 63.9 us (0.979)
  waiting for transfers between devices: 24.5 us -> 22.5 us
    ppermute x15, waiting for transfers between devices: 24.5 us -> 22.5 us  [swapped(): return lax.ppermute(value, axis, [(i, i ^ k) for i in range(n)])]
    pallas_call x1 -> x9, Pallas kernels: 2.7 us -> 3.74 us  [the longest x4 1.02 us: body(): call(functools.partial(other_grads_kernel, index_local, k), (shape((flat[...]
  transfers between devices with their start and end apart: 15 -> 15, of which waited for: 11 -> 11; matrix products, arithmetic and copies ran while one was open for 0% -> 0% of each run, Pallas kernels for 7% -> 12%
where the time goes in v4:
time: 63.9 us; the launch traced here: 63.7 us
  waiting for transfers between devices  22.5 us (35%)
  starting transfers between devices  14.7 us (23%)
  blocking collectives  13.2 us (21%)
  Pallas kernels  12.4 us (19%)
  between operations  0.78 us (1%)
    ppermute x15, waiting for transfers between devices, swapped(): return lax.ppermute(value, axis, [(i, i ^ k) for i in range(n)])  22.5 us
    ppermute x15, starting transfers between devices, swapped(): return lax.ppermute(value, axis, [(i, i ^ k) for i in range(n)])  14.7 us
    all_to_all x1, blocking collectives, body(): lax.all_to_all(jnp.broadcast_to(stats, (n_ctx,) + stats.shape), 'ctx', 0, 0)  13.2 us
    pallas_call x1, Pallas kernels, body(): call(functools.partial(scores_kernel, n_rows, heads_local), (shape((n_row...  4.19 us
    pallas_call x1, Pallas kernels, body(): call(functools.partial(logits_kernel, n_rows, index_local, (index_local *...  2.34 us
  transfers between devices with their start and end apart: 15, of which 11 were waited for; matrix products, arithmetic and copies ran while one was open for 0% of the time, Pallas kernels for 12%

profile of v4, /device:TPU:0, one launch (start us, length us, event | category | flops | bytes accessed | tf_op | source)
XLA Modules:
  0.0 63.7 jit_solution(1514676653808803045)
XLA Ops:
  0.6 2.3 %shard_map.77 = (f32[64,512]{1,0:T(8,128)S(1)}, f32[64,1024]{1,0:T(8,128)S(1)}, bf16[1024,128]{1,0:T(8,128)(2,1)S(1)}, bf16[1024,128]{1,0:T(8,128)(2,1)S(1)}, f3...) custom-call(s32[64]{0:T(128)} %pos_hbm.1, bf16[1024,128]{1,0:T(8,128)(2,1)} %bitcast.7, ...), custom_call_target="tpu_custom_call" | custom-call | flops 134217728 | bytes 3538944 | tf_op jit(solution)/shard_map/pallas_call | solution.py:293
  4.5 2.9 %collective-permute-start.1 = (f32[64,512]{1,0:T(8,128)S(1)}, f32[64,512]{1,0:T(8,128)S(1)}, u32[]{:S(2)}, u32[]{:S(2)}) collective-permute-start(f32[64,512]{1,0:T(8,128)S(1)} %add.21.mine_ref), channel_id=1, source_target_pairs={{0,2},{1,3},{2,0},{3,1},{4,6},{5,7},{6,4},{7,5},{8,10},{9,11},{10,... | collective-permute-start | bytes 393224 | tf_op jit(solution)/shard_map/ppermute | solution.py:290
  7.5 4.2 %shard_map.79 = (f32[2048,1024]{1,0:T(8,128)S(1)}, f32[32,128]{1,0:T(8,128)S(1)}) custom-call(f32[64,1024]{1,0:T(8,128)S(1)} %get-tuple-element.36.bias_ref, bf16[2048,576]{1,0:T(8,128)(2,1)S(1)} %get-tuple-element.41.q_ref, bf16[576,1024]{1,0:T(8,128)(2,1)S(1)} %get-tuple-element.42.lat_ref), custom_call_target="tpu_custom_call" | custom-call | flops 2415919104 | bytes 2359296 | tf_op jit(solution)/shard_map/pallas_call | solution.py:336
  11.9 13.2 %all_to_all.5.all_ref = f32[8,40,128]{2,1,0:T(8,128)S(1)} all-to-all(f32[8,40,128]{2,1,0:T(8,128)S(1)} %broadcast_in_dim.3), channel_id=1, replica_groups=mesh['ctx'=8,'heads'=4] {'ctx'}, dimensions={0} | all-to-all | bytes 327680 | tf_op jit(solution)/shard_map/all_to_all | solution.py:351
  25.1 0.8 %shard_map.81 = (f32[72,512]{1,0:T(8,128)S(1)}, f32[40,128]{1,0:T(8,128)S(1)}) custom-call(f32[8,40,128]{2,1,0:T(8,128)S(1)} %all_to_all.5.all_ref, f32[40,128]{1,0:T(8,128)S(1)} %get-tuple-element.44.own_ref, f32[2048,1024]{1,0:T(8,128)S(1)} %get-tuple-element.45.p_ref), custom_call_target="tpu_custom_call" | custom-call | flops 2097152 | tf_op jit(solution)/shard_map/pallas_call | solution.py:352
  26.5 0.8 %collective-permute-done.2.other_ref = f32[72,512]{1,0:T(8,128)S(1)} collective-permute-done((f32[72,512]{1,0:T(8,128)S(1)}, f32[72,512]{1,0:T(8,128)S(1)}, u32[]{:S(2)}, u32[]{:S(2)}) %collective-permute-start.2) | collective-permute-done | bytes 147488 | tf_op jit(solution)/shard_map/ppermute | solution.py:290
  27.3 1.4 %collective-permute-start.3 = (f32[64,512]{1,0:T(8,128)S(1)}, f32[64,512]{1,0:T(8,128)S(1)}, u32[]{:S(2)}, u32[]{:S(2)}) collective-permute-start(f32[64,512]{1,0:T(8,128)S(1)} %slice_add_fusion), channel_id=1, source_target_pairs={{0,2},{1,3},{2,0},{3,1},{4,6},{5,7},{6,4},{7,5},{8,10},{9,11},{10,... | collective-permute-start | bytes 393224 | tf_op jit(solution)/shard_map/ppermute | solution.py:290
  28.7 0.7 %shard_map.84 = (f32[1024,1024]{1,0:T(8,128)S(1)}, bf16[128,1024]{1,0:T(8,128)(2,1)S(1)}) custom-call(bf16[1024,128]{1,0:T(8,128)(2,1)S(1)} %get-tuple-element.37.iq_ref, bf16[1024,128]{1,0:T(8,128)(2,1)S(1)} %get-tuple-element.38.ik_ref, f32[1024,128]{1,0:T(8,128)S(1)} %get-tuple-element.39.w_ref), custom_call_target="tpu_custom_call" | custom-call | flops 268435456 | tf_op jit(solution)/shard_map/pallas_call | solution.py:372
  29.8 3.2 %collective-permute-done.3 = f32[64,512]{1,0:T(8,128)S(1)} collective-permute-done((f32[64,512]{1,0:T(8,128)S(1)}, f32[64,512]{1,0:T(8,128)S(1)}, u32[]{:S(2)}, u32[]{:S(2)}) %collective-permute-start.3) | collective-permute-done | bytes 131104 | tf_op jit(solution)/shard_map/ppermute | solution.py:290
  33.6 0.8 %collective-permute-done.4.g_ref = f32[64,512]{1,0:T(8,128)S(1)} collective-permute-done((f32[64,512]{1,0:T(8,128)S(1)}, f32[64,512]{1,0:T(8,128)S(1)}, u32[]{:S(2)}, u32[]{:S(2)}) %collective-permute-start.4) | collective-permute-done | bytes 131104 | tf_op jit(solution)/shard_map/ppermute | solution.py:290
  35.2 1.0 %collective-permute-start.5 = (f32[256,128]{1,0:T(8,128)S(1)}, f32[256,128]{1,0:T(8,128)S(1)}, u32[]{:S(2)}, u32[]{:S(2)}) collective-permute-start(f32[256,128]{1,0:T(8,128)S(1)} %get-tuple-element.59), channel_id=1, source_target_pairs={{0,4},{4,0},{8,12},{12,8},{16,20},{20,16},{24,28},{28,24},{1,5},{5... | collective-permute-start | bytes 393224 | tf_op jit(solution)/shard_map/ppermute | solution.py:290
  36.6 2.1 %collective-permute-start.7 = (f32[256,128]{1,0:T(8,128)S(1)}, f32[256,128]{1,0:T(8,128)S(1)}, u32[]{:S(2)}, u32[]{:S(2)}) collective-permute-start(f32[256,128]{1,0:T(8,128)S(1)} %get-tuple-element.61), channel_id=1, source_target_pairs={{0,12},{4,8},{8,4},{12,0},{16,28},{20,24},{24,20},{28,16},{1,13},{... | collective-permute-start | bytes 393224 | tf_op jit(solution)/shard_map/ppermute | solution.py:290
  39.0 1.8 %collective-permute-done.5 = f32[256,128]{1,0:T(8,128)S(1)} collective-permute-done((f32[256,128]{1,0:T(8,128)S(1)}, f32[256,128]{1,0:T(8,128)S(1)}, u32[]{:S(2)}, u32[]{:S(2)}) %collective-permute-start.5) | collective-permute-done | bytes 131104 | tf_op jit(solution)/shard_map/ppermute | solution.py:290
  40.8 1.8 %collective-permute-done.6 = f32[256,128]{1,0:T(8,128)S(1)} collective-permute-done((f32[256,128]{1,0:T(8,128)S(1)}, f32[256,128]{1,0:T(8,128)S(1)}, u32[]{:S(2)}, u32[]{:S(2)}) %collective-permute-start.6) | collective-permute-done | bytes 131104 | tf_op jit(solution)/shard_map/ppermute | solution.py:290
  42.6 2.2 %collective-permute-done.7 = f32[256,128]{1,0:T(8,128)S(1)} collective-permute-done((f32[256,128]{1,0:T(8,128)S(1)}, f32[256,128]{1,0:T(8,128)S(1)}, u32[]{:S(2)}, u32[]{:S(2)}) %collective-permute-start.7) | collective-permute-done | bytes 131104 | tf_op jit(solution)/shard_map/ppermute | solution.py:290
  45.8 1.2 %collective-permute-start.13 = (f32[256,128]{1,0:T(8,128)S(1)}, f32[256,128]{1,0:T(8,128)S(1)}, u32[]{:S(2)}, u32[]{:S(2)}) collective-permute-start(f32[256,128]{1,0:T(8,128)S(1)} %get-tuple-element.66), channel_id=1, source_target_pairs={{0,2},{1,3},{2,0},{3,1},{4,6},{5,7},{6,4},{7,5},{8,10},{9,11},{10,... | collective-permute-start | bytes 393224 | tf_op jit(solution)/shard_map/ppermute | solution.py:290
  47.0 0.7 %collective-permute-start.14 = (f32[256,128]{1,0:T(8,128)S(1)}, f32[256,128]{1,0:T(8,128)S(1)}, u32[]{:S(2)}, u32[]{:S(2)}) collective-permute-start(f32[256,128]{1,0:T(8,128)S(1)} %get-tuple-element.67), channel_id=1, source_target_pairs={{0,3},{1,2},{2,1},{3,0},{4,7},{5,6},{6,5},{7,4},{8,11},{9,10},{10,... | collective-permute-start | bytes 393224 | tf_op jit(solution)/shard_map/ppermute | solution.py:290
  47.6 5.2 %collective-permute-done.8 = f32[256,128]{1,0:T(8,128)S(1)} collective-permute-done((f32[256,128]{1,0:T(8,128)S(1)}, f32[256,128]{1,0:T(8,128)S(1)}, u32[]{:S(2)}, u32[]{:S(2)}) %collective-permute-start.8) | collective-permute-done | bytes 131104 | tf_op jit(solution)/shard_map/ppermute | solution.py:290
  53.0 2.5 %collective-permute-start.11 = (f32[256,128]{1,0:T(8,128)S(1)}, f32[256,128]{1,0:T(8,128)S(1)}, u32[]{:S(2)}, u32[]{:S(2)}) collective-permute-start(f32[256,128]{1,0:T(8,128)S(1)} %add.27.refs_0_), channel_id=1, source_target_pairs={{0,12},{4,8},{8,4},{12,0},{16,28},{20,24},{24,20},{28,16},{1,13},{... | collective-permute-start | bytes 393224 | tf_op jit(solution)/shard_map/ppermute | solution.py:290
  55.5 0.9 %collective-permute-start.9 = (f32[256,128]{1,0:T(8,128)S(1)}, f32[256,128]{1,0:T(8,128)S(1)}, u32[]{:S(2)}, u32[]{:S(2)}) collective-permute-start(f32[256,128]{1,0:T(8,128)S(1)} %add.27.refs_0_), channel_id=1, source_target_pairs={{0,4},{4,0},{8,12},{12,8},{16,20},{20,16},{24,28},{28,24},{1,5},{5... | collective-permute-start | bytes 393224 | tf_op jit(solution)/shard_map/ppermute | solution.py:290
  56.5 2.9 %collective-permute-done.10.refs_2_ = f32[256,128]{1,0:T(8,128)S(1)} collective-permute-done((f32[256,128]{1,0:T(8,128)S(1)}, f32[256,128]{1,0:T(8,128)S(1)}, u32[]{:S(2)}, u32[]{:S(2)}) %collective-permute-start.10) | collective-permute-done | bytes 131104 | tf_op jit(solution)/shard_map/ppermute | solution.py:290
  59.3 2.2 %collective-permute-done.11.refs_3_ = f32[256,128]{1,0:T(8,128)S(1)} collective-permute-done((f32[256,128]{1,0:T(8,128)S(1)}, f32[256,128]{1,0:T(8,128)S(1)}, u32[]{:S(2)}, u32[]{:S(2)}) %collective-permute-start.11) | collective-permute-done | bytes 131104 | tf_op jit(solution)/shard_map/ppermute | solution.py:290
  61.5 1.4 %collective-permute-done.9.refs_1_ = f32[256,128]{1,0:T(8,128)S(1)} collective-permute-done((f32[256,128]{1,0:T(8,128)S(1)}, f32[256,128]{1,0:T(8,128)S(1)}, u32[]{:S(2)}, u32[]{:S(2)}) %collective-permute-start.9) | collective-permute-done | bytes 131104 | tf_op jit(solution)/shard_map/ppermute | solution.py:290
  62.9 0.9 %shard_map.91 = (f32[1024,128]{1,0:T(8,128)}, f32[256,128]{1,0:T(8,128)}) custom-call(f32[256,128]{1,0:T(8,128)S(1)} %add.27.refs_0_, f32[256,128]{1,0:T(8,128)S(1)} %collective-permute-done.9.refs_1_, f32[256,128]{1,0:T(8,128)S(1)} %collective-permute-done.10.refs_2_, f32[256,128]{1,0:T(8,128)S(1)} %collective-permute-done.11.refs_3_, ...), custom_call_target="tpu_custom_call" | custom-call | tf_op jit(solution)/shard_map/pallas_call | solution.py:416
  (28 shorter events, 5.9 us)
Async XLA Ops:
  3.0 1.5 %collective-permute-start = (f32[64,512]{1,0:T(8,128)S(1)}, f32[64,512]{1,0:T(8,128)S(1)}, u32[]{:S(2)}, u32[]{:S(2)}) collective-permute-start(f32[64,512]{1,0:T(8,128)S(1)} %get-tuple-element.40), channel_id=1, source_target_pairs={{0,1},{1,0},{2,3},{3,2},{4,5},{5,4},{6,7},{7,6},{8,9},{9,8},{10,11... | collective-permute-start | bytes 393224 | tf_op jit(solution)/shard_map/ppermute | solution.py:290
  4.5 7.1 %collective-permute-start.1 = (f32[64,512]{1,0:T(8,128)S(1)}, f32[64,512]{1,0:T(8,128)S(1)}, u32[]{:S(2)}, u32[]{:S(2)}) collective-permute-start(f32[64,512]{1,0:T(8,128)S(1)} %add.21.mine_ref), channel_id=1, source_target_pairs={{0,2},{1,3},{2,0},{3,1},{4,6},{5,7},{6,4},{7,5},{8,10},{9,11},{10,... | collective-permute-start | bytes 393224 | tf_op jit(solution)/shard_map/ppermute | solution.py:290
  25.9 1.4 %collective-permute-start.2 = (f32[72,512]{1,0:T(8,128)S(1)}, f32[72,512]{1,0:T(8,128)S(1)}, u32[]{:S(2)}, u32[]{:S(2)}) collective-permute-start(f32[72,512]{1,0:T(8,128)S(1)} %get-tuple-element.47), channel_id=1, source_target_pairs={{0,1},{1,0},{2,3},{3,2},{4,5},{5,4},{6,7},{7,6},{8,9},{9,8},{10,11... | collective-permute-start | bytes 442376 | tf_op jit(solution)/shard_map/ppermute | solution.py:290
  27.3 5.6 %collective-permute-start.3 = (f32[64,512]{1,0:T(8,128)S(1)}, f32[64,512]{1,0:T(8,128)S(1)}, u32[]{:S(2)}, u32[]{:S(2)}) collective-permute-start(f32[64,512]{1,0:T(8,128)S(1)} %slice_add_fusion), channel_id=1, source_target_pairs={{0,2},{1,3},{2,0},{3,1},{4,6},{5,7},{6,4},{7,5},{8,10},{9,11},{10,... | collective-permute-start | bytes 393224 | tf_op jit(solution)/shard_map/ppermute | solution.py:290
  33.0 1.4 %collective-permute-start.4 = (f32[64,512]{1,0:T(8,128)S(1)}, f32[64,512]{1,0:T(8,128)S(1)}, u32[]{:S(2)}, u32[]{:S(2)}) collective-permute-start(f32[64,512]{1,0:T(8,128)S(1)} %subtract_multiply_fusion.g_ref), channel_id=1, source_target_pairs={{0,1},{1,0},{2,3},{3,2},{4,5},{5,4},{6,7},{7,6},{8,9},{9,8},{10,11... | collective-permute-start | bytes 393224 | tf_op jit(solution)/shard_map/ppermute | solution.py:290
  35.2 5.6 %collective-permute-start.5 = (f32[256,128]{1,0:T(8,128)S(1)}, f32[256,128]{1,0:T(8,128)S(1)}, u32[]{:S(2)}, u32[]{:S(2)}) collective-permute-start(f32[256,128]{1,0:T(8,128)S(1)} %get-tuple-element.59), channel_id=1, source_target_pairs={{0,4},{4,0},{8,12},{12,8},{16,20},{20,16},{24,28},{28,24},{1,5},{5... | collective-permute-start | bytes 393224 | tf_op jit(solution)/shard_map/ppermute | solution.py:290
  36.2 6.4 %collective-permute-start.6 = (f32[256,128]{1,0:T(8,128)S(1)}, f32[256,128]{1,0:T(8,128)S(1)}, u32[]{:S(2)}, u32[]{:S(2)}) collective-permute-start(f32[256,128]{1,0:T(8,128)S(1)} %get-tuple-element.60), channel_id=1, source_target_pairs={{0,8},{4,12},{8,0},{12,4},{16,24},{20,28},{24,16},{28,20},{1,9},{5... | collective-permute-start | bytes 393224 | tf_op jit(solution)/shard_map/ppermute | solution.py:290
  36.6 8.2 %collective-permute-start.7 = (f32[256,128]{1,0:T(8,128)S(1)}, f32[256,128]{1,0:T(8,128)S(1)}, u32[]{:S(2)}, u32[]{:S(2)}) collective-permute-start(f32[256,128]{1,0:T(8,128)S(1)} %get-tuple-element.61), channel_id=1, source_target_pairs={{0,12},{4,8},{8,4},{12,0},{16,28},{20,24},{24,20},{28,16},{1,13},{... | collective-permute-start | bytes 393224 | tf_op jit(solution)/shard_map/ppermute | solution.py:290
  44.8 8.0 %collective-permute-start.8 = (f32[256,128]{1,0:T(8,128)S(1)}, f32[256,128]{1,0:T(8,128)S(1)}, u32[]{:S(2)}, u32[]{:S(2)}) collective-permute-start(f32[256,128]{1,0:T(8,128)S(1)} %add_add_fusion), channel_id=1, source_target_pairs={{0,16},{4,20},{8,24},{12,28},{16,0},{20,4},{24,8},{28,12},{1,17},{... | collective-permute-start | bytes 393224 | tf_op jit(solution)/shard_map/ppermute | solution.py:290
  45.7 9.8 %collective-permute-start.12 = (f32[256,128]{1,0:T(8,128)S(1)}, f32[256,128]{1,0:T(8,128)S(1)}, u32[]{:S(2)}, u32[]{:S(2)}) collective-permute-start(f32[256,128]{1,0:T(8,128)S(1)} %get-tuple-element.65), channel_id=1, source_target_pairs={{0,1},{1,0},{2,3},{3,2},{4,5},{5,4},{6,7},{7,6},{8,9},{9,8},{10,11... | collective-permute-start | bytes 393224 | tf_op jit(solution)/shard_map/ppermute | solution.py:290
  45.8 10.7 %collective-permute-start.13 = (f32[256,128]{1,0:T(8,128)S(1)}, f32[256,128]{1,0:T(8,128)S(1)}, u32[]{:S(2)}, u32[]{:S(2)}) collective-permute-start(f32[256,128]{1,0:T(8,128)S(1)} %get-tuple-element.66), channel_id=1, source_target_pairs={{0,2},{1,3},{2,0},{3,1},{4,6},{5,7},{6,4},{7,5},{8,10},{9,11},{10,... | collective-permute-start | bytes 393224 | tf_op jit(solution)/shard_map/ppermute | solution.py:290
  47.0 9.5 %collective-permute-start.14 = (f32[256,128]{1,0:T(8,128)S(1)}, f32[256,128]{1,0:T(8,128)S(1)}, u32[]{:S(2)}, u32[]{:S(2)}) collective-permute-start(f32[256,128]{1,0:T(8,128)S(1)} %get-tuple-element.67), channel_id=1, source_target_pairs={{0,3},{1,2},{2,1},{3,0},{4,7},{5,6},{6,5},{7,4},{8,11},{9,10},{10,... | collective-permute-start | bytes 393224 | tf_op jit(solution)/shard_map/ppermute | solution.py:290
  52.9 6.4 %collective-permute-start.10 = (f32[256,128]{1,0:T(8,128)S(1)}, f32[256,128]{1,0:T(8,128)S(1)}, u32[]{:S(2)}, u32[]{:S(2)}) collective-permute-start(f32[256,128]{1,0:T(8,128)S(1)} %add.27.refs_0_), channel_id=1, source_target_pairs={{0,8},{4,12},{8,0},{12,4},{16,24},{20,28},{24,16},{28,20},{1,9},{5... | collective-permute-start | bytes 393224 | tf_op jit(solution)/shard_map/ppermute | solution.py:290
  53.0 8.5 %collective-permute-start.11 = (f32[256,128]{1,0:T(8,128)S(1)}, f32[256,128]{1,0:T(8,128)S(1)}, u32[]{:S(2)}, u32[]{:S(2)}) collective-permute-start(f32[256,128]{1,0:T(8,128)S(1)} %add.27.refs_0_), channel_id=1, source_target_pairs={{0,12},{4,8},{8,4},{12,0},{16,28},{20,24},{24,20},{28,16},{1,13},{... | collective-permute-start | bytes 393224 | tf_op jit(solution)/shard_map/ppermute | solution.py:290
  55.5 7.4 %collective-permute-start.9 = (f32[256,128]{1,0:T(8,128)S(1)}, f32[256,128]{1,0:T(8,128)S(1)}, u32[]{:S(2)}, u32[]{:S(2)}) collective-permute-start(f32[256,128]{1,0:T(8,128)S(1)} %add.27.refs_0_), channel_id=1, source_target_pairs={{0,4},{4,0},{8,12},{12,8},{16,20},{20,16},{24,28},{28,24},{1,5},{5... | collective-permute-start | bytes 393224 | tf_op jit(solution)/shard_map/ppermute | solution.py:290

commit v5 on v4

--- a/solution.py
+++ b/solution.py
@@ -59,8 +59,8 @@
 
 def logits_kernel(
     n_rows, n_heads, scale,
-    pos_hbm, iq_hbm, ik_hbm, iw_hbm, q_hbm, lat_hbm,
-    send_ref, bias_ref, iq_ref, ik_ref, w_ref, q_ref, lat_ref,
+    pos_hbm, iq_hbm, ik_hbm, iw_hbm, lat_hbm,
+    send_ref, bias_ref, iq_ref, ik_ref, w_ref, lat_ref,
     iw_ref, pos_ref, sems,
 ):
     half = send_ref.shape[1]
@@ -73,7 +73,6 @@
                 (ik_hbm, ik_ref),
                 (iq_hbm, iq_ref),
                 (lat_hbm, lat_ref),
-                (q_hbm, q_ref),
             )
         )
     ]
@@ -97,14 +96,18 @@
     core = lax.axis_index("heads") & 1
     head_sums(n_rows, n_heads, iq_ref, ik_ref[half_at(1 - core, half), :], w_ref, send_ref)
     copies[4].wait()
-    copies[5].wait()
-
-
-def kept_logits_kernel(n_rows, n_heads, bias_ref, iq_ref, ik_ref, w_ref, keep_ref):
+
+
+def kept_logits_kernel(
+    n_rows, n_heads, bias_ref, iq_ref, ik_ref, w_ref, q_hbm, keep_ref, q_ref, sem
+):
+    copy = pltpu.make_async_copy(q_hbm, q_ref, sem)
+    copy.start()
     half = keep_ref.shape[1]
     core = lax.axis_index("heads") & 1
     head_sums(n_rows, n_heads, iq_ref, ik_ref[half_at(core, half), :], w_ref, keep_ref)
     keep_ref[...] += bias_ref[:, half_at(core, half)]
+    copy.wait()
 
 
 def scores_kernel(n_rows, n_heads, bias_ref, q_ref, lat_ref, p_ref, stat_ref, s_even, s_odd):
@@ -143,16 +146,18 @@
     e_ref[...] = e
     col[:n_rows, 0:1] = top
     col[n_rows:, 0:1] = jnp.sum(e, axis=1, keepdims=True)
-    n = stat_ref.shape[0]
-    out_ref[:n, :] = stat_ref[...]
+    n = stat_ref.shape[0] // 2
+    size = stat_ref[:, :n_rows] * SCORE_LOG2 + jnp.log2(stat_ref[:, n_rows:])
+    out_ref[:n, :n_rows] = size[:n, :]
+    out_ref[:n, n_rows:] = size[n:, :]
     out_ref[n:, :] = jnp.transpose(col[...])[: out_ref.shape[0] - n, :]
 
 
-def joined(stats, unit):
+def joined(stats):
     n = stats[0].shape[1] // 2
     tops = [s[:, :n] for s in stats]
     top = functools.reduce(jnp.maximum, tops)
-    total = sum(s[:, n:] * jnp.exp2((t - top) * unit) for s, t in zip(stats, tops))
+    total = sum(s[:, n:] * jnp.exp2(t - top) for s, t in zip(stats, tops))
     return top, total
 
 
@@ -168,9 +173,19 @@
 def target_kernel(n_rows, n_heads, all_ref, own_ref, p_ref, send_ref, weight_ref):
     half = send_ref.shape[1]
     n = all_ref.shape[0]
-    top, total = joined([all_ref[k, :n_heads, :] for k in range(n)], SCORE_LOG2)
-    weight = jnp.exp2((own_ref[:n_heads, :n_rows] - top) * SCORE_LOG2) / total
-    peak, mass = joined([all_ref[k, n_heads:, :] for k in range(n)], 1.0)
+    some = n_heads // 2
+    sizes = [all_ref[k, :some, :] for k in range(n)]
+    top = functools.reduce(jnp.maximum, sizes)
+    total = sum(jnp.exp2(s - top) for s in sizes)
+    tops = own_ref[:, :n_rows] * SCORE_LOG2
+    weight = jnp.concatenate(
+        [
+            jnp.exp2(tops[:some, :] - top[:, :n_rows]) / total[:, :n_rows],
+            jnp.exp2(tops[some:, :] - top[:, n_rows:]) / total[:, n_rows:],
+        ],
+        axis=0,
+    )
+    peak, mass = joined([all_ref[k, some:, :] for k in range(n)])
     weight_ref[:n_heads, :n_rows] = weight
     for ref, first in ((weight_ref, n_heads), (send_ref, n_rows)):
         ref[first:, :n_rows] = peak
@@ -188,7 +203,7 @@
 def probs_kernel(mine_ref, other_ref, own_ref, e_ref, prob_ref, col):
     n_rows = e_ref.shape[0]
     first = mine_ref.shape[0] - 8
-    peak, mass = joined([mine_ref[first:, :], other_ref[n_rows:, : 2 * n_rows]], 1.0)
+    peak, mass = joined([mine_ref[first:, :], other_ref[n_rows:, : 2 * n_rows]])
     factor = jnp.exp2(own_ref[own_ref.shape[0] - 8 :, :n_rows] - peak) / mass
     col[:8, :n_rows] = factor
     prob_ref[...] = e_ref[...] * jnp.transpose(col[...])[:n_rows, 0:1]
@@ -290,7 +305,7 @@
         return lax.ppermute(value, axis, [(i, i ^ k) for i in range(n)])
 
     flat = (n_rows * index_local, depth)
-    send, bias, iq, ik, w, q, lat = call(
+    send, bias, iq, ik, w, lat = call(
         functools.partial(
             logits_kernel, n_rows, index_local, (index_local * n_heads * depth) ** (-0.5)
         ),
@@ -300,17 +315,16 @@
             shape(flat, BF16),
             shape((keys, depth), BF16),
             shape((flat[0], LANES), F32),
-            shape((n_rows * heads_local, width), BF16),
             shape((width, keys), BF16),
         ),
-        [HBM] * 6,
+        [HBM] * 5,
         scratch=[
             pltpu.VMEM((index_local, n_rows), F32),
             pltpu.SMEM((n_rows,), jnp.int32),
-            pltpu.SemaphoreType.DMA((6,)),
+            pltpu.SemaphoreType.DMA((5,)),
         ],
         flops=flat[0] * depth * keys,
-        nbytes=queries.size * 2 + latents.size * 2,
+        nbytes=latents.size * 2,
     )(
         *(
             pltpu.with_memory_space_constraint(x, pltpu.HBM)
@@ -319,18 +333,22 @@
                 index_queries.reshape(flat),
                 index_keys,
                 index_weights.T,
-                queries.reshape(n_rows * heads_local, width),
                 latents.T,
             )
-        ),
+        )
     )
     got = swapped(send, "heads", 1)
-    keep = call(
+    flat_queries = pltpu.with_memory_space_constraint(
+        queries.reshape(n_rows * heads_local, width), pltpu.HBM
+    )
+    keep, q = call(
         functools.partial(kept_logits_kernel, n_rows, index_local),
-        shape((n_rows, half), F32),
-        [VMEM] * 4,
+        (shape((n_rows, half), F32), shape(flat_queries.shape, BF16)),
+        [VMEM] * 4 + [HBM],
+        scratch=[pltpu.SemaphoreType.DMA],
         flops=flat[0] * depth * keys,
-    )(bias, iq, ik, w)
+        nbytes=queries.size * 2,
+    )(bias, iq, ik, w, flat_queries)
     logit_mine = keep + got
     logit_other = swapped(logit_mine, "heads", 2)
     probs, stats = call(
@@ -342,13 +360,13 @@
         exps=n_rows * heads_local * keys,
         nbytes=queries.size * 2,
     )(bias, q, lat)
-    exps, stats = call(
+    exps, sizes = call(
         index_stats_kernel,
-        (shape((n_rows, half), F32), shape((heads_local + 8, 2 * n_rows), F32)),
+        (shape((n_rows, half), F32), shape((heads_local // 2 + 8, 2 * n_rows), F32)),
         [VMEM] * 3,
         scratch=[pltpu.VMEM((LANES, LANES), F32)],
     )(logit_mine, logit_other, stats)
-    everyone = lax.all_to_all(jnp.broadcast_to(stats, (n_ctx,) + stats.shape), "ctx", 0, 0)
+    everyone = lax.all_to_all(jnp.broadcast_to(sizes, (n_ctx,) + sizes.shape), "ctx", 0, 0)
     send, weight = call(
         functools.partial(target_kernel, n_rows, heads_local),
         (shape((n_rows + 8, half), F32), shape((heads_local + 8, 2 * n_rows), F32)),
@@ -367,7 +385,7 @@
         shape((n_rows, half), F32),
         [VMEM] * 4,
         scratch=[pltpu.VMEM((LANES, LANES), F32)],
-    )(weight, got, stats, exps)
+    )(weight, got, sizes, exps)
     target = keep + got[:n_rows]
     masked, iq_t = call(
         mask_kernel,

time: 63.9 us -> 62.1 us (0.972)
  waiting for transfers between devices: 22.5 us -> 20.8 us
    ppermute x15, waiting for transfers between devices: 22.5 us -> 20.8 us  [swapped(): return lax.ppermute(value, axis, [(i, i ^ k) for i in range(n)])]
    pallas_call x1, Pallas kernels: 0.63 us -> 1.76 us  [body(): call(functools.partial(kept_logits_kernel, n_rows, index_local), (shape((...]
    pallas_call x1, Pallas kernels: 2.34 us -> 1.7 us  [body(): call(functools.partial(logits_kernel, n_rows, index_local, (index_local *...]
  transfers between devices with their start and end apart: 15 -> 15, of which waited for: 11 -> 10; matrix products, arithmetic and copies ran while one was open for 0% -> 0% of each run, Pallas kernels for 12% -> 15%
where the time goes in v5:
time: 62.1 us; the launch traced here: 61.9 us
  waiting for transfers between devices  20.8 us (33%)
  starting transfers between devices  14.5 us (23%)
  blocking collectives  12.9 us (21%)
  Pallas kernels  12.8 us (21%)
  between operations  0.79 us (1%)
    ppermute x15, waiting for transfers between devices, swapped(): return lax.ppermute(value, axis, [(i, i ^ k) for i in range(n)])  20.8 us
    ppermute x15, starting transfers between devices, swapped(): return lax.ppermute(value, axis, [(i, i ^ k) for i in range(n)])  14.5 us
    all_to_all x1, blocking collectives, body(): lax.all_to_all(jnp.broadcast_to(sizes, (n_ctx,) + sizes.shape), 'ctx', 0, 0)  12.9 us
    pallas_call x1, Pallas kernels, body(): call(functools.partial(scores_kernel, n_rows, heads_local), (shape((n_row...  4.19 us
    pallas_call x1, Pallas kernels, body(): call(functools.partial(kept_logits_kernel, n_rows, index_local), (shape((...  1.76 us
    pallas_call x1, Pallas kernels, body(): call(functools.partial(logits_kernel, n_rows, index_local, (index_local *...  1.7 us
  transfers between devices with their start and end apart: 15, of which 10 were waited for; matrix products, arithmetic and copies ran while one was open for 0% of the time, Pallas kernels for 15%

profile of v5, /device:TPU:0, one launch (start us, length us, event | category | flops | bytes accessed | tf_op | source)
XLA Modules:
  0.0 61.9 jit_solution(5616593444378622392)
XLA Ops:
  0.6 1.7 %shard_map.77 = (f32[64,512]{1,0:T(8,128)S(1)}, f32[64,1024]{1,0:T(8,128)S(1)}, bf16[1024,128]{1,0:T(8,128)(2,1)S(1)}, bf16[1024,128]{1,0:T(8,128)(2,1)S(1)}, f3...) custom-call(s32[64]{0:T(128)} %pos_hbm.1, bf16[1024,128]{1,0:T(8,128)(2,1)} %bitcast.7, bf16[1024,128]{1,0:T(8,128)(2,1)} %ik_hbm.1, ...), custom_call_target="tpu_custom_call" | custom-call | flops 134217728 | bytes 1179648 | tf_op jit(solution)/shard_map/pallas_call | solution.py:308
  2.9 1.8 %shard_map.78 = (f32[64,512]{1,0:T(8,128)S(1)}, bf16[2048,576]{1,0:T(8,128)(2,1)S(1)}) custom-call(f32[64,1024]{1,0:T(8,128)S(1)} %get-tuple-element.37.bias_ref, bf16[1024,128]{1,0:T(8,128)(2,1)S(1)} %get-tuple-element.38.iq_ref, bf16[1024,128]{1,0:T(8,128)(2,1)S(1)} %get-tuple-element.39.ik_ref, f32[1024,128]{1,0:T(8,128)S(1)} %get-tuple-element.40.w_ref, ...), custom_call_target="tpu_custom_call" | custom-call | flops 134217728 | bytes 2359296 | tf_op jit(solution)/shard_map/pallas_call | solution.py:344
  4.7 2.6 %collective-permute-start.1 = (f32[64,512]{1,0:T(8,128)S(1)}, f32[64,512]{1,0:T(8,128)S(1)}, u32[]{:S(2)}, u32[]{:S(2)}) collective-permute-start(f32[64,512]{1,0:T(8,128)S(1)} %add.21.mine_ref), channel_id=1, source_target_pairs={{0,2},{1,3},{2,0},{3,1},{4,6},{5,7},{6,4},{7,5},{8,10},{9,11},{10,... | collective-permute-start | bytes 393224 | tf_op jit(solution)/shard_map/ppermute | solution.py:305
  7.3 4.2 %shard_map.79 = (f32[2048,1024]{1,0:T(8,128)S(1)}, f32[32,128]{1,0:T(8,128)S(1)}) custom-call(f32[64,1024]{1,0:T(8,128)S(1)} %get-tuple-element.37.bias_ref, bf16[2048,576]{1,0:T(8,128)(2,1)S(1)} %get-tuple-element.43.q_ref, bf16[576,1024]{1,0:T(8,128)(2,1)S(1)} %get-tuple-element.44.lat_ref), custom_call_target="tpu_custom_call" | custom-call | flops 2415919104 | bytes 2359296 | tf_op jit(solution)/shard_map/pallas_call | solution.py:354
  11.7 12.9 %all_to_all.5.all_ref = f32[8,24,128]{2,1,0:T(8,128)S(1)} all-to-all(f32[8,24,128]{2,1,0:T(8,128)S(1)} %broadcast_in_dim.3), channel_id=1, replica_groups=mesh['ctx'=8,'heads'=4] {'ctx'}, dimensions={0} | all-to-all | bytes 196608 | tf_op jit(solution)/shard_map/all_to_all | solution.py:369
  25.9 0.8 %collective-permute-done.2.other_ref = f32[72,512]{1,0:T(8,128)S(1)} collective-permute-done((f32[72,512]{1,0:T(8,128)S(1)}, f32[72,512]{1,0:T(8,128)S(1)}, u32[]{:S(2)}, u32[]{:S(2)}) %collective-permute-start.2) | collective-permute-done | bytes 147488 | tf_op jit(solution)/shard_map/ppermute | solution.py:305
  26.7 1.6 %collective-permute-start.3 = (f32[64,512]{1,0:T(8,128)S(1)}, f32[64,512]{1,0:T(8,128)S(1)}, u32[]{:S(2)}, u32[]{:S(2)}) collective-permute-start(f32[64,512]{1,0:T(8,128)S(1)} %slice_add_fusion), channel_id=1, source_target_pairs={{0,2},{1,3},{2,0},{3,1},{4,6},{5,7},{6,4},{7,5},{8,10},{9,11},{10,... | collective-permute-start | bytes 393224 | tf_op jit(solution)/shard_map/ppermute | solution.py:305
  28.3 0.7 %shard_map.84 = (f32[1024,1024]{1,0:T(8,128)S(1)}, bf16[128,1024]{1,0:T(8,128)(2,1)S(1)}) custom-call(bf16[1024,128]{1,0:T(8,128)(2,1)S(1)} %get-tuple-element.38.iq_ref, bf16[1024,128]{1,0:T(8,128)(2,1)S(1)} %get-tuple-element.39.ik_ref, f32[1024,128]{1,0:T(8,128)S(1)} %get-tuple-element.40.w_ref), custom_call_target="tpu_custom_call" | custom-call | flops 268435456 | tf_op jit(solution)/shard_map/pallas_call | solution.py:390
  29.4 3.0 %collective-permute-done.3 = f32[64,512]{1,0:T(8,128)S(1)} collective-permute-done((f32[64,512]{1,0:T(8,128)S(1)}, f32[64,512]{1,0:T(8,128)S(1)}, u32[]{:S(2)}, u32[]{:S(2)}) %collective-permute-start.3) | collective-permute-done | bytes 131104 | tf_op jit(solution)/shard_map/ppermute | solution.py:305
  33.0 0.8 %collective-permute-done.4.g_ref = f32[64,512]{1,0:T(8,128)S(1)} collective-permute-done((f32[64,512]{1,0:T(8,128)S(1)}, f32[64,512]{1,0:T(8,128)S(1)}, u32[]{:S(2)}, u32[]{:S(2)}) %collective-permute-start.4) | collective-permute-done | bytes 131104 | tf_op jit(solution)/shard_map/ppermute | solution.py:305
  34.1 0.8 %collective-permute-start.7 = (f32[256,128]{1,0:T(8,128)S(1)}, f32[256,128]{1,0:T(8,128)S(1)}, u32[]{:S(2)}, u32[]{:S(2)}) collective-permute-start(f32[256,128]{1,0:T(8,128)S(1)} %get-tuple-element.63), channel_id=1, source_target_pairs={{0,12},{4,8},{8,4},{12,0},{16,28},{20,24},{24,20},{28,16},{1,13},{... | collective-permute-start | bytes 393224 | tf_op jit(solution)/shard_map/ppermute | solution.py:305
  35.1 1.1 %collective-permute-start.6 = (f32[256,128]{1,0:T(8,128)S(1)}, f32[256,128]{1,0:T(8,128)S(1)}, u32[]{:S(2)}, u32[]{:S(2)}) collective-permute-start(f32[256,128]{1,0:T(8,128)S(1)} %get-tuple-element.62), channel_id=1, source_target_pairs={{0,8},{4,12},{8,0},{12,4},{16,24},{20,28},{24,16},{28,20},{1,9},{5... | collective-permute-start | bytes 393224 | tf_op jit(solution)/shard_map/ppermute | solution.py:305
  36.5 1.8 %collective-permute-start.5 = (f32[256,128]{1,0:T(8,128)S(1)}, f32[256,128]{1,0:T(8,128)S(1)}, u32[]{:S(2)}, u32[]{:S(2)}) collective-permute-start(f32[256,128]{1,0:T(8,128)S(1)} %get-tuple-element.61), channel_id=1, source_target_pairs={{0,4},{4,0},{8,12},{12,8},{16,20},{20,16},{24,28},{28,24},{1,5},{5... | collective-permute-start | bytes 393224 | tf_op jit(solution)/shard_map/ppermute | solution.py:305
  38.5 2.9 %collective-permute-done.7 = f32[256,128]{1,0:T(8,128)S(1)} collective-permute-done((f32[256,128]{1,0:T(8,128)S(1)}, f32[256,128]{1,0:T(8,128)S(1)}, u32[]{:S(2)}, u32[]{:S(2)}) %collective-permute-start.7) | collective-permute-done | bytes 131104 | tf_op jit(solution)/shard_map/ppermute | solution.py:305
  41.4 0.8 %collective-permute-done.6 = f32[256,128]{1,0:T(8,128)S(1)} collective-permute-done((f32[256,128]{1,0:T(8,128)S(1)}, f32[256,128]{1,0:T(8,128)S(1)}, u32[]{:S(2)}, u32[]{:S(2)}) %collective-permute-start.6) | collective-permute-done | bytes 131104 | tf_op jit(solution)/shard_map/ppermute | solution.py:305
  42.2 1.2 %collective-permute-done.5 = f32[256,128]{1,0:T(8,128)S(1)} collective-permute-done((f32[256,128]{1,0:T(8,128)S(1)}, f32[256,128]{1,0:T(8,128)S(1)}, u32[]{:S(2)}, u32[]{:S(2)}) %collective-permute-start.5) | collective-permute-done | bytes 131104 | tf_op jit(solution)/shard_map/ppermute | solution.py:305
  44.2 1.6 %collective-permute-start.13 = (f32[256,128]{1,0:T(8,128)S(1)}, f32[256,128]{1,0:T(8,128)S(1)}, u32[]{:S(2)}, u32[]{:S(2)}) collective-permute-start(f32[256,128]{1,0:T(8,128)S(1)} %get-tuple-element.68), channel_id=1, source_target_pairs={{0,2},{1,3},{2,0},{3,1},{4,6},{5,7},{6,4},{7,5},{8,10},{9,11},{10,... | collective-permute-start | bytes 393224 | tf_op jit(solution)/shard_map/ppermute | solution.py:305
  46.1 5.5 %collective-permute-done.8 = f32[256,128]{1,0:T(8,128)S(1)} collective-permute-done((f32[256,128]{1,0:T(8,128)S(1)}, f32[256,128]{1,0:T(8,128)S(1)}, u32[]{:S(2)}, u32[]{:S(2)}) %collective-permute-start.8) | collective-permute-done | bytes 131104 | tf_op jit(solution)/shard_map/ppermute | solution.py:305
  51.6 1.0 %collective-permute-start.9 = (f32[256,128]{1,0:T(8,128)S(1)}, f32[256,128]{1,0:T(8,128)S(1)}, u32[]{:S(2)}, u32[]{:S(2)}) collective-permute-start(f32[256,128]{1,0:T(8,128)S(1)} %add.27.refs_0_), channel_id=1, source_target_pairs={{0,4},{4,0},{8,12},{12,8},{16,20},{20,16},{24,28},{28,24},{1,5},{5... | collective-permute-start | bytes 393224 | tf_op jit(solution)/shard_map/ppermute | solution.py:305
  52.5 2.6 %collective-permute-start.11 = (f32[256,128]{1,0:T(8,128)S(1)}, f32[256,128]{1,0:T(8,128)S(1)}, u32[]{:S(2)}, u32[]{:S(2)}) collective-permute-start(f32[256,128]{1,0:T(8,128)S(1)} %add.27.refs_0_), channel_id=1, source_target_pairs={{0,12},{4,8},{8,4},{12,0},{16,28},{20,24},{24,20},{28,16},{1,13},{... | collective-permute-start | bytes 393224 | tf_op jit(solution)/shard_map/ppermute | solution.py:305
  55.1 2.0 %collective-permute-done.9.refs_1_ = f32[256,128]{1,0:T(8,128)S(1)} collective-permute-done((f32[256,128]{1,0:T(8,128)S(1)}, f32[256,128]{1,0:T(8,128)S(1)}, u32[]{:S(2)}, u32[]{:S(2)}) %collective-permute-start.9) | collective-permute-done | bytes 131104 | tf_op jit(solution)/shard_map/ppermute | solution.py:305
  57.1 1.4 %collective-permute-done.10.refs_2_ = f32[256,128]{1,0:T(8,128)S(1)} collective-permute-done((f32[256,128]{1,0:T(8,128)S(1)}, f32[256,128]{1,0:T(8,128)S(1)}, u32[]{:S(2)}, u32[]{:S(2)}) %collective-permute-start.10) | collective-permute-done | bytes 131104 | tf_op jit(solution)/shard_map/ppermute | solution.py:305
  58.6 2.5 %collective-permute-done.11.refs_3_ = f32[256,128]{1,0:T(8,128)S(1)} collective-permute-done((f32[256,128]{1,0:T(8,128)S(1)}, f32[256,128]{1,0:T(8,128)S(1)}, u32[]{:S(2)}, u32[]{:S(2)}) %collective-permute-start.11) | collective-permute-done | bytes 131104 | tf_op jit(solution)/shard_map/ppermute | solution.py:305
  61.1 0.9 %shard_map.91 = (f32[1024,128]{1,0:T(8,128)}, f32[256,128]{1,0:T(8,128)}) custom-call(f32[256,128]{1,0:T(8,128)S(1)} %add.27.refs_0_, f32[256,128]{1,0:T(8,128)S(1)} %collective-permute-done.9.refs_1_, f32[256,128]{1,0:T(8,128)S(1)} %collective-permute-done.10.refs_2_, f32[256,128]{1,0:T(8,128)S(1)} %collective-permute-done.11.refs_3_, ...), custom_call_target="tpu_custom_call" | custom-call | tf_op jit(solution)/shard_map/pallas_call | solution.py:434
  (28 shorter events, 5.2 us)
Async XLA Ops:
  2.3 2.3 %collective-permute-start = (f32[64,512]{1,0:T(8,128)S(1)}, f32[64,512]{1,0:T(8,128)S(1)}, u32[]{:S(2)}, u32[]{:S(2)}) collective-permute-start(f32[64,512]{1,0:T(8,128)S(1)} %get-tuple-element.42), channel_id=1, source_target_pairs={{0,1},{1,0},{2,3},{3,2},{4,5},{5,4},{6,7},{7,6},{8,9},{9,8},{10,11... | collective-permute-start | bytes 393224 | tf_op jit(solution)/shard_map/ppermute | solution.py:305
  4.7 6.8 %collective-permute-start.1 = (f32[64,512]{1,0:T(8,128)S(1)}, f32[64,512]{1,0:T(8,128)S(1)}, u32[]{:S(2)}, u32[]{:S(2)}) collective-permute-start(f32[64,512]{1,0:T(8,128)S(1)} %add.21.mine_ref), channel_id=1, source_target_pairs={{0,2},{1,3},{2,0},{3,1},{4,6},{5,7},{6,4},{7,5},{8,10},{9,11},{10,... | collective-permute-start | bytes 393224 | tf_op jit(solution)/shard_map/ppermute | solution.py:305
  25.3 1.4 %collective-permute-start.2 = (f32[72,512]{1,0:T(8,128)S(1)}, f32[72,512]{1,0:T(8,128)S(1)}, u32[]{:S(2)}, u32[]{:S(2)}) collective-permute-start(f32[72,512]{1,0:T(8,128)S(1)} %get-tuple-element.49), channel_id=1, source_target_pairs={{0,1},{1,0},{2,3},{3,2},{4,5},{5,4},{6,7},{7,6},{8,9},{9,8},{10,11... | collective-permute-start | bytes 442376 | tf_op jit(solution)/shard_map/ppermute | solution.py:305
  26.7 5.6 %collective-permute-start.3 = (f32[64,512]{1,0:T(8,128)S(1)}, f32[64,512]{1,0:T(8,128)S(1)}, u32[]{:S(2)}, u32[]{:S(2)}) collective-permute-start(f32[64,512]{1,0:T(8,128)S(1)} %slice_add_fusion), channel_id=1, source_target_pairs={{0,2},{1,3},{2,0},{3,1},{4,6},{5,7},{6,4},{7,5},{8,10},{9,11},{10,... | collective-permute-start | bytes 393224 | tf_op jit(solution)/shard_map/ppermute | solution.py:305
  32.4 1.4 %collective-permute-start.4 = (f32[64,512]{1,0:T(8,128)S(1)}, f32[64,512]{1,0:T(8,128)S(1)}, u32[]{:S(2)}, u32[]{:S(2)}) collective-permute-start(f32[64,512]{1,0:T(8,128)S(1)} %subtract_multiply_fusion.g_ref), channel_id=1, source_target_pairs={{0,1},{1,0},{2,3},{3,2},{4,5},{5,4},{6,7},{7,6},{8,9},{9,8},{10,11... | collective-permute-start | bytes 393224 | tf_op jit(solution)/shard_map/ppermute | solution.py:305
  34.1 7.3 %collective-permute-start.7 = (f32[256,128]{1,0:T(8,128)S(1)}, f32[256,128]{1,0:T(8,128)S(1)}, u32[]{:S(2)}, u32[]{:S(2)}) collective-permute-start(f32[256,128]{1,0:T(8,128)S(1)} %get-tuple-element.63), channel_id=1, source_target_pairs={{0,12},{4,8},{8,4},{12,0},{16,28},{20,24},{24,20},{28,16},{1,13},{... | collective-permute-start | bytes 393224 | tf_op jit(solution)/shard_map/ppermute | solution.py:305
  35.1 7.1 %collective-permute-start.6 = (f32[256,128]{1,0:T(8,128)S(1)}, f32[256,128]{1,0:T(8,128)S(1)}, u32[]{:S(2)}, u32[]{:S(2)}) collective-permute-start(f32[256,128]{1,0:T(8,128)S(1)} %get-tuple-element.62), channel_id=1, source_target_pairs={{0,8},{4,12},{8,0},{12,4},{16,24},{20,28},{24,16},{28,20},{1,9},{5... | collective-permute-start | bytes 393224 | tf_op jit(solution)/shard_map/ppermute | solution.py:305
  36.5 6.9 %collective-permute-start.5 = (f32[256,128]{1,0:T(8,128)S(1)}, f32[256,128]{1,0:T(8,128)S(1)}, u32[]{:S(2)}, u32[]{:S(2)}) collective-permute-start(f32[256,128]{1,0:T(8,128)S(1)} %get-tuple-element.61), channel_id=1, source_target_pairs={{0,4},{4,0},{8,12},{12,8},{16,20},{20,16},{24,28},{28,24},{1,5},{5... | collective-permute-start | bytes 393224 | tf_op jit(solution)/shard_map/ppermute | solution.py:305
  43.4 8.1 %collective-permute-start.8 = (f32[256,128]{1,0:T(8,128)S(1)}, f32[256,128]{1,0:T(8,128)S(1)}, u32[]{:S(2)}, u32[]{:S(2)}) collective-permute-start(f32[256,128]{1,0:T(8,128)S(1)} %add_add_fusion), channel_id=1, source_target_pairs={{0,16},{4,20},{8,24},{12,28},{16,0},{20,4},{24,8},{28,12},{1,17},{... | collective-permute-start | bytes 393224 | tf_op jit(solution)/shard_map/ppermute | solution.py:305
  44.1 8.4 %collective-permute-start.12 = (f32[256,128]{1,0:T(8,128)S(1)}, f32[256,128]{1,0:T(8,128)S(1)}, u32[]{:S(2)}, u32[]{:S(2)}) collective-permute-start(f32[256,128]{1,0:T(8,128)S(1)} %get-tuple-element.67), channel_id=1, source_target_pairs={{0,1},{1,0},{2,3},{3,2},{4,5},{5,4},{6,7},{7,6},{8,9},{9,8},{10,11... | collective-permute-start | bytes 393224 | tf_op jit(solution)/shard_map/ppermute | solution.py:305
  44.2 10.9 %collective-permute-start.13 = (f32[256,128]{1,0:T(8,128)S(1)}, f32[256,128]{1,0:T(8,128)S(1)}, u32[]{:S(2)}, u32[]{:S(2)}) collective-permute-start(f32[256,128]{1,0:T(8,128)S(1)} %get-tuple-element.68), channel_id=1, source_target_pairs={{0,2},{1,3},{2,0},{3,1},{4,6},{5,7},{6,4},{7,5},{8,10},{9,11},{10,... | collective-permute-start | bytes 393224 | tf_op jit(solution)/shard_map/ppermute | solution.py:305
  45.8 9.3 %collective-permute-start.14 = (f32[256,128]{1,0:T(8,128)S(1)}, f32[256,128]{1,0:T(8,128)S(1)}, u32[]{:S(2)}, u32[]{:S(2)}) collective-permute-start(f32[256,128]{1,0:T(8,128)S(1)} %get-tuple-element.69), channel_id=1, source_target_pairs={{0,3},{1,2},{2,1},{3,0},{4,7},{5,6},{6,5},{7,4},{8,11},{9,10},{10,... | collective-permute-start | bytes 393224 | tf_op jit(solution)/shard_map/ppermute | solution.py:305
  51.6 5.5 %collective-permute-start.9 = (f32[256,128]{1,0:T(8,128)S(1)}, f32[256,128]{1,0:T(8,128)S(1)}, u32[]{:S(2)}, u32[]{:S(2)}) collective-permute-start(f32[256,128]{1,0:T(8,128)S(1)} %add.27.refs_0_), channel_id=1, source_target_pairs={{0,4},{4,0},{8,12},{12,8},{16,20},{20,16},{24,28},{28,24},{1,5},{5... | collective-permute-start | bytes 393224 | tf_op jit(solution)/shard_map/ppermute | solution.py:305
  52.5 6.0 %collective-permute-start.10 = (f32[256,128]{1,0:T(8,128)S(1)}, f32[256,128]{1,0:T(8,128)S(1)}, u32[]{:S(2)}, u32[]{:S(2)}) collective-permute-start(f32[256,128]{1,0:T(8,128)S(1)} %add.27.refs_0_), channel_id=1, source_target_pairs={{0,8},{4,12},{8,0},{12,4},{16,24},{20,28},{24,16},{28,20},{1,9},{5... | collective-permute-start | bytes 393224 | tf_op jit(solution)/shard_map/ppermute | solution.py:305
  52.5 8.5 %collective-permute-start.11 = (f32[256,128]{1,0:T(8,128)S(1)}, f32[256,128]{1,0:T(8,128)S(1)}, u32[]{:S(2)}, u32[]{:S(2)}) collective-permute-start(f32[256,128]{1,0:T(8,128)S(1)} %add.27.refs_0_), channel_id=1, source_target_pairs={{0,12},{4,8},{8,4},{12,0},{16,28},{20,24},{24,20},{28,16},{1,13},{... | collective-permute-start | bytes 393224 | tf_op jit(solution)/shard_map/ppermute | solution.py:305

commit v6 on v5

--- a/solution.py
+++ b/solution.py
@@ -18,7 +18,6 @@
 VMEM = pl.BlockSpec(memory_space=pltpu.VMEM)
 HBM = pl.BlockSpec(memory_space=pltpu.HBM)
 CONTRACT_LAST = (((1,), (1,)), ((), ()))
-COLUMNS = 256
 QUAD = 4
 
 
@@ -101,7 +100,7 @@
 def kept_logits_kernel(
     n_rows, n_heads, bias_ref, iq_ref, ik_ref, w_ref, q_hbm, keep_ref, q_ref, sem
 ):
-    copy = pltpu.make_async_copy(q_hbm, q_ref, sem)
+    copy = pltpu.make_async_copy(q_hbm.at[pl.ds(0, q_ref.shape[0]), :], q_ref, sem)
     copy.start()
     half = keep_ref.shape[1]
     core = lax.axis_index("heads") & 1
@@ -110,32 +109,38 @@
     copy.wait()
 
 
-def scores_kernel(n_rows, n_heads, bias_ref, q_ref, lat_ref, p_ref, stat_ref, s_even, s_odd):
+def scores_kernel(
+    n_rows, n_heads, bias_ref, q_ref, q_hbm, lat_ref, p_ref, stat_ref, s_even, s_odd, q_rest, sem
+):
+    ready = q_ref.shape[0]
+    copy = pltpu.make_async_copy(q_hbm.at[pl.ds(ready, q_rest.shape[0]), :], q_rest, sem)
+    copy.start()
     block = s_even.shape[0]
-    keys = lat_ref.shape[1]
-    steps = keys // COLUMNS
-    per = block // n_heads // steps
-    strips = n_rows * n_heads // block * steps
-    for step in range(strips + steps):
-        if step < strips:
-            b, n = divmod(step, steps)
-            held = s_even if b % 2 == 0 else s_odd
-            held[:, n * COLUMNS : (n + 1) * COLUMNS] = jnp.dot(
-                q_ref[b * block : (b + 1) * block, :],
-                lat_ref[:, n * COLUMNS : (n + 1) * COLUMNS],
-                preferred_element_type=F32,
-            )
-        if step >= steps:
-            b, n = divmod(step - steps, steps)
-            held = s_even if b % 2 == 0 else s_odd
-            for i in range(n * per, (n + 1) * per):
-                row = b * (block // n_heads) + i
-                x = held[i * n_heads : (i + 1) * n_heads, :] + bias_ref[row : row + 1, :]
-                top = jnp.max(x, axis=1, keepdims=True)
-                e = jnp.exp2((x - top) * SCORE_LOG2)
-                p_ref[row * n_heads : (row + 1) * n_heads, :] = e
-                stat_ref[:, row : row + 1] = top
-                stat_ref[:, n_rows + row : n_rows + row + 1] = jnp.sum(e, axis=1, keepdims=True)
+    blocks = n_rows * n_heads // block
+
+    def dots(b):
+        held = s_even if b % 2 == 0 else s_odd
+        first = b * block
+        if first == ready:
+            copy.wait()
+        source = q_ref[first : first + block, :] if first < ready else q_rest[
+            first - ready : first - ready + block, :
+        ]
+        held[...] = jnp.dot(source, lat_ref[...], preferred_element_type=F32)
+
+    dots(0)
+    for b in range(blocks):
+        if b + 1 < blocks:
+            dots(b + 1)
+        held = s_even if b % 2 == 0 else s_odd
+        for i in range(block // n_heads):
+            row = b * (block // n_heads) + i
+            x = held[i * n_heads : (i + 1) * n_heads, :] + bias_ref[row : row + 1, :]
+            top = jnp.max(x, axis=1, keepdims=True)
+            e = jnp.exp2((x - top) * SCORE_LOG2)
+            p_ref[row * n_heads : (row + 1) * n_heads, :] = e
+            stat_ref[:, row : row + 1] = top
+            stat_ref[:, n_rows + row : n_rows + row + 1] = jnp.sum(e, axis=1, keepdims=True)
 
 
 def index_stats_kernel(mine_ref, other_ref, stat_ref, e_ref, out_ref, col):
@@ -341,9 +346,10 @@
     flat_queries = pltpu.with_memory_space_constraint(
         queries.reshape(n_rows * heads_local, width), pltpu.HBM
     )
+    ready = n_rows * heads_local // 2
     keep, q = call(
         functools.partial(kept_logits_kernel, n_rows, index_local),
-        (shape((n_rows, half), F32), shape(flat_queries.shape, BF16)),
+        (shape((n_rows, half), F32), shape((ready, width), BF16)),
         [VMEM] * 4 + [HBM],
         scratch=[pltpu.SemaphoreType.DMA],
         flops=flat[0] * depth * keys,
@@ -354,12 +360,13 @@
     probs, stats = call(
         functools.partial(scores_kernel, n_rows, heads_local),
         (shape((n_rows * heads_local, keys), F32), shape((heads_local, 2 * n_rows), F32)),
-        [VMEM] * 3,
-        scratch=[pltpu.VMEM((256, keys), F32)] * 2,
+        [VMEM, VMEM, HBM, VMEM],
+        scratch=[pltpu.VMEM((256, keys), F32)] * 2
+        + [pltpu.VMEM((n_rows * heads_local - ready, width), BF16), pltpu.SemaphoreType.DMA],
         flops=2 * queries.size * keys,
         exps=n_rows * heads_local * keys,
         nbytes=queries.size * 2,
-    )(bias, q, lat)
+    )(bias, q, flat_queries, lat)
     exps, sizes = call(
         index_stats_kernel,
         (shape((n_rows, half), F32), shape((heads_local // 2 + 8, 2 * n_rows), F32)),

time: 62.1 us -> 61.7 us (level)
  transfers between devices with their start and end apart: 15 -> 15, of which waited for: 10 -> 10; matrix products, arithmetic and copies ran while one was open for 0% -> 0% of each run, Pallas kernels for 15% -> 14%
where the time goes in v6:
time: 61.7 us; the launch traced here: 61.5 us
  waiting for transfers between devices  20.8 us (34%)
  starting transfers between devices  14.5 us (24%)
  blocking collectives  12.7 us (21%)
  Pallas kernels  12.5 us (20%)
  between operations  0.8 us (1%)
    ppermute x15, waiting for transfers between devices, swapped(): return lax.ppermute(value, axis, [(i, i ^ k) for i in range(n)])  20.8 us
    ppermute x15, starting transfers between devices, swapped(): return lax.ppermute(value, axis, [(i, i ^ k) for i in range(n)])  14.5 us
    all_to_all x1, blocking collectives, body(): lax.all_to_all(jnp.broadcast_to(sizes, (n_ctx,) + sizes.shape), 'ctx', 0, 0)  12.7 us
    pallas_call x1, Pallas kernels, body(): call(functools.partial(scores_kernel, n_rows, heads_local), (shape((n_row...  4.38 us
    pallas_call x1, Pallas kernels, body(): call(functools.partial(logits_kernel, n_rows, index_local, (index_local *...  1.7 us
    pallas_call x1, Pallas kernels, body(): call(functools.partial(kept_logits_kernel, n_rows, index_local), (shape((...  1.33 us
  transfers between devices with their start and end apart: 15, of which 10 were waited for; matrix products, arithmetic and copies ran while one was open for 0% of the time, Pallas kernels for 14%

profile of v6, /device:TPU:0, one launch (start us, length us, event | category | flops | bytes accessed | tf_op | source)
XLA Modules:
  0.0 61.5 jit_solution(11208112642623878755)
XLA Ops:
  0.6 1.7 %shard_map.77 = (f32[64,512]{1,0:T(8,128)S(1)}, f32[64,1024]{1,0:T(8,128)S(1)}, bf16[1024,128]{1,0:T(8,128)(2,1)S(1)}, bf16[1024,128]{1,0:T(8,128)(2,1)S(1)}, f3...) custom-call(s32[64]{0:T(128)} %pos_hbm.1, bf16[1024,128]{1,0:T(8,128)(2,1)} %bitcast.8, bf16[1024,128]{1,0:T(8,128)(2,1)} %ik_hbm.1, ...), custom_call_target="tpu_custom_call" | custom-call | flops 134217728 | bytes 1179648 | tf_op jit(solution)/shard_map/pallas_call | solution.py:313
  2.9 1.3 %shard_map.78 = (f32[64,512]{1,0:T(8,128)S(1)}, bf16[1024,576]{1,0:T(8,128)(2,1)S(1)}) custom-call(f32[64,1024]{1,0:T(8,128)S(1)} %get-tuple-element.37.bias_ref, bf16[1024,128]{1,0:T(8,128)(2,1)S(1)} %get-tuple-element.38.iq_ref, bf16[1024,128]{1,0:T(8,128)(2,1)S(1)} %get-tuple-element.39.ik_ref, f32[1024,128]{1,0:T(8,128)S(1)} %get-tuple-element.40.w_ref, ...), custom_call_target="tpu_custom_call" | custom-call | flops 134217728 | bytes 2359296 | tf_op jit(solution)/shard_map/pallas_call | solution.py:350
  4.3 2.6 %collective-permute-start.1 = (f32[64,512]{1,0:T(8,128)S(1)}, f32[64,512]{1,0:T(8,128)S(1)}, u32[]{:S(2)}, u32[]{:S(2)}) collective-permute-start(f32[64,512]{1,0:T(8,128)S(1)} %add.21.mine_ref), channel_id=1, source_target_pairs={{0,2},{1,3},{2,0},{3,1},{4,6},{5,7},{6,4},{7,5},{8,10},{9,11},{10,... | collective-permute-start | bytes 393224 | tf_op jit(solution)/shard_map/ppermute | solution.py:310
  6.9 4.4 %shard_map.79 = (f32[2048,1024]{1,0:T(8,128)S(1)}, f32[32,128]{1,0:T(8,128)S(1)}) custom-call(f32[64,1024]{1,0:T(8,128)S(1)} %get-tuple-element.37.bias_ref, bf16[1024,576]{1,0:T(8,128)(2,1)S(1)} %get-tuple-element.43.q_ref, bf16[2048,576]{1,0:T(8,128)(2,1)} %bitcast.6, bf16[576,1024]{1,0:T(8,128)(2,1)S(1)} %get-tuple-element.44.lat_ref), custom_call_target="tpu_custom_call" | custom-call | flops 2415919104 | bytes 2359296 | tf_op jit(solution)/shard_map/pallas_call | solution.py:360
  11.5 12.7 %all_to_all.5.all_ref = f32[8,24,128]{2,1,0:T(8,128)S(1)} all-to-all(f32[8,24,128]{2,1,0:T(8,128)S(1)} %broadcast_in_dim.3), channel_id=1, replica_groups=mesh['ctx'=8,'heads'=4] {'ctx'}, dimensions={0} | all-to-all | bytes 196608 | tf_op jit(solution)/shard_map/all_to_all | solution.py:376
  25.5 0.8 %collective-permute-done.2.other_ref = f32[72,512]{1,0:T(8,128)S(1)} collective-permute-done((f32[72,512]{1,0:T(8,128)S(1)}, f32[72,512]{1,0:T(8,128)S(1)}, u32[]{:S(2)}, u32[]{:S(2)}) %collective-permute-start.2) | collective-permute-done | bytes 147488 | tf_op jit(solution)/shard_map/ppermute | solution.py:310
  26.3 1.6 %collective-permute-start.3 = (f32[64,512]{1,0:T(8,128)S(1)}, f32[64,512]{1,0:T(8,128)S(1)}, u32[]{:S(2)}, u32[]{:S(2)}) collective-permute-start(f32[64,512]{1,0:T(8,128)S(1)} %slice_add_fusion), channel_id=1, source_target_pairs={{0,2},{1,3},{2,0},{3,1},{4,6},{5,7},{6,4},{7,5},{8,10},{9,11},{10,... | collective-permute-start | bytes 393224 | tf_op jit(solution)/shard_map/ppermute | solution.py:310
  27.9 0.7 %shard_map.84 = (f32[1024,1024]{1,0:T(8,128)S(1)}, bf16[128,1024]{1,0:T(8,128)(2,1)S(1)}) custom-call(bf16[1024,128]{1,0:T(8,128)(2,1)S(1)} %get-tuple-element.38.iq_ref, bf16[1024,128]{1,0:T(8,128)(2,1)S(1)} %get-tuple-element.39.ik_ref, f32[1024,128]{1,0:T(8,128)S(1)} %get-tuple-element.40.w_ref), custom_call_target="tpu_custom_call" | custom-call | flops 268435456 | tf_op jit(solution)/shard_map/pallas_call | solution.py:397
  28.9 3.0 %collective-permute-done.3 = f32[64,512]{1,0:T(8,128)S(1)} collective-permute-done((f32[64,512]{1,0:T(8,128)S(1)}, f32[64,512]{1,0:T(8,128)S(1)}, u32[]{:S(2)}, u32[]{:S(2)}) %collective-permute-start.3) | collective-permute-done | bytes 131104 | tf_op jit(solution)/shard_map/ppermute | solution.py:310
  32.6 0.8 %collective-permute-done.4.g_ref = f32[64,512]{1,0:T(8,128)S(1)} collective-permute-done((f32[64,512]{1,0:T(8,128)S(1)}, f32[64,512]{1,0:T(8,128)S(1)}, u32[]{:S(2)}, u32[]{:S(2)}) %collective-permute-start.4) | collective-permute-done | bytes 131104 | tf_op jit(solution)/shard_map/ppermute | solution.py:310
  33.6 0.8 %collective-permute-start.7 = (f32[256,128]{1,0:T(8,128)S(1)}, f32[256,128]{1,0:T(8,128)S(1)}, u32[]{:S(2)}, u32[]{:S(2)}) collective-permute-start(f32[256,128]{1,0:T(8,128)S(1)} %get-tuple-element.63), channel_id=1, source_target_pairs={{0,12},{4,8},{8,4},{12,0},{16,28},{20,24},{24,20},{28,16},{1,13},{... | collective-permute-start | bytes 393224 | tf_op jit(solution)/shard_map/ppermute | solution.py:310
  34.7 1.1 %collective-permute-start.6 = (f32[256,128]{1,0:T(8,128)S(1)}, f32[256,128]{1,0:T(8,128)S(1)}, u32[]{:S(2)}, u32[]{:S(2)}) collective-permute-start(f32[256,128]{1,0:T(8,128)S(1)} %get-tuple-element.62), channel_id=1, source_target_pairs={{0,8},{4,12},{8,0},{12,4},{16,24},{20,28},{24,16},{28,20},{1,9},{5... | collective-permute-start | bytes 393224 | tf_op jit(solution)/shard_map/ppermute | solution.py:310
  36.0 1.8 %collective-permute-start.5 = (f32[256,128]{1,0:T(8,128)S(1)}, f32[256,128]{1,0:T(8,128)S(1)}, u32[]{:S(2)}, u32[]{:S(2)}) collective-permute-start(f32[256,128]{1,0:T(8,128)S(1)} %get-tuple-element.61), channel_id=1, source_target_pairs={{0,4},{4,0},{8,12},{12,8},{16,20},{20,16},{24,28},{28,24},{1,5},{5... | collective-permute-start | bytes 393224 | tf_op jit(solution)/shard_map/ppermute | solution.py:310
  38.1 2.9 %collective-permute-done.7 = f32[256,128]{1,0:T(8,128)S(1)} collective-permute-done((f32[256,128]{1,0:T(8,128)S(1)}, f32[256,128]{1,0:T(8,128)S(1)}, u32[]{:S(2)}, u32[]{:S(2)}) %collective-permute-start.7) | collective-permute-done | bytes 131104 | tf_op jit(solution)/shard_map/ppermute | solution.py:310
  41.0 0.8 %collective-permute-done.6 = f32[256,128]{1,0:T(8,128)S(1)} collective-permute-done((f32[256,128]{1,0:T(8,128)S(1)}, f32[256,128]{1,0:T(8,128)S(1)}, u32[]{:S(2)}, u32[]{:S(2)}) %collective-permute-start.6) | collective-permute-done | bytes 131104 | tf_op jit(solution)/shard_map/ppermute | solution.py:310
  41.8 1.2 %collective-permute-done.5 = f32[256,128]{1,0:T(8,128)S(1)} collective-permute-done((f32[256,128]{1,0:T(8,128)S(1)}, f32[256,128]{1,0:T(8,128)S(1)}, u32[]{:S(2)}, u32[]{:S(2)}) %collective-permute-start.5) | collective-permute-done | bytes 131104 | tf_op jit(solution)/shard_map/ppermute | solution.py:310
  43.8 1.6 %collective-permute-start.13 = (f32[256,128]{1,0:T(8,128)S(1)}, f32[256,128]{1,0:T(8,128)S(1)}, u32[]{:S(2)}, u32[]{:S(2)}) collective-permute-start(f32[256,128]{1,0:T(8,128)S(1)} %get-tuple-element.68), channel_id=1, source_target_pairs={{0,2},{1,3},{2,0},{3,1},{4,6},{5,7},{6,4},{7,5},{8,10},{9,11},{10,... | collective-permute-start | bytes 393224 | tf_op jit(solution)/shard_map/ppermute | solution.py:310
  45.7 5.5 %collective-permute-done.8 = f32[256,128]{1,0:T(8,128)S(1)} collective-permute-done((f32[256,128]{1,0:T(8,128)S(1)}, f32[256,128]{1,0:T(8,128)S(1)}, u32[]{:S(2)}, u32[]{:S(2)}) %collective-permute-start.8) | collective-permute-done | bytes 131104 | tf_op jit(solution)/shard_map/ppermute | solution.py:310
  51.2 0.9 %collective-permute-start.9 = (f32[256,128]{1,0:T(8,128)S(1)}, f32[256,128]{1,0:T(8,128)S(1)}, u32[]{:S(2)}, u32[]{:S(2)}) collective-permute-start(f32[256,128]{1,0:T(8,128)S(1)} %add.27.refs_0_), channel_id=1, source_target_pairs={{0,4},{4,0},{8,12},{12,8},{16,20},{20,16},{24,28},{28,24},{1,5},{5... | collective-permute-start | bytes 393224 | tf_op jit(solution)/shard_map/ppermute | solution.py:310
  52.1 2.6 %collective-permute-start.11 = (f32[256,128]{1,0:T(8,128)S(1)}, f32[256,128]{1,0:T(8,128)S(1)}, u32[]{:S(2)}, u32[]{:S(2)}) collective-permute-start(f32[256,128]{1,0:T(8,128)S(1)} %add.27.refs_0_), channel_id=1, source_target_pairs={{0,12},{4,8},{8,4},{12,0},{16,28},{20,24},{24,20},{28,16},{1,13},{... | collective-permute-start | bytes 393224 | tf_op jit(solution)/shard_map/ppermute | solution.py:310
  54.7 2.0 %collective-permute-done.9.refs_1_ = f32[256,128]{1,0:T(8,128)S(1)} collective-permute-done((f32[256,128]{1,0:T(8,128)S(1)}, f32[256,128]{1,0:T(8,128)S(1)}, u32[]{:S(2)}, u32[]{:S(2)}) %collective-permute-start.9) | collective-permute-done | bytes 131104 | tf_op jit(solution)/shard_map/ppermute | solution.py:310
  56.7 1.4 %collective-permute-done.10.refs_2_ = f32[256,128]{1,0:T(8,128)S(1)} collective-permute-done((f32[256,128]{1,0:T(8,128)S(1)}, f32[256,128]{1,0:T(8,128)S(1)}, u32[]{:S(2)}, u32[]{:S(2)}) %collective-permute-start.10) | collective-permute-done | bytes 131104 | tf_op jit(solution)/shard_map/ppermute | solution.py:310
  58.1 2.5 %collective-permute-done.11.refs_3_ = f32[256,128]{1,0:T(8,128)S(1)} collective-permute-done((f32[256,128]{1,0:T(8,128)S(1)}, f32[256,128]{1,0:T(8,128)S(1)}, u32[]{:S(2)}, u32[]{:S(2)}) %collective-permute-start.11) | collective-permute-done | bytes 131104 | tf_op jit(solution)/shard_map/ppermute | solution.py:310
  60.6 0.9 %shard_map.91 = (f32[1024,128]{1,0:T(8,128)}, f32[256,128]{1,0:T(8,128)}) custom-call(f32[256,128]{1,0:T(8,128)S(1)} %add.27.refs_0_, f32[256,128]{1,0:T(8,128)S(1)} %collective-permute-done.9.refs_1_, f32[256,128]{1,0:T(8,128)S(1)} %collective-permute-done.10.refs_2_, f32[256,128]{1,0:T(8,128)S(1)} %collective-permute-done.11.refs_3_, ...), custom_call_target="tpu_custom_call" | custom-call | tf_op jit(solution)/shard_map/pallas_call | solution.py:441
  (28 shorter events, 5.2 us)
Async XLA Ops:
  2.3 1.9 %collective-permute-start = (f32[64,512]{1,0:T(8,128)S(1)}, f32[64,512]{1,0:T(8,128)S(1)}, u32[]{:S(2)}, u32[]{:S(2)}) collective-permute-start(f32[64,512]{1,0:T(8,128)S(1)} %get-tuple-element.42), channel_id=1, source_target_pairs={{0,1},{1,0},{2,3},{3,2},{4,5},{5,4},{6,7},{7,6},{8,9},{9,8},{10,11... | collective-permute-start | bytes 393224 | tf_op jit(solution)/shard_map/ppermute | solution.py:310
  4.3 7.0 %collective-permute-start.1 = (f32[64,512]{1,0:T(8,128)S(1)}, f32[64,512]{1,0:T(8,128)S(1)}, u32[]{:S(2)}, u32[]{:S(2)}) collective-permute-start(f32[64,512]{1,0:T(8,128)S(1)} %add.21.mine_ref), channel_id=1, source_target_pairs={{0,2},{1,3},{2,0},{3,1},{4,6},{5,7},{6,4},{7,5},{8,10},{9,11},{10,... | collective-permute-start | bytes 393224 | tf_op jit(solution)/shard_map/ppermute | solution.py:310
  24.9 1.4 %collective-permute-start.2 = (f32[72,512]{1,0:T(8,128)S(1)}, f32[72,512]{1,0:T(8,128)S(1)}, u32[]{:S(2)}, u32[]{:S(2)}) collective-permute-start(f32[72,512]{1,0:T(8,128)S(1)} %get-tuple-element.49), channel_id=1, source_target_pairs={{0,1},{1,0},{2,3},{3,2},{4,5},{5,4},{6,7},{7,6},{8,9},{9,8},{10,11... | collective-permute-start | bytes 442376 | tf_op jit(solution)/shard_map/ppermute | solution.py:310
  26.3 5.6 %collective-permute-start.3 = (f32[64,512]{1,0:T(8,128)S(1)}, f32[64,512]{1,0:T(8,128)S(1)}, u32[]{:S(2)}, u32[]{:S(2)}) collective-permute-start(f32[64,512]{1,0:T(8,128)S(1)} %slice_add_fusion), channel_id=1, source_target_pairs={{0,2},{1,3},{2,0},{3,1},{4,6},{5,7},{6,4},{7,5},{8,10},{9,11},{10,... | collective-permute-start | bytes 393224 | tf_op jit(solution)/shard_map/ppermute | solution.py:310
  32.0 1.4 %collective-permute-start.4 = (f32[64,512]{1,0:T(8,128)S(1)}, f32[64,512]{1,0:T(8,128)S(1)}, u32[]{:S(2)}, u32[]{:S(2)}) collective-permute-start(f32[64,512]{1,0:T(8,128)S(1)} %subtract_multiply_fusion.g_ref), channel_id=1, source_target_pairs={{0,1},{1,0},{2,3},{3,2},{4,5},{5,4},{6,7},{7,6},{8,9},{9,8},{10,11... | collective-permute-start | bytes 393224 | tf_op jit(solution)/shard_map/ppermute | solution.py:310
  33.6 7.3 %collective-permute-start.7 = (f32[256,128]{1,0:T(8,128)S(1)}, f32[256,128]{1,0:T(8,128)S(1)}, u32[]{:S(2)}, u32[]{:S(2)}) collective-permute-start(f32[256,128]{1,0:T(8,128)S(1)} %get-tuple-element.63), channel_id=1, source_target_pairs={{0,12},{4,8},{8,4},{12,0},{16,28},{20,24},{24,20},{28,16},{1,13},{... | collective-permute-start | bytes 393224 | tf_op jit(solution)/shard_map/ppermute | solution.py:310
  34.7 7.1 %collective-permute-start.6 = (f32[256,128]{1,0:T(8,128)S(1)}, f32[256,128]{1,0:T(8,128)S(1)}, u32[]{:S(2)}, u32[]{:S(2)}) collective-permute-start(f32[256,128]{1,0:T(8,128)S(1)} %get-tuple-element.62), channel_id=1, source_target_pairs={{0,8},{4,12},{8,0},{12,4},{16,24},{20,28},{24,16},{28,20},{1,9},{5... | collective-permute-start | bytes 393224 | tf_op jit(solution)/shard_map/ppermute | solution.py:310
  36.0 6.9 %collective-permute-start.5 = (f32[256,128]{1,0:T(8,128)S(1)}, f32[256,128]{1,0:T(8,128)S(1)}, u32[]{:S(2)}, u32[]{:S(2)}) collective-permute-start(f32[256,128]{1,0:T(8,128)S(1)} %get-tuple-element.61), channel_id=1, source_target_pairs={{0,4},{4,0},{8,12},{12,8},{16,20},{20,16},{24,28},{28,24},{1,5},{5... | collective-permute-start | bytes 393224 | tf_op jit(solution)/shard_map/ppermute | solution.py:310
  43.0 8.2 %collective-permute-start.8 = (f32[256,128]{1,0:T(8,128)S(1)}, f32[256,128]{1,0:T(8,128)S(1)}, u32[]{:S(2)}, u32[]{:S(2)}) collective-permute-start(f32[256,128]{1,0:T(8,128)S(1)} %add_add_fusion), channel_id=1, source_target_pairs={{0,16},{4,20},{8,24},{12,28},{16,0},{20,4},{24,8},{28,12},{1,17},{... | collective-permute-start | bytes 393224 | tf_op jit(solution)/shard_map/ppermute | solution.py:310
  43.7 8.4 %collective-permute-start.12 = (f32[256,128]{1,0:T(8,128)S(1)}, f32[256,128]{1,0:T(8,128)S(1)}, u32[]{:S(2)}, u32[]{:S(2)}) collective-permute-start(f32[256,128]{1,0:T(8,128)S(1)} %get-tuple-element.67), channel_id=1, source_target_pairs={{0,1},{1,0},{2,3},{3,2},{4,5},{5,4},{6,7},{7,6},{8,9},{9,8},{10,11... | collective-permute-start | bytes 393224 | tf_op jit(solution)/shard_map/ppermute | solution.py:310
  43.8 10.9 %collective-permute-start.13 = (f32[256,128]{1,0:T(8,128)S(1)}, f32[256,128]{1,0:T(8,128)S(1)}, u32[]{:S(2)}, u32[]{:S(2)}) collective-permute-start(f32[256,128]{1,0:T(8,128)S(1)} %get-tuple-element.68), channel_id=1, source_target_pairs={{0,2},{1,3},{2,0},{3,1},{4,6},{5,7},{6,4},{7,5},{8,10},{9,11},{10,... | collective-permute-start | bytes 393224 | tf_op jit(solution)/shard_map/ppermute | solution.py:310
  45.4 9.3 %collective-permute-start.14 = (f32[256,128]{1,0:T(8,128)S(1)}, f32[256,128]{1,0:T(8,128)S(1)}, u32[]{:S(2)}, u32[]{:S(2)}) collective-permute-start(f32[256,128]{1,0:T(8,128)S(1)} %get-tuple-element.69), channel_id=1, source_target_pairs={{0,3},{1,2},{2,1},{3,0},{4,7},{5,6},{6,5},{7,4},{8,11},{9,10},{10,... | collective-permute-start | bytes 393224 | tf_op jit(solution)/shard_map/ppermute | solution.py:310
  51.2 5.5 %collective-permute-start.9 = (f32[256,128]{1,0:T(8,128)S(1)}, f32[256,128]{1,0:T(8,128)S(1)}, u32[]{:S(2)}, u32[]{:S(2)}) collective-permute-start(f32[256,128]{1,0:T(8,128)S(1)} %add.27.refs_0_), channel_id=1, source_target_pairs={{0,4},{4,0},{8,12},{12,8},{16,20},{20,16},{24,28},{28,24},{1,5},{5... | collective-permute-start | bytes 393224 | tf_op jit(solution)/shard_map/ppermute | solution.py:310
  52.1 6.0 %collective-permute-start.10 = (f32[256,128]{1,0:T(8,128)S(1)}, f32[256,128]{1,0:T(8,128)S(1)}, u32[]{:S(2)}, u32[]{:S(2)}) collective-permute-start(f32[256,128]{1,0:T(8,128)S(1)} %add.27.refs_0_), channel_id=1, source_target_pairs={{0,8},{4,12},{8,0},{12,4},{16,24},{20,28},{24,16},{28,20},{1,9},{5... | collective-permute-start | bytes 393224 | tf_op jit(solution)/shard_map/ppermute | solution.py:310
  52.1 8.5 %collective-permute-start.11 = (f32[256,128]{1,0:T(8,128)S(1)}, f32[256,128]{1,0:T(8,128)S(1)}, u32[]{:S(2)}, u32[]{:S(2)}) collective-permute-start(f32[256,128]{1,0:T(8,128)S(1)} %add.27.refs_0_), channel_id=1, source_target_pairs={{0,12},{4,8},{8,4},{12,0},{16,28},{20,24},{24,20},{28,16},{1,13},{... | collective-permute-start | bytes 393224 | tf_op jit(solution)/shard_map/ppermute | solution.py:310

commit v7 on v6

--- a/solution.py
+++ b/solution.py
@@ -17,6 +17,7 @@
 LANES = 128
 VMEM = pl.BlockSpec(memory_space=pltpu.VMEM)
 HBM = pl.BlockSpec(memory_space=pltpu.HBM)
+SMEM = pl.BlockSpec(memory_space=pltpu.SMEM)
 CONTRACT_LAST = (((1,), (1,)), ((), ()))
 QUAD = 4
 
@@ -59,7 +60,7 @@
 def logits_kernel(
     n_rows, n_heads, scale,
     pos_hbm, iq_hbm, ik_hbm, iw_hbm, lat_hbm,
-    send_ref, bias_ref, iq_ref, ik_ref, w_ref, lat_ref,
+    send_ref, bias_ref, iq_ref, ik_ref, w_ref, lat_ref, rows_ref,
     iw_ref, pos_ref, sems,
 ):
     half = send_ref.shape[1]
@@ -78,7 +79,16 @@
     for copy in copies:
         copy.start()
     copies[0].wait()
-    place = lax.axis_index("ctx") * 2 * half + lax.broadcasted_iota(jnp.int32, (8, 2 * half), 1)
+    start = lax.axis_index("ctx") * 2 * half
+    count = jnp.int32(0)
+    for seen in (True, False):
+        for row in range(n_rows):
+            rows_ref[count] = row
+            count += ((pos_ref[row] >= start) == seen).astype(jnp.int32)
+        if seen:
+            visible = count
+    rows_ref[n_rows + 1] = visible
+    place = start + lax.broadcasted_iota(jnp.int32, (8, 2 * half), 1)
     sublane = lax.broadcasted_iota(jnp.int32, (8, 1), 0)
     for first in range(0, n_rows, 8):
         pos = jnp.zeros((8, 1), jnp.int32)
@@ -110,37 +120,83 @@
 
 
 def scores_kernel(
-    n_rows, n_heads, bias_ref, q_ref, q_hbm, lat_ref, p_ref, stat_ref, s_even, s_odd, q_rest, sem
+    n_rows, n_heads, order_ref, bias_ref, q_ref, q_hbm, lat_ref, p_ref, stat_ref, s_even, s_odd, q_all, sems
 ):
     ready = q_ref.shape[0]
-    copy = pltpu.make_async_copy(q_hbm.at[pl.ds(ready, q_rest.shape[0]), :], q_rest, sem)
-    copy.start()
+    rest = pl.ds(ready, q_all.shape[0] - ready)
+    copies = (
+        pltpu.make_async_copy(q_hbm.at[rest, :], q_all.at[rest, :], sems.at[0]),
+        pltpu.make_async_copy(q_ref, q_all.at[pl.ds(0, ready), :], sems.at[1]),
+    )
+    for copy in copies:
+        copy.start()
     block = s_even.shape[0]
-    blocks = n_rows * n_heads // block
-
-    def dots(b):
+    per = block // n_heads
+    blocks = n_rows // per
+    lane = lax.broadcasted_iota(jnp.int32, (n_heads, 2 * n_rows), 1)
+
+    def scores(b, source):
         held = s_even if b % 2 == 0 else s_odd
-        first = b * block
-        if first == ready:
+        held[...] = jnp.dot(source, lat_ref[...], preferred_element_type=F32)
+
+    def finish(b, i, bias, at):
+        held = s_even if b % 2 == 0 else s_odd
+        x = held[i * n_heads : (i + 1) * n_heads, :] + bias
+        top = jnp.max(x, axis=1, keepdims=True)
+        e = jnp.exp2((x - top) * SCORE_LOG2)
+        p_ref[at, :] = e
+        return top, jnp.sum(e, axis=1, keepdims=True)
+
+    def all_rows():
+        def source(b):
+            first = b * block
+            if first == ready:
+                copies[0].wait()
+            return (q_ref if first < ready else q_all)[first : first + block, :]
+
+        scores(0, source(0))
+        for b in range(blocks):
+            if b + 1 < blocks:
+                scores(b + 1, source(b + 1))
+            for i in range(per):
+                row = b * per + i
+                at = slice(row * n_heads, (row + 1) * n_heads)
+                top, total = finish(b, i, bias_ref[row : row + 1, :], at)
+                stat_ref[:, row : row + 1] = top
+                stat_ref[:, n_rows + row : n_rows + row + 1] = total
+        copies[1].wait()
+
+    def some_rows(n_blocks):
+        for copy in copies:
             copy.wait()
-        source = q_ref[first : first + block, :] if first < ready else q_rest[
-            first - ready : first - ready + block, :
-        ]
-        held[...] = jnp.dot(source, lat_ref[...], preferred_element_type=F32)
-
-    dots(0)
-    for b in range(blocks):
-        if b + 1 < blocks:
-            dots(b + 1)
-        held = s_even if b % 2 == 0 else s_odd
-        for i in range(block // n_heads):
-            row = b * (block // n_heads) + i
-            x = held[i * n_heads : (i + 1) * n_heads, :] + bias_ref[row : row + 1, :]
-            top = jnp.max(x, axis=1, keepdims=True)
-            e = jnp.exp2((x - top) * SCORE_LOG2)
-            p_ref[row * n_heads : (row + 1) * n_heads, :] = e
-            stat_ref[:, row : row + 1] = top
-            stat_ref[:, n_rows + row : n_rows + row + 1] = jnp.sum(e, axis=1, keepdims=True)
+        stats = jnp.where(lane < n_rows, NEG, 1.0)
+
+        def place(row):
+            return pl.ds(pl.multiple_of(row * n_heads, n_heads), n_heads)
+
+        def source(b):
+            rows = [order_ref[b * per + i] for i in range(per)]
+            return jnp.concatenate([q_all[place(row), :] for row in rows], axis=0)
+
+        scores(0, source(0))
+        for b in range(n_blocks):
+            if b + 1 < n_blocks:
+                scores(b + 1, source(b + 1))
+            for i in range(per):
+                row = order_ref[b * per + i]
+                top, total = finish(b, i, bias_ref[pl.ds(row, 1), :], place(row))
+                stats = jnp.where(lane == row, top, jnp.where(lane == row + n_rows, total, stats))
+        for i in range(n_blocks * per, n_rows):
+            p_ref[place(order_ref[i]), :] = jnp.zeros((n_heads, p_ref.shape[1]), F32)
+        stat_ref[...] = stats
+
+    needed = (order_ref[n_rows + 1] + per - 1) // per
+    sizes = range(2, blocks, 2)
+    least = -1
+    for size in sizes:
+        pl.when((needed > least) & (needed <= size))(functools.partial(some_rows, size))
+        least = size
+    pl.when(needed > least)(all_rows)
 
 
 def index_stats_kernel(mine_ref, other_ref, stat_ref, e_ref, out_ref, col):
@@ -310,7 +366,7 @@
         return lax.ppermute(value, axis, [(i, i ^ k) for i in range(n)])
 
     flat = (n_rows * index_local, depth)
-    send, bias, iq, ik, w, lat = call(
+    send, bias, iq, ik, w, lat, order = call(
         functools.partial(
             logits_kernel, n_rows, index_local, (index_local * n_heads * depth) ** (-0.5)
         ),
@@ -321,8 +377,10 @@
             shape((keys, depth), BF16),
             shape((flat[0], LANES), F32),
             shape((width, keys), BF16),
+            shape((n_rows + 8,), jnp.int32),
         ),
         [HBM] * 5,
+        out_specs=(VMEM,) * 6 + (SMEM,),
         scratch=[
             pltpu.VMEM((index_local, n_rows), F32),
             pltpu.SMEM((n_rows,), jnp.int32),
@@ -346,7 +404,7 @@
     flat_queries = pltpu.with_memory_space_constraint(
         queries.reshape(n_rows * heads_local, width), pltpu.HBM
     )
-    ready = n_rows * heads_local // 2
+    ready = n_rows * heads_local // 4
     keep, q = call(
         functools.partial(kept_logits_kernel, n_rows, index_local),
         (shape((n_rows, half), F32), shape((ready, width), BF16)),
@@ -360,13 +418,13 @@
     probs, stats = call(
         functools.partial(scores_kernel, n_rows, heads_local),
         (shape((n_rows * heads_local, keys), F32), shape((heads_local, 2 * n_rows), F32)),
-        [VMEM, VMEM, HBM, VMEM],
+        [SMEM, VMEM, VMEM, HBM, VMEM],
         scratch=[pltpu.VMEM((256, keys), F32)] * 2
-        + [pltpu.VMEM((n_rows * heads_local - ready, width), BF16), pltpu.SemaphoreType.DMA],
+        + [pltpu.VMEM(flat_queries.shape, BF16), pltpu.SemaphoreType.DMA((2,))],
         flops=2 * queries.size * keys,
         exps=n_rows * heads_local * keys,
         nbytes=queries.size * 2,
-    )(bias, q, flat_queries, lat)
+    )(order, bias, q, flat_queries, lat)
     exps, sizes = call(
         index_stats_kernel,
         (shape((n_rows, half), F32), shape((heads_local // 2 + 8, 2 * n_rows), F32)),

time: 61.7 us -> 63.2 us (1.024)
  Pallas kernels: 12.5 us -> 14.4 us
  blocking collectives: 12.7 us -> 11.9 us
  waiting for transfers between devices: 20.8 us -> 21.5 us
    pallas_call x1, Pallas kernels: 4.38 us -> 5.61 us  [body(): call(functools.partial(scores_kernel, n_rows, heads_local), (shape((n_row...]
    all_to_all x1, blocking collectives: 12.7 us -> 11.9 us  [body(): lax.all_to_all(jnp.broadcast_to(sizes, (n_ctx,) + sizes.shape), 'ctx', 0, 0)]
    pallas_call x1, Pallas kernels: 1.7 us -> 2.49 us  [body(): call(functools.partial(logits_kernel, n_rows, index_local, (index_local *...]
    ppermute x15, waiting for transfers between devices: 20.8 us -> 21.5 us  [swapped(): return lax.ppermute(value, axis, [(i, i ^ k) for i in range(n)])]
  transfers between devices with their start and end apart: 15 -> 15, of which waited for: 10 -> 10; matrix products, arithmetic and copies ran while one was open for 0% -> 0% of each run, Pallas kernels for 14% -> 16%
where the time goes in v7:
time: 63.2 us; the launch traced here: 62.9 us
  waiting for transfers between devices  21.5 us (34%)
  Pallas kernels  14.4 us (23%)
  starting transfers between devices  14.1 us (22%)
  blocking collectives  11.9 us (19%)
  between operations  0.96 us (2%)
    ppermute x15, waiting for transfers between devices, swapped(): return lax.ppermute(value, axis, [(i, i ^ k) for i in range(n)])  21.5 us
    ppermute x15, starting transfers between devices, swapped(): return lax.ppermute(value, axis, [(i, i ^ k) for i in range(n)])  14.1 us
    all_to_all x1, blocking collectives, body(): lax.all_to_all(jnp.broadcast_to(sizes, (n_ctx,) + sizes.shape), 'ctx', 0, 0)  11.9 us
    pallas_call x1, Pallas kernels, body(): call(functools.partial(scores_kernel, n_rows, heads_local), (shape((n_row...  5.61 us
    pallas_call x1, Pallas kernels, body(): call(functools.partial(logits_kernel, n_rows, index_local, (index_local *...  2.49 us
  transfers between devices with their start and end apart: 15, of which 10 were waited for; matrix products, arithmetic and copies ran while one was open for 0% of the time, Pallas kernels for 16%

profile of v7, /device:TPU:0, one launch (start us, length us, event | category | flops | bytes accessed | tf_op | source)
XLA Modules:
  0.0 62.9 jit_solution(1815818050998366628)
XLA Ops:
  0.6 2.5 %shard_map.77 = (f32[64,512]{1,0:T(8,128)S(1)}, f32[64,1024]{1,0:T(8,128)S(1)}, bf16[1024,128]{1,0:T(8,128)(2,1)S(1)}, bf16[1024,128]{1,0:T(8,128)(2,1)S(1)}, f3...) custom-call(s32[64]{0:T(128)} %pos_hbm.1, bf16[1024,128]{1,0:T(8,128)(2,1)} %bitcast.8, ...), custom_call_target="tpu_custom_call" | custom-call | flops 134217728 | bytes 1179648 | tf_op jit(solution)/shard_map/pallas_call | solution.py:369
  3.7 1.1 %shard_map.78 = (f32[64,512]{1,0:T(8,128)S(1)}, bf16[512,576]{1,0:T(8,128)(2,1)S(1)}) custom-call(f32[64,1024]{1,0:T(8,128)S(1)} %get-tuple-element.38.bias_ref, bf16[1024,128]{1,0:T(8,128)(2,1)S(1)} %get-tuple-element.39.iq_ref, bf16[1024,128]{1,0:T(8,128)(2,1)S(1)} %get-tuple-element.40.ik_ref, f32[1024,128]{1,0:T(8,128)S(1)} %get-tuple-element.41.w_ref, ...), custom_call_target="tpu_custom_call" | custom-call | flops 134217728 | bytes 2359296 | tf_op jit(solution)/shard_map/pallas_call | solution.py:408
  4.8 2.8 %collective-permute-start.1 = (f32[64,512]{1,0:T(8,128)S(1)}, f32[64,512]{1,0:T(8,128)S(1)}, u32[]{:S(2)}, u32[]{:S(2)}) collective-permute-start(f32[64,512]{1,0:T(8,128)S(1)} %add.21.mine_ref), channel_id=1, source_target_pairs={{0,2},{1,3},{2,0},{3,1},{4,6},{5,7},{6,4},{7,5},{8,10},{9,11},{10,... | collective-permute-start | bytes 393224 | tf_op jit(solution)/shard_map/ppermute | solution.py:366
  7.6 5.6 %shard_map.79 = (f32[2048,1024]{1,0:T(8,128)S(1)}, f32[32,128]{1,0:T(8,128)S(1)}) custom-call(s32[72]{0:T(128)S(1)} %get-tuple-element.44.order_ref, f32[64,1024]{1,0:T(8,128)S(1)} %get-tuple-element.38.bias_ref, bf16[512,576]{1,0:T(8,128)(2,1)S(1)} %get-tuple-element.45.q_ref, bf16[2048,576]{1,0:T(8,128)(2,1)} %bitcast.6, ...), custom_call_target="tpu_custom_call" | custom-call | flops 2415919104 | bytes 2359296 | tf_op jit(solution)/shard_map/pallas_call | solution.py:418
  13.5 11.9 %all_to_all.5.all_ref = f32[8,24,128]{2,1,0:T(8,128)S(1)} all-to-all(f32[8,24,128]{2,1,0:T(8,128)S(1)} %broadcast_in_dim.3), channel_id=1, replica_groups=mesh['ctx'=8,'heads'=4] {'ctx'}, dimensions={0} | all-to-all | bytes 196608 | tf_op jit(solution)/shard_map/all_to_all | solution.py:434
  26.8 0.8 %collective-permute-done.2.other_ref = f32[72,512]{1,0:T(8,128)S(1)} collective-permute-done((f32[72,512]{1,0:T(8,128)S(1)}, f32[72,512]{1,0:T(8,128)S(1)}, u32[]{:S(2)}, u32[]{:S(2)}) %collective-permute-start.2) | collective-permute-done | bytes 147488 | tf_op jit(solution)/shard_map/ppermute | solution.py:366
  27.6 0.9 %collective-permute-start.3 = (f32[64,512]{1,0:T(8,128)S(1)}, f32[64,512]{1,0:T(8,128)S(1)}, u32[]{:S(2)}, u32[]{:S(2)}) collective-permute-start(f32[64,512]{1,0:T(8,128)S(1)} %slice_add_fusion), channel_id=1, source_target_pairs={{0,2},{1,3},{2,0},{3,1},{4,6},{5,7},{6,4},{7,5},{8,10},{9,11},{10,... | collective-permute-start | bytes 393224 | tf_op jit(solution)/shard_map/ppermute | solution.py:366
  29.5 3.6 %collective-permute-done.3 = f32[64,512]{1,0:T(8,128)S(1)} collective-permute-done((f32[64,512]{1,0:T(8,128)S(1)}, f32[64,512]{1,0:T(8,128)S(1)}, u32[]{:S(2)}, u32[]{:S(2)}) %collective-permute-start.3) | collective-permute-done | bytes 131104 | tf_op jit(solution)/shard_map/ppermute | solution.py:366
  33.9 0.8 %collective-permute-done.4.g_ref = f32[64,512]{1,0:T(8,128)S(1)} collective-permute-done((f32[64,512]{1,0:T(8,128)S(1)}, f32[64,512]{1,0:T(8,128)S(1)}, u32[]{:S(2)}, u32[]{:S(2)}) %collective-permute-start.4) | collective-permute-done | bytes 131104 | tf_op jit(solution)/shard_map/ppermute | solution.py:366
  34.9 0.8 %collective-permute-start.7 = (f32[256,128]{1,0:T(8,128)S(1)}, f32[256,128]{1,0:T(8,128)S(1)}, u32[]{:S(2)}, u32[]{:S(2)}) collective-permute-start(f32[256,128]{1,0:T(8,128)S(1)} %get-tuple-element.65), channel_id=1, source_target_pairs={{0,12},{4,8},{8,4},{12,0},{16,28},{20,24},{24,20},{28,16},{1,13},{... | collective-permute-start | bytes 393224 | tf_op jit(solution)/shard_map/ppermute | solution.py:366
  35.9 1.1 %collective-permute-start.6 = (f32[256,128]{1,0:T(8,128)S(1)}, f32[256,128]{1,0:T(8,128)S(1)}, u32[]{:S(2)}, u32[]{:S(2)}) collective-permute-start(f32[256,128]{1,0:T(8,128)S(1)} %get-tuple-element.64), channel_id=1, source_target_pairs={{0,8},{4,12},{8,0},{12,4},{16,24},{20,28},{24,16},{28,20},{1,9},{5... | collective-permute-start | bytes 393224 | tf_op jit(solution)/shard_map/ppermute | solution.py:366
  37.3 1.8 %collective-permute-start.5 = (f32[256,128]{1,0:T(8,128)S(1)}, f32[256,128]{1,0:T(8,128)S(1)}, u32[]{:S(2)}, u32[]{:S(2)}) collective-permute-start(f32[256,128]{1,0:T(8,128)S(1)} %get-tuple-element.63), channel_id=1, source_target_pairs={{0,4},{4,0},{8,12},{12,8},{16,20},{20,16},{24,28},{28,24},{1,5},{5... | collective-permute-start | bytes 393224 | tf_op jit(solution)/shard_map/ppermute | solution.py:366
  39.3 2.9 %collective-permute-done.7 = f32[256,128]{1,0:T(8,128)S(1)} collective-permute-done((f32[256,128]{1,0:T(8,128)S(1)}, f32[256,128]{1,0:T(8,128)S(1)}, u32[]{:S(2)}, u32[]{:S(2)}) %collective-permute-start.7) | collective-permute-done | bytes 131104 | tf_op jit(solution)/shard_map/ppermute | solution.py:366
  42.2 0.8 %collective-permute-done.6 = f32[256,128]{1,0:T(8,128)S(1)} collective-permute-done((f32[256,128]{1,0:T(8,128)S(1)}, f32[256,128]{1,0:T(8,128)S(1)}, u32[]{:S(2)}, u32[]{:S(2)}) %collective-permute-start.6) | collective-permute-done | bytes 131104 | tf_op jit(solution)/shard_map/ppermute | solution.py:366
  43.1 1.2 %collective-permute-done.5 = f32[256,128]{1,0:T(8,128)S(1)} collective-permute-done((f32[256,128]{1,0:T(8,128)S(1)}, f32[256,128]{1,0:T(8,128)S(1)}, u32[]{:S(2)}, u32[]{:S(2)}) %collective-permute-start.5) | collective-permute-done | bytes 131104 | tf_op jit(solution)/shard_map/ppermute | solution.py:366
  45.0 0.9 %collective-permute-start.13 = (f32[256,128]{1,0:T(8,128)S(1)}, f32[256,128]{1,0:T(8,128)S(1)}, u32[]{:S(2)}, u32[]{:S(2)}) collective-permute-start(f32[256,128]{1,0:T(8,128)S(1)} %get-tuple-element.70), channel_id=1, source_target_pairs={{0,2},{1,3},{2,0},{3,1},{4,6},{5,7},{6,4},{7,5},{8,10},{9,11},{10,... | collective-permute-start | bytes 393224 | tf_op jit(solution)/shard_map/ppermute | solution.py:366
  46.0 0.9 %collective-permute-start.14 = (f32[256,128]{1,0:T(8,128)S(1)}, f32[256,128]{1,0:T(8,128)S(1)}, u32[]{:S(2)}, u32[]{:S(2)}) collective-permute-start(f32[256,128]{1,0:T(8,128)S(1)} %get-tuple-element.71), channel_id=1, source_target_pairs={{0,3},{1,2},{2,1},{3,0},{4,7},{5,6},{6,5},{7,4},{8,11},{9,10},{10,... | collective-permute-start | bytes 393224 | tf_op jit(solution)/shard_map/ppermute | solution.py:366
  46.9 5.5 %collective-permute-done.8 = f32[256,128]{1,0:T(8,128)S(1)} collective-permute-done((f32[256,128]{1,0:T(8,128)S(1)}, f32[256,128]{1,0:T(8,128)S(1)}, u32[]{:S(2)}, u32[]{:S(2)}) %collective-permute-start.8) | collective-permute-done | bytes 131104 | tf_op jit(solution)/shard_map/ppermute | solution.py:366
  52.4 1.0 %collective-permute-start.9 = (f32[256,128]{1,0:T(8,128)S(1)}, f32[256,128]{1,0:T(8,128)S(1)}, u32[]{:S(2)}, u32[]{:S(2)}) collective-permute-start(f32[256,128]{1,0:T(8,128)S(1)} %add.27.refs_0_), channel_id=1, source_target_pairs={{0,4},{4,0},{8,12},{12,8},{16,20},{20,16},{24,28},{28,24},{1,5},{5... | collective-permute-start | bytes 393224 | tf_op jit(solution)/shard_map/ppermute | solution.py:366
  53.4 2.6 %collective-permute-start.11 = (f32[256,128]{1,0:T(8,128)S(1)}, f32[256,128]{1,0:T(8,128)S(1)}, u32[]{:S(2)}, u32[]{:S(2)}) collective-permute-start(f32[256,128]{1,0:T(8,128)S(1)} %add.27.refs_0_), channel_id=1, source_target_pairs={{0,12},{4,8},{8,4},{12,0},{16,28},{20,24},{24,20},{28,16},{1,13},{... | collective-permute-start | bytes 393224 | tf_op jit(solution)/shard_map/ppermute | solution.py:366
  56.0 2.0 %collective-permute-done.9.refs_1_ = f32[256,128]{1,0:T(8,128)S(1)} collective-permute-done((f32[256,128]{1,0:T(8,128)S(1)}, f32[256,128]{1,0:T(8,128)S(1)}, u32[]{:S(2)}, u32[]{:S(2)}) %collective-permute-start.9) | collective-permute-done | bytes 131104 | tf_op jit(solution)/shard_map/ppermute | solution.py:366
  57.9 1.4 %collective-permute-done.10.refs_2_ = f32[256,128]{1,0:T(8,128)S(1)} collective-permute-done((f32[256,128]{1,0:T(8,128)S(1)}, f32[256,128]{1,0:T(8,128)S(1)}, u32[]{:S(2)}, u32[]{:S(2)}) %collective-permute-start.10) | collective-permute-done | bytes 131104 | tf_op jit(solution)/shard_map/ppermute | solution.py:366
  59.4 2.5 %collective-permute-done.11.refs_3_ = f32[256,128]{1,0:T(8,128)S(1)} collective-permute-done((f32[256,128]{1,0:T(8,128)S(1)}, f32[256,128]{1,0:T(8,128)S(1)}, u32[]{:S(2)}, u32[]{:S(2)}) %collective-permute-start.11) | collective-permute-done | bytes 131104 | tf_op jit(solution)/shard_map/ppermute | solution.py:366
  61.9 0.9 %shard_map.91 = (f32[1024,128]{1,0:T(8,128)}, f32[256,128]{1,0:T(8,128)}) custom-call(f32[256,128]{1,0:T(8,128)S(1)} %add.27.refs_0_, f32[256,128]{1,0:T(8,128)S(1)} %collective-permute-done.9.refs_1_, f32[256,128]{1,0:T(8,128)S(1)} %collective-permute-done.10.refs_2_, f32[256,128]{1,0:T(8,128)S(1)} %collective-permute-done.11.refs_3_, ...), custom_call_target="tpu_custom_call" | custom-call | tf_op jit(solution)/shard_map/pallas_call | solution.py:499
  (28 shorter events, 5.7 us)
Async XLA Ops:
  3.1 1.7 %collective-permute-start = (f32[64,512]{1,0:T(8,128)S(1)}, f32[64,512]{1,0:T(8,128)S(1)}, u32[]{:S(2)}, u32[]{:S(2)}) collective-permute-start(f32[64,512]{1,0:T(8,128)S(1)} %get-tuple-element.43), channel_id=1, source_target_pairs={{0,1},{1,0},{2,3},{3,2},{4,5},{5,4},{6,7},{7,6},{8,9},{9,8},{10,11... | collective-permute-start | bytes 393224 | tf_op jit(solution)/shard_map/ppermute | solution.py:366
  4.8 8.4 %collective-permute-start.1 = (f32[64,512]{1,0:T(8,128)S(1)}, f32[64,512]{1,0:T(8,128)S(1)}, u32[]{:S(2)}, u32[]{:S(2)}) collective-permute-start(f32[64,512]{1,0:T(8,128)S(1)} %add.21.mine_ref), channel_id=1, source_target_pairs={{0,2},{1,3},{2,0},{3,1},{4,6},{5,7},{6,4},{7,5},{8,10},{9,11},{10,... | collective-permute-start | bytes 393224 | tf_op jit(solution)/shard_map/ppermute | solution.py:366
  26.1 1.4 %collective-permute-start.2 = (f32[72,512]{1,0:T(8,128)S(1)}, f32[72,512]{1,0:T(8,128)S(1)}, u32[]{:S(2)}, u32[]{:S(2)}) collective-permute-start(f32[72,512]{1,0:T(8,128)S(1)} %get-tuple-element.51), channel_id=1, source_target_pairs={{0,1},{1,0},{2,3},{3,2},{4,5},{5,4},{6,7},{7,6},{8,9},{9,8},{10,11... | collective-permute-start | bytes 442376 | tf_op jit(solution)/shard_map/ppermute | solution.py:366
  27.6 5.6 %collective-permute-start.3 = (f32[64,512]{1,0:T(8,128)S(1)}, f32[64,512]{1,0:T(8,128)S(1)}, u32[]{:S(2)}, u32[]{:S(2)}) collective-permute-start(f32[64,512]{1,0:T(8,128)S(1)} %slice_add_fusion), channel_id=1, source_target_pairs={{0,2},{1,3},{2,0},{3,1},{4,6},{5,7},{6,4},{7,5},{8,10},{9,11},{10,... | collective-permute-start | bytes 393224 | tf_op jit(solution)/shard_map/ppermute | solution.py:366
  33.2 1.4 %collective-permute-start.4 = (f32[64,512]{1,0:T(8,128)S(1)}, f32[64,512]{1,0:T(8,128)S(1)}, u32[]{:S(2)}, u32[]{:S(2)}) collective-permute-start(f32[64,512]{1,0:T(8,128)S(1)} %subtract_multiply_fusion.g_ref), channel_id=1, source_target_pairs={{0,1},{1,0},{2,3},{3,2},{4,5},{5,4},{6,7},{7,6},{8,9},{9,8},{10,11... | collective-permute-start | bytes 393224 | tf_op jit(solution)/shard_map/ppermute | solution.py:366
  34.9 7.3 %collective-permute-start.7 = (f32[256,128]{1,0:T(8,128)S(1)}, f32[256,128]{1,0:T(8,128)S(1)}, u32[]{:S(2)}, u32[]{:S(2)}) collective-permute-start(f32[256,128]{1,0:T(8,128)S(1)} %get-tuple-element.65), channel_id=1, source_target_pairs={{0,12},{4,8},{8,4},{12,0},{16,28},{20,24},{24,20},{28,16},{1,13},{... | collective-permute-start | bytes 393224 | tf_op jit(solution)/shard_map/ppermute | solution.py:366
  35.9 7.1 %collective-permute-start.6 = (f32[256,128]{1,0:T(8,128)S(1)}, f32[256,128]{1,0:T(8,128)S(1)}, u32[]{:S(2)}, u32[]{:S(2)}) collective-permute-start(f32[256,128]{1,0:T(8,128)S(1)} %get-tuple-element.64), channel_id=1, source_target_pairs={{0,8},{4,12},{8,0},{12,4},{16,24},{20,28},{24,16},{28,20},{1,9},{5... | collective-permute-start | bytes 393224 | tf_op jit(solution)/shard_map/ppermute | solution.py:366
  37.3 6.9 %collective-permute-start.5 = (f32[256,128]{1,0:T(8,128)S(1)}, f32[256,128]{1,0:T(8,128)S(1)}, u32[]{:S(2)}, u32[]{:S(2)}) collective-permute-start(f32[256,128]{1,0:T(8,128)S(1)} %get-tuple-element.63), channel_id=1, source_target_pairs={{0,4},{4,0},{8,12},{12,8},{16,20},{20,16},{24,28},{28,24},{1,5},{5... | collective-permute-start | bytes 393224 | tf_op jit(solution)/shard_map/ppermute | solution.py:366
  44.2 8.1 %collective-permute-start.8 = (f32[256,128]{1,0:T(8,128)S(1)}, f32[256,128]{1,0:T(8,128)S(1)}, u32[]{:S(2)}, u32[]{:S(2)}) collective-permute-start(f32[256,128]{1,0:T(8,128)S(1)} %add_add_fusion), channel_id=1, source_target_pairs={{0,16},{4,20},{8,24},{12,28},{16,0},{20,4},{24,8},{28,12},{1,17},{... | collective-permute-start | bytes 393224 | tf_op jit(solution)/shard_map/ppermute | solution.py:366
  45.0 8.4 %collective-permute-start.12 = (f32[256,128]{1,0:T(8,128)S(1)}, f32[256,128]{1,0:T(8,128)S(1)}, u32[]{:S(2)}, u32[]{:S(2)}) collective-permute-start(f32[256,128]{1,0:T(8,128)S(1)} %get-tuple-element.69), channel_id=1, source_target_pairs={{0,1},{1,0},{2,3},{3,2},{4,5},{5,4},{6,7},{7,6},{8,9},{9,8},{10,11... | collective-permute-start | bytes 393224 | tf_op jit(solution)/shard_map/ppermute | solution.py:366
  45.0 10.9 %collective-permute-start.13 = (f32[256,128]{1,0:T(8,128)S(1)}, f32[256,128]{1,0:T(8,128)S(1)}, u32[]{:S(2)}, u32[]{:S(2)}) collective-permute-start(f32[256,128]{1,0:T(8,128)S(1)} %get-tuple-element.70), channel_id=1, source_target_pairs={{0,2},{1,3},{2,0},{3,1},{4,6},{5,7},{6,4},{7,5},{8,10},{9,11},{10,... | collective-permute-start | bytes 393224 | tf_op jit(solution)/shard_map/ppermute | solution.py:366
  46.0 10.0 %collective-permute-start.14 = (f32[256,128]{1,0:T(8,128)S(1)}, f32[256,128]{1,0:T(8,128)S(1)}, u32[]{:S(2)}, u32[]{:S(2)}) collective-permute-start(f32[256,128]{1,0:T(8,128)S(1)} %get-tuple-element.71), channel_id=1, source_target_pairs={{0,3},{1,2},{2,1},{3,0},{4,7},{5,6},{6,5},{7,4},{8,11},{9,10},{10,... | collective-permute-start | bytes 393224 | tf_op jit(solution)/shard_map/ppermute | solution.py:366
  52.4 5.5 %collective-permute-start.9 = (f32[256,128]{1,0:T(8,128)S(1)}, f32[256,128]{1,0:T(8,128)S(1)}, u32[]{:S(2)}, u32[]{:S(2)}) collective-permute-start(f32[256,128]{1,0:T(8,128)S(1)} %add.27.refs_0_), channel_id=1, source_target_pairs={{0,4},{4,0},{8,12},{12,8},{16,20},{20,16},{24,28},{28,24},{1,5},{5... | collective-permute-start | bytes 393224 | tf_op jit(solution)/shard_map/ppermute | solution.py:366
  53.4 6.0 %collective-permute-start.10 = (f32[256,128]{1,0:T(8,128)S(1)}, f32[256,128]{1,0:T(8,128)S(1)}, u32[]{:S(2)}, u32[]{:S(2)}) collective-permute-start(f32[256,128]{1,0:T(8,128)S(1)} %add.27.refs_0_), channel_id=1, source_target_pairs={{0,8},{4,12},{8,0},{12,4},{16,24},{20,28},{24,16},{28,20},{1,9},{5... | collective-permute-start | bytes 393224 | tf_op jit(solution)/shard_map/ppermute | solution.py:366
  53.4 8.5 %collective-permute-start.11 = (f32[256,128]{1,0:T(8,128)S(1)}, f32[256,128]{1,0:T(8,128)S(1)}, u32[]{:S(2)}, u32[]{:S(2)}) collective-permute-start(f32[256,128]{1,0:T(8,128)S(1)} %add.27.refs_0_), channel_id=1, source_target_pairs={{0,12},{4,8},{8,4},{12,0},{16,28},{20,24},{24,20},{28,16},{1,13},{... | collective-permute-start | bytes 393224 | tf_op jit(solution)/shard_map/ppermute | solution.py:366

commit v8 on v7

--- a/solution.py
+++ b/solution.py
@@ -80,14 +80,13 @@
         copy.start()
     copies[0].wait()
     start = lax.axis_index("ctx") * 2 * half
+    for row in range(n_rows):
+        rows_ref[row] = 0
     count = jnp.int32(0)
-    for seen in (True, False):
-        for row in range(n_rows):
-            rows_ref[count] = row
-            count += ((pos_ref[row] >= start) == seen).astype(jnp.int32)
-        if seen:
-            visible = count
-    rows_ref[n_rows + 1] = visible
+    for row in range(n_rows):
+        rows_ref[count] = row
+        count += (pos_ref[row] >= start).astype(jnp.int32)
+    rows_ref[n_rows + 1] = count
     place = start + lax.broadcasted_iota(jnp.int32, (8, 2 * half), 1)
     sublane = lax.broadcasted_iota(jnp.int32, (8, 1), 0)
     for first in range(0, n_rows, 8):
@@ -167,6 +166,9 @@
         copies[1].wait()
 
     def some_rows(n_blocks):
+        for row in range(n_rows):
+            at = slice(row * n_heads, (row + 1) * n_heads)
+            p_ref[at, :] = jnp.zeros((n_heads, p_ref.shape[1]), F32)
         for copy in copies:
             copy.wait()
         stats = jnp.where(lane < n_rows, NEG, 1.0)
@@ -186,8 +188,6 @@
                 row = order_ref[b * per + i]
                 top, total = finish(b, i, bias_ref[pl.ds(row, 1), :], place(row))
                 stats = jnp.where(lane == row, top, jnp.where(lane == row + n_rows, total, stats))
-        for i in range(n_blocks * per, n_rows):
-            p_ref[place(order_ref[i]), :] = jnp.zeros((n_heads, p_ref.shape[1]), F32)
         stat_ref[...] = stats
 
     needed = (order_ref[n_rows + 1] + per - 1) // per
@@ -404,7 +404,7 @@
     flat_queries = pltpu.with_memory_space_constraint(
         queries.reshape(n_rows * heads_local, width), pltpu.HBM
     )
-    ready = n_rows * heads_local // 4
+    ready = n_rows * heads_local // 2
     keep, q = call(
         functools.partial(kept_logits_kernel, n_rows, index_local),
         (shape((n_rows, half), F32), shape((ready, width), BF16)),

time: 63.2 us -> 62.6 us (level)
  waiting for transfers between devices: 21.5 us -> 20.8 us
    ppermute x15, waiting for transfers between devices: 21.5 us -> 20.8 us  [swapped(): return lax.ppermute(value, axis, [(i, i ^ k) for i in range(n)])]
where the time goes in v8:
time: 62.6 us; the launch traced here: 62.4 us
  waiting for transfers between devices  20.8 us (33%)
  starting transfers between devices  14.5 us (23%)
  Pallas kernels  14.1 us (23%)
  blocking collectives  11.8 us (19%)
  between operations  0.96 us (2%)
    ppermute x15, waiting for transfers between devices, swapped(): return lax.ppermute(value, axis, [(i, i ^ k) for i in range(n)])  20.8 us
    ppermute x15, starting transfers between devices, swapped(): return lax.ppermute(value, axis, [(i, i ^ k) for i in range(n)])  14.5 us
    all_to_all x1, blocking collectives, body(): lax.all_to_all(jnp.broadcast_to(sizes, (n_ctx,) + sizes.shape), 'ctx', 0, 0)  11.8 us
    pallas_call x1, Pallas kernels, body(): call(functools.partial(scores_kernel, n_rows, heads_local), (shape((n_row...  5.25 us
    pallas_call x1, Pallas kernels, body(): call(functools.partial(logits_kernel, n_rows, index_local, (index_local *...  2.36 us
    pallas_call x1, Pallas kernels, body(): call(functools.partial(kept_logits_kernel, n_rows, index_local), (shape((...  1.33 us
  transfers between devices with their start and end apart: 15, of which 10 were waited for; matrix products, arithmetic and copies ran while one was open for 0% of the time, Pallas kernels for 16%

profile of v8, /device:TPU:0, one launch (start us, length us, event | category | flops | bytes accessed | tf_op | source)
XLA Modules:
  0.0 62.4 jit_solution(10090767299100740204)
XLA Ops:
  0.6 2.4 %shard_map.77 = (f32[64,512]{1,0:T(8,128)S(1)}, f32[64,1024]{1,0:T(8,128)S(1)}, bf16[1024,128]{1,0:T(8,128)(2,1)S(1)}, bf16[1024,128]{1,0:T(8,128)(2,1)S(1)}, f3...) custom-call(s32[64]{0:T(128)} %pos_hbm.1, bf16[1024,128]{1,0:T(8,128)(2,1)} %bitcast.8, ...), custom_call_target="tpu_custom_call" | custom-call | flops 134217728 | bytes 1179648 | tf_op jit(solution)/shard_map/pallas_call | solution.py:369
  3.6 1.3 %shard_map.78 = (f32[64,512]{1,0:T(8,128)S(1)}, bf16[1024,576]{1,0:T(8,128)(2,1)S(1)}) custom-call(f32[64,1024]{1,0:T(8,128)S(1)} %get-tuple-element.38.bias_ref, bf16[1024,128]{1,0:T(8,128)(2,1)S(1)} %get-tuple-element.39.iq_ref, bf16[1024,128]{1,0:T(8,128)(2,1)S(1)} %get-tuple-element.40.ik_ref, f32[1024,128]{1,0:T(8,128)S(1)} %get-tuple-element.41.w_ref, ...), custom_call_target="tpu_custom_call" | custom-call | flops 134217728 | bytes 2359296 | tf_op jit(solution)/shard_map/pallas_call | solution.py:408
  4.9 2.6 %collective-permute-start.1 = (f32[64,512]{1,0:T(8,128)S(1)}, f32[64,512]{1,0:T(8,128)S(1)}, u32[]{:S(2)}, u32[]{:S(2)}) collective-permute-start(f32[64,512]{1,0:T(8,128)S(1)} %add.21.mine_ref), channel_id=1, source_target_pairs={{0,2},{1,3},{2,0},{3,1},{4,6},{5,7},{6,4},{7,5},{8,10},{9,11},{10,... | collective-permute-start | bytes 393224 | tf_op jit(solution)/shard_map/ppermute | solution.py:366
  7.5 5.3 %shard_map.79 = (f32[2048,1024]{1,0:T(8,128)S(1)}, f32[32,128]{1,0:T(8,128)S(1)}) custom-call(s32[72]{0:T(128)S(1)} %get-tuple-element.44.order_ref, f32[64,1024]{1,0:T(8,128)S(1)} %get-tuple-element.38.bias_ref, bf16[1024,576]{1,0:T(8,128)(2,1)S(1)} %get-tuple-element.45.q_ref, bf16[2048,576]{1,0:T(8,128)(2,1)} %bitcast.6, ...), custom_call_target="tpu_custom_call" | custom-call | flops 2415919104 | bytes 2359296 | tf_op jit(solution)/shard_map/pallas_call | solution.py:418
  13.0 11.8 %all_to_all.5.all_ref = f32[8,24,128]{2,1,0:T(8,128)S(1)} all-to-all(f32[8,24,128]{2,1,0:T(8,128)S(1)} %broadcast_in_dim.3), channel_id=1, replica_groups=mesh['ctx'=8,'heads'=4] {'ctx'}, dimensions={0} | all-to-all | bytes 196608 | tf_op jit(solution)/shard_map/all_to_all | solution.py:434
  26.2 0.8 %collective-permute-done.2.other_ref = f32[72,512]{1,0:T(8,128)S(1)} collective-permute-done((f32[72,512]{1,0:T(8,128)S(1)}, f32[72,512]{1,0:T(8,128)S(1)}, u32[]{:S(2)}, u32[]{:S(2)}) %collective-permute-start.2) | collective-permute-done | bytes 147488 | tf_op jit(solution)/shard_map/ppermute | solution.py:366
  27.0 1.6 %collective-permute-start.3 = (f32[64,512]{1,0:T(8,128)S(1)}, f32[64,512]{1,0:T(8,128)S(1)}, u32[]{:S(2)}, u32[]{:S(2)}) collective-permute-start(f32[64,512]{1,0:T(8,128)S(1)} %slice_add_fusion), channel_id=1, source_target_pairs={{0,2},{1,3},{2,0},{3,1},{4,6},{5,7},{6,4},{7,5},{8,10},{9,11},{10,... | collective-permute-start | bytes 393224 | tf_op jit(solution)/shard_map/ppermute | solution.py:366
  28.6 0.7 %shard_map.84 = (f32[1024,1024]{1,0:T(8,128)S(1)}, bf16[128,1024]{1,0:T(8,128)(2,1)S(1)}) custom-call(bf16[1024,128]{1,0:T(8,128)(2,1)S(1)} %get-tuple-element.39.iq_ref, bf16[1024,128]{1,0:T(8,128)(2,1)S(1)} %get-tuple-element.40.ik_ref, f32[1024,128]{1,0:T(8,128)S(1)} %get-tuple-element.41.w_ref), custom_call_target="tpu_custom_call" | custom-call | flops 268435456 | tf_op jit(solution)/shard_map/pallas_call | solution.py:455
  29.6 3.0 %collective-permute-done.3 = f32[64,512]{1,0:T(8,128)S(1)} collective-permute-done((f32[64,512]{1,0:T(8,128)S(1)}, f32[64,512]{1,0:T(8,128)S(1)}, u32[]{:S(2)}, u32[]{:S(2)}) %collective-permute-start.3) | collective-permute-done | bytes 131104 | tf_op jit(solution)/shard_map/ppermute | solution.py:366
  33.3 0.8 %collective-permute-done.4.g_ref = f32[64,512]{1,0:T(8,128)S(1)} collective-permute-done((f32[64,512]{1,0:T(8,128)S(1)}, f32[64,512]{1,0:T(8,128)S(1)}, u32[]{:S(2)}, u32[]{:S(2)}) %collective-permute-start.4) | collective-permute-done | bytes 131104 | tf_op jit(solution)/shard_map/ppermute | solution.py:366
  34.3 0.8 %collective-permute-start.7 = (f32[256,128]{1,0:T(8,128)S(1)}, f32[256,128]{1,0:T(8,128)S(1)}, u32[]{:S(2)}, u32[]{:S(2)}) collective-permute-start(f32[256,128]{1,0:T(8,128)S(1)} %get-tuple-element.65), channel_id=1, source_target_pairs={{0,12},{4,8},{8,4},{12,0},{16,28},{20,24},{24,20},{28,16},{1,13},{... | collective-permute-start | bytes 393224 | tf_op jit(solution)/shard_map/ppermute | solution.py:366
  35.3 1.1 %collective-permute-start.6 = (f32[256,128]{1,0:T(8,128)S(1)}, f32[256,128]{1,0:T(8,128)S(1)}, u32[]{:S(2)}, u32[]{:S(2)}) collective-permute-start(f32[256,128]{1,0:T(8,128)S(1)} %get-tuple-element.64), channel_id=1, source_target_pairs={{0,8},{4,12},{8,0},{12,4},{16,24},{20,28},{24,16},{28,20},{1,9},{5... | collective-permute-start | bytes 393224 | tf_op jit(solution)/shard_map/ppermute | solution.py:366
  36.7 1.8 %collective-permute-start.5 = (f32[256,128]{1,0:T(8,128)S(1)}, f32[256,128]{1,0:T(8,128)S(1)}, u32[]{:S(2)}, u32[]{:S(2)}) collective-permute-start(f32[256,128]{1,0:T(8,128)S(1)} %get-tuple-element.63), channel_id=1, source_target_pairs={{0,4},{4,0},{8,12},{12,8},{16,20},{20,16},{24,28},{28,24},{1,5},{5... | collective-permute-start | bytes 393224 | tf_op jit(solution)/shard_map/ppermute | solution.py:366
  38.8 2.9 %collective-permute-done.7 = f32[256,128]{1,0:T(8,128)S(1)} collective-permute-done((f32[256,128]{1,0:T(8,128)S(1)}, f32[256,128]{1,0:T(8,128)S(1)}, u32[]{:S(2)}, u32[]{:S(2)}) %collective-permute-start.7) | collective-permute-done | bytes 131104 | tf_op jit(solution)/shard_map/ppermute | solution.py:366
  41.7 0.8 %collective-permute-done.6 = f32[256,128]{1,0:T(8,128)S(1)} collective-permute-done((f32[256,128]{1,0:T(8,128)S(1)}, f32[256,128]{1,0:T(8,128)S(1)}, u32[]{:S(2)}, u32[]{:S(2)}) %collective-permute-start.6) | collective-permute-done | bytes 131104 | tf_op jit(solution)/shard_map/ppermute | solution.py:366
  42.5 1.2 %collective-permute-done.5 = f32[256,128]{1,0:T(8,128)S(1)} collective-permute-done((f32[256,128]{1,0:T(8,128)S(1)}, f32[256,128]{1,0:T(8,128)S(1)}, u32[]{:S(2)}, u32[]{:S(2)}) %collective-permute-start.5) | collective-permute-done | bytes 131104 | tf_op jit(solution)/shard_map/ppermute | solution.py:366
  44.5 1.6 %collective-permute-start.13 = (f32[256,128]{1,0:T(8,128)S(1)}, f32[256,128]{1,0:T(8,128)S(1)}, u32[]{:S(2)}, u32[]{:S(2)}) collective-permute-start(f32[256,128]{1,0:T(8,128)S(1)} %get-tuple-element.70), channel_id=1, source_target_pairs={{0,2},{1,3},{2,0},{3,1},{4,6},{5,7},{6,4},{7,5},{8,10},{9,11},{10,... | collective-permute-start | bytes 393224 | tf_op jit(solution)/shard_map/ppermute | solution.py:366
  46.3 5.5 %collective-permute-done.8 = f32[256,128]{1,0:T(8,128)S(1)} collective-permute-done((f32[256,128]{1,0:T(8,128)S(1)}, f32[256,128]{1,0:T(8,128)S(1)}, u32[]{:S(2)}, u32[]{:S(2)}) %collective-permute-start.8) | collective-permute-done | bytes 131104 | tf_op jit(solution)/shard_map/ppermute | solution.py:366
  51.9 0.9 %collective-permute-start.9 = (f32[256,128]{1,0:T(8,128)S(1)}, f32[256,128]{1,0:T(8,128)S(1)}, u32[]{:S(2)}, u32[]{:S(2)}) collective-permute-start(f32[256,128]{1,0:T(8,128)S(1)} %add.27.refs_0_), channel_id=1, source_target_pairs={{0,4},{4,0},{8,12},{12,8},{16,20},{20,16},{24,28},{28,24},{1,5},{5... | collective-permute-start | bytes 393224 | tf_op jit(solution)/shard_map/ppermute | solution.py:366
  52.8 2.6 %collective-permute-start.11 = (f32[256,128]{1,0:T(8,128)S(1)}, f32[256,128]{1,0:T(8,128)S(1)}, u32[]{:S(2)}, u32[]{:S(2)}) collective-permute-start(f32[256,128]{1,0:T(8,128)S(1)} %add.27.refs_0_), channel_id=1, source_target_pairs={{0,12},{4,8},{8,4},{12,0},{16,28},{20,24},{24,20},{28,16},{1,13},{... | collective-permute-start | bytes 393224 | tf_op jit(solution)/shard_map/ppermute | solution.py:366
  55.4 2.0 %collective-permute-done.9.refs_1_ = f32[256,128]{1,0:T(8,128)S(1)} collective-permute-done((f32[256,128]{1,0:T(8,128)S(1)}, f32[256,128]{1,0:T(8,128)S(1)}, u32[]{:S(2)}, u32[]{:S(2)}) %collective-permute-start.9) | collective-permute-done | bytes 131104 | tf_op jit(solution)/shard_map/ppermute | solution.py:366
  57.4 1.4 %collective-permute-done.10.refs_2_ = f32[256,128]{1,0:T(8,128)S(1)} collective-permute-done((f32[256,128]{1,0:T(8,128)S(1)}, f32[256,128]{1,0:T(8,128)S(1)}, u32[]{:S(2)}, u32[]{:S(2)}) %collective-permute-start.10) | collective-permute-done | bytes 131104 | tf_op jit(solution)/shard_map/ppermute | solution.py:366
  58.8 2.5 %collective-permute-done.11.refs_3_ = f32[256,128]{1,0:T(8,128)S(1)} collective-permute-done((f32[256,128]{1,0:T(8,128)S(1)}, f32[256,128]{1,0:T(8,128)S(1)}, u32[]{:S(2)}, u32[]{:S(2)}) %collective-permute-start.11) | collective-permute-done | bytes 131104 | tf_op jit(solution)/shard_map/ppermute | solution.py:366
  61.3 0.9 %shard_map.91 = (f32[1024,128]{1,0:T(8,128)}, f32[256,128]{1,0:T(8,128)}) custom-call(f32[256,128]{1,0:T(8,128)S(1)} %add.27.refs_0_, f32[256,128]{1,0:T(8,128)S(1)} %collective-permute-done.9.refs_1_, f32[256,128]{1,0:T(8,128)S(1)} %collective-permute-done.10.refs_2_, f32[256,128]{1,0:T(8,128)S(1)} %collective-permute-done.11.refs_3_, ...), custom_call_target="tpu_custom_call" | custom-call | tf_op jit(solution)/shard_map/pallas_call | solution.py:499
  (28 shorter events, 5.2 us)
Async XLA Ops:
  3.0 1.9 %collective-permute-start = (f32[64,512]{1,0:T(8,128)S(1)}, f32[64,512]{1,0:T(8,128)S(1)}, u32[]{:S(2)}, u32[]{:S(2)}) collective-permute-start(f32[64,512]{1,0:T(8,128)S(1)} %get-tuple-element.43), channel_id=1, source_target_pairs={{0,1},{1,0},{2,3},{3,2},{4,5},{5,4},{6,7},{7,6},{8,9},{9,8},{10,11... | collective-permute-start | bytes 393224 | tf_op jit(solution)/shard_map/ppermute | solution.py:366
  4.9 7.8 %collective-permute-start.1 = (f32[64,512]{1,0:T(8,128)S(1)}, f32[64,512]{1,0:T(8,128)S(1)}, u32[]{:S(2)}, u32[]{:S(2)}) collective-permute-start(f32[64,512]{1,0:T(8,128)S(1)} %add.21.mine_ref), channel_id=1, source_target_pairs={{0,2},{1,3},{2,0},{3,1},{4,6},{5,7},{6,4},{7,5},{8,10},{9,11},{10,... | collective-permute-start | bytes 393224 | tf_op jit(solution)/shard_map/ppermute | solution.py:366
  25.6 1.4 %collective-permute-start.2 = (f32[72,512]{1,0:T(8,128)S(1)}, f32[72,512]{1,0:T(8,128)S(1)}, u32[]{:S(2)}, u32[]{:S(2)}) collective-permute-start(f32[72,512]{1,0:T(8,128)S(1)} %get-tuple-element.51), channel_id=1, source_target_pairs={{0,1},{1,0},{2,3},{3,2},{4,5},{5,4},{6,7},{7,6},{8,9},{9,8},{10,11... | collective-permute-start | bytes 442376 | tf_op jit(solution)/shard_map/ppermute | solution.py:366
  27.0 5.6 %collective-permute-start.3 = (f32[64,512]{1,0:T(8,128)S(1)}, f32[64,512]{1,0:T(8,128)S(1)}, u32[]{:S(2)}, u32[]{:S(2)}) collective-permute-start(f32[64,512]{1,0:T(8,128)S(1)} %slice_add_fusion), channel_id=1, source_target_pairs={{0,2},{1,3},{2,0},{3,1},{4,6},{5,7},{6,4},{7,5},{8,10},{9,11},{10,... | collective-permute-start | bytes 393224 | tf_op jit(solution)/shard_map/ppermute | solution.py:366
  32.7 1.4 %collective-permute-start.4 = (f32[64,512]{1,0:T(8,128)S(1)}, f32[64,512]{1,0:T(8,128)S(1)}, u32[]{:S(2)}, u32[]{:S(2)}) collective-permute-start(f32[64,512]{1,0:T(8,128)S(1)} %subtract_multiply_fusion.g_ref), channel_id=1, source_target_pairs={{0,1},{1,0},{2,3},{3,2},{4,5},{5,4},{6,7},{7,6},{8,9},{9,8},{10,11... | collective-permute-start | bytes 393224 | tf_op jit(solution)/shard_map/ppermute | solution.py:366
  34.3 7.3 %collective-permute-start.7 = (f32[256,128]{1,0:T(8,128)S(1)}, f32[256,128]{1,0:T(8,128)S(1)}, u32[]{:S(2)}, u32[]{:S(2)}) collective-permute-start(f32[256,128]{1,0:T(8,128)S(1)} %get-tuple-element.65), channel_id=1, source_target_pairs={{0,12},{4,8},{8,4},{12,0},{16,28},{20,24},{24,20},{28,16},{1,13},{... | collective-permute-start | bytes 393224 | tf_op jit(solution)/shard_map/ppermute | solution.py:366
  35.3 7.2 %collective-permute-start.6 = (f32[256,128]{1,0:T(8,128)S(1)}, f32[256,128]{1,0:T(8,128)S(1)}, u32[]{:S(2)}, u32[]{:S(2)}) collective-permute-start(f32[256,128]{1,0:T(8,128)S(1)} %get-tuple-element.64), channel_id=1, source_target_pairs={{0,8},{4,12},{8,0},{12,4},{16,24},{20,28},{24,16},{28,20},{1,9},{5... | collective-permute-start | bytes 393224 | tf_op jit(solution)/shard_map/ppermute | solution.py:366
  36.7 6.9 %collective-permute-start.5 = (f32[256,128]{1,0:T(8,128)S(1)}, f32[256,128]{1,0:T(8,128)S(1)}, u32[]{:S(2)}, u32[]{:S(2)}) collective-permute-start(f32[256,128]{1,0:T(8,128)S(1)} %get-tuple-element.63), channel_id=1, source_target_pairs={{0,4},{4,0},{8,12},{12,8},{16,20},{20,16},{24,28},{28,24},{1,5},{5... | collective-permute-start | bytes 393224 | tf_op jit(solution)/shard_map/ppermute | solution.py:366
  43.7 8.2 %collective-permute-start.8 = (f32[256,128]{1,0:T(8,128)S(1)}, f32[256,128]{1,0:T(8,128)S(1)}, u32[]{:S(2)}, u32[]{:S(2)}) collective-permute-start(f32[256,128]{1,0:T(8,128)S(1)} %add_add_fusion), channel_id=1, source_target_pairs={{0,16},{4,20},{8,24},{12,28},{16,0},{20,4},{24,8},{28,12},{1,17},{... | collective-permute-start | bytes 393224 | tf_op jit(solution)/shard_map/ppermute | solution.py:366
  44.4 8.4 %collective-permute-start.12 = (f32[256,128]{1,0:T(8,128)S(1)}, f32[256,128]{1,0:T(8,128)S(1)}, u32[]{:S(2)}, u32[]{:S(2)}) collective-permute-start(f32[256,128]{1,0:T(8,128)S(1)} %get-tuple-element.69), channel_id=1, source_target_pairs={{0,1},{1,0},{2,3},{3,2},{4,5},{5,4},{6,7},{7,6},{8,9},{9,8},{10,11... | collective-permute-start | bytes 393224 | tf_op jit(solution)/shard_map/ppermute | solution.py:366
  44.5 10.9 %collective-permute-start.13 = (f32[256,128]{1,0:T(8,128)S(1)}, f32[256,128]{1,0:T(8,128)S(1)}, u32[]{:S(2)}, u32[]{:S(2)}) collective-permute-start(f32[256,128]{1,0:T(8,128)S(1)} %get-tuple-element.70), channel_id=1, source_target_pairs={{0,2},{1,3},{2,0},{3,1},{4,6},{5,7},{6,4},{7,5},{8,10},{9,11},{10,... | collective-permute-start | bytes 393224 | tf_op jit(solution)/shard_map/ppermute | solution.py:366
  46.1 9.3 %collective-permute-start.14 = (f32[256,128]{1,0:T(8,128)S(1)}, f32[256,128]{1,0:T(8,128)S(1)}, u32[]{:S(2)}, u32[]{:S(2)}) collective-permute-start(f32[256,128]{1,0:T(8,128)S(1)} %get-tuple-element.71), channel_id=1, source_target_pairs={{0,3},{1,2},{2,1},{3,0},{4,7},{5,6},{6,5},{7,4},{8,11},{9,10},{10,... | collective-permute-start | bytes 393224 | tf_op jit(solution)/shard_map/ppermute | solution.py:366
  51.9 5.5 %collective-permute-start.9 = (f32[256,128]{1,0:T(8,128)S(1)}, f32[256,128]{1,0:T(8,128)S(1)}, u32[]{:S(2)}, u32[]{:S(2)}) collective-permute-start(f32[256,128]{1,0:T(8,128)S(1)} %add.27.refs_0_), channel_id=1, source_target_pairs={{0,4},{4,0},{8,12},{12,8},{16,20},{20,16},{24,28},{28,24},{1,5},{5... | collective-permute-start | bytes 393224 | tf_op jit(solution)/shard_map/ppermute | solution.py:366
  52.8 6.0 %collective-permute-start.10 = (f32[256,128]{1,0:T(8,128)S(1)}, f32[256,128]{1,0:T(8,128)S(1)}, u32[]{:S(2)}, u32[]{:S(2)}) collective-permute-start(f32[256,128]{1,0:T(8,128)S(1)} %add.27.refs_0_), channel_id=1, source_target_pairs={{0,8},{4,12},{8,0},{12,4},{16,24},{20,28},{24,16},{28,20},{1,9},{5... | collective-permute-start | bytes 393224 | tf_op jit(solution)/shard_map/ppermute | solution.py:366
  52.8 8.5 %collective-permute-start.11 = (f32[256,128]{1,0:T(8,128)S(1)}, f32[256,128]{1,0:T(8,128)S(1)}, u32[]{:S(2)}, u32[]{:S(2)}) collective-permute-start(f32[256,128]{1,0:T(8,128)S(1)} %add.27.refs_0_), channel_id=1, source_target_pairs={{0,12},{4,8},{8,4},{12,0},{16,28},{20,24},{24,20},{28,16},{1,13},{... | collective-permute-start | bytes 393224 | tf_op jit(solution)/shard_map/ppermute | solution.py:366

commit v9 on v6

--- a/solution.py
+++ b/solution.py
@@ -48,9 +48,8 @@
         )
         for i in range(per):
             row = b * per + i
-            at = slice(row * n_heads, (row + 1) * n_heads)
             out_ref[row : row + 1, :] = jnp.sum(
-                jnp.maximum(dots[i * n_heads : (i + 1) * n_heads, :], 0.0) * w_ref[at, 0:1],
+                jnp.maximum(dots[i * n_heads : (i + 1) * n_heads, :], 0.0) * w_ref[:, row : row + 1],
                 axis=0,
                 keepdims=True,
             )
@@ -86,10 +85,7 @@
             pos = jnp.where(sublane == i, pos_ref[first + i], pos)
         bias_ref[first : first + 8, :] = jnp.where(place <= pos, 0.0, NEG)
     copies[1].wait()
-    for row in range(n_rows):
-        w_ref[row * n_heads : (row + 1) * n_heads, :] = jnp.broadcast_to(
-            iw_ref[:, row : row + 1] * scale, (n_heads, LANES)
-        )
+    w_ref[...] = iw_ref[...] * scale
     copies[2].wait()
     copies[3].wait()
     core = lax.axis_index("heads") & 1
@@ -128,10 +124,8 @@
         ]
         held[...] = jnp.dot(source, lat_ref[...], preferred_element_type=F32)
 
-    dots(0)
     for b in range(blocks):
-        if b + 1 < blocks:
-            dots(b + 1)
+        dots(b)
         held = s_even if b % 2 == 0 else s_odd
         for i in range(block // n_heads):
             row = b * (block // n_heads) + i
@@ -216,10 +210,15 @@
 
 def mask_kernel(iq_ref, ik_ref, w_ref, wm_ref, iqt_ref):
     rows = 256
+    n_heads = w_ref.shape[0]
     for b in range(iq_ref.shape[0] // rows):
         at = slice(b * rows, (b + 1) * rows)
         dots = lax.dot_general(iq_ref[at, :], ik_ref[...], CONTRACT_LAST, preferred_element_type=F32)
-        wm_ref[at, :] = jnp.where(dots > 0.0, w_ref[at, 0:1], 0.0)
+        for i in range(rows // n_heads):
+            row, part = b * (rows // n_heads) + i, slice(i * n_heads, (i + 1) * n_heads)
+            wm_ref[b * rows + i * n_heads : b * rows + (i + 1) * n_heads, :] = jnp.where(
+                dots[part, :] > 0.0, w_ref[:, row : row + 1], 0.0
+            )
         iqt_ref[:, at] = jnp.transpose(iq_ref[at, :])
 
 
@@ -319,7 +318,7 @@
             shape((n_rows, keys), F32),
             shape(flat, BF16),
             shape((keys, depth), BF16),
-            shape((flat[0], LANES), F32),
+            shape((index_local, n_rows), F32),
             shape((width, keys), BF16),
         ),
         [HBM] * 5,
@@ -346,7 +345,7 @@
     flat_queries = pltpu.with_memory_space_constraint(
         queries.reshape(n_rows * heads_local, width), pltpu.HBM
     )
-    ready = n_rows * heads_local // 2
+    ready = n_rows * heads_local // 8 * 3
     keep, q = call(
         functools.partial(kept_logits_kernel, n_rows, index_local),
         (shape((n_rows, half), F32), shape((ready, width), BF16)),

time: 61.7 us -> 61.8 us (level)
  no operation moved by 1% of the time
where the time goes in v9:
time: 61.8 us; the launch traced here: 61.6 us
  waiting for transfers between devices  21 us (34%)
  starting transfers between devices  14.4 us (23%)
  blocking collectives  12.7 us (21%)
  Pallas kernels  12.5 us (20%)
  between operations  0.8 us (1%)
    ppermute x15, waiting for transfers between devices, swapped(): return lax.ppermute(value, axis, [(i, i ^ k) for i in range(n)])  21 us
    ppermute x15, starting transfers between devices, swapped(): return lax.ppermute(value, axis, [(i, i ^ k) for i in range(n)])  14.4 us
    all_to_all x1, blocking collectives, body(): lax.all_to_all(jnp.broadcast_to(sizes, (n_ctx,) + sizes.shape), 'ctx', 0, 0)  12.7 us
    pallas_call x1, Pallas kernels, body(): call(functools.partial(scores_kernel, n_rows, heads_local), (shape((n_row...  4.47 us
    pallas_call x1, Pallas kernels, body(): call(functools.partial(logits_kernel, n_rows, index_local, (index_local *...  1.7 us
  transfers between devices with their start and end apart: 15, of which 10 were waited for; matrix products, arithmetic and copies ran while one was open for 0% of the time, Pallas kernels for 14%

profile of v9, /device:TPU:0, one launch (start us, length us, event | category | flops | bytes accessed | tf_op | source)
XLA Modules:
  0.0 61.6 jit_solution(11156713650712580843)
XLA Ops:
  0.6 1.7 %shard_map.77 = (f32[64,512]{1,0:T(8,128)S(1)}, f32[64,1024]{1,0:T(8,128)S(1)}, bf16[1024,128]{1,0:T(8,128)(2,1)S(1)}, bf16[1024,128]{1,0:T(8,128)(2,1)S(1)}, f3...) custom-call(s32[64]{0:T(128)} %pos_hbm.1, bf16[1024,128]{1,0:T(8,128)(2,1)} %bitcast.8, bf16[1024,128]{1,0:T(8,128)(2,1)} %ik_hbm.1, ...), custom_call_target="tpu_custom_call" | custom-call | flops 134217728 | bytes 1179648 | tf_op jit(solution)/shard_map/pallas_call | solution.py:312
  2.9 1.2 %shard_map.78 = (f32[64,512]{1,0:T(8,128)S(1)}, bf16[768,576]{1,0:T(8,128)(2,1)S(1)}) custom-call(f32[64,1024]{1,0:T(8,128)S(1)} %get-tuple-element.37.bias_ref, bf16[1024,128]{1,0:T(8,128)(2,1)S(1)} %get-tuple-element.38.iq_ref, bf16[1024,128]{1,0:T(8,128)(2,1)S(1)} %get-tuple-element.39.ik_ref, f32[16,64]{1,0:T(8,128)S(1)} %get-tuple-element.40.w_ref, ...), custom_call_target="tpu_custom_call" | custom-call | flops 134217728 | bytes 2359296 | tf_op jit(solution)/shard_map/pallas_call | solution.py:349
  4.2 2.7 %collective-permute-start.1 = (f32[64,512]{1,0:T(8,128)S(1)}, f32[64,512]{1,0:T(8,128)S(1)}, u32[]{:S(2)}, u32[]{:S(2)}) collective-permute-start(f32[64,512]{1,0:T(8,128)S(1)} %add.21.mine_ref), channel_id=1, source_target_pairs={{0,2},{1,3},{2,0},{3,1},{4,6},{5,7},{6,4},{7,5},{8,10},{9,11},{10,... | collective-permute-start | bytes 393224 | tf_op jit(solution)/shard_map/ppermute | solution.py:309
  6.8 4.5 %shard_map.79 = (f32[2048,1024]{1,0:T(8,128)S(1)}, f32[32,128]{1,0:T(8,128)S(1)}) custom-call(f32[64,1024]{1,0:T(8,128)S(1)} %get-tuple-element.37.bias_ref, bf16[768,576]{1,0:T(8,128)(2,1)S(1)} %get-tuple-element.43.q_ref, bf16[2048,576]{1,0:T(8,128)(2,1)} %bitcast.6, bf16[576,1024]{1,0:T(8,128)(2,1)S(1)} %get-tuple-element.44.lat_ref), custom_call_target="tpu_custom_call" | custom-call | flops 2415919104 | bytes 2359296 | tf_op jit(solution)/shard_map/pallas_call | solution.py:359
  11.6 12.7 %all_to_all.5.all_ref = f32[8,24,128]{2,1,0:T(8,128)S(1)} all-to-all(f32[8,24,128]{2,1,0:T(8,128)S(1)} %broadcast_in_dim.3), channel_id=1, replica_groups=mesh['ctx'=8,'heads'=4] {'ctx'}, dimensions={0} | all-to-all | bytes 196608 | tf_op jit(solution)/shard_map/all_to_all | solution.py:375
  25.6 0.8 %collective-permute-done.2.other_ref = f32[72,512]{1,0:T(8,128)S(1)} collective-permute-done((f32[72,512]{1,0:T(8,128)S(1)}, f32[72,512]{1,0:T(8,128)S(1)}, u32[]{:S(2)}, u32[]{:S(2)}) %collective-permute-start.2) | collective-permute-done | bytes 147488 | tf_op jit(solution)/shard_map/ppermute | solution.py:309
  26.4 1.4 %collective-permute-start.3 = (f32[64,512]{1,0:T(8,128)S(1)}, f32[64,512]{1,0:T(8,128)S(1)}, u32[]{:S(2)}, u32[]{:S(2)}) collective-permute-start(f32[64,512]{1,0:T(8,128)S(1)} %slice_add_fusion), channel_id=1, source_target_pairs={{0,2},{1,3},{2,0},{3,1},{4,6},{5,7},{6,4},{7,5},{8,10},{9,11},{10,... | collective-permute-start | bytes 393224 | tf_op jit(solution)/shard_map/ppermute | solution.py:309
  27.8 0.7 %shard_map.84 = (f32[1024,1024]{1,0:T(8,128)S(1)}, bf16[128,1024]{1,0:T(8,128)(2,1)S(1)}) custom-call(bf16[1024,128]{1,0:T(8,128)(2,1)S(1)} %get-tuple-element.38.iq_ref, bf16[1024,128]{1,0:T(8,128)(2,1)S(1)} %get-tuple-element.39.ik_ref, f32[16,64]{1,0:T(8,128)S(1)} %get-tuple-element.40.w_ref), custom_call_target="tpu_custom_call" | custom-call | flops 268435456 | tf_op jit(solution)/shard_map/pallas_call | solution.py:396
  28.8 3.2 %collective-permute-done.3 = f32[64,512]{1,0:T(8,128)S(1)} collective-permute-done((f32[64,512]{1,0:T(8,128)S(1)}, f32[64,512]{1,0:T(8,128)S(1)}, u32[]{:S(2)}, u32[]{:S(2)}) %collective-permute-start.3) | collective-permute-done | bytes 131104 | tf_op jit(solution)/shard_map/ppermute | solution.py:309
  32.7 0.8 %collective-permute-done.4.g_ref = f32[64,512]{1,0:T(8,128)S(1)} collective-permute-done((f32[64,512]{1,0:T(8,128)S(1)}, f32[64,512]{1,0:T(8,128)S(1)}, u32[]{:S(2)}, u32[]{:S(2)}) %collective-permute-start.4) | collective-permute-done | bytes 131104 | tf_op jit(solution)/shard_map/ppermute | solution.py:309
  33.7 0.8 %collective-permute-start.7 = (f32[256,128]{1,0:T(8,128)S(1)}, f32[256,128]{1,0:T(8,128)S(1)}, u32[]{:S(2)}, u32[]{:S(2)}) collective-permute-start(f32[256,128]{1,0:T(8,128)S(1)} %get-tuple-element.63), channel_id=1, source_target_pairs={{0,12},{4,8},{8,4},{12,0},{16,28},{20,24},{24,20},{28,16},{1,13},{... | collective-permute-start | bytes 393224 | tf_op jit(solution)/shard_map/ppermute | solution.py:309
  34.7 1.1 %collective-permute-start.6 = (f32[256,128]{1,0:T(8,128)S(1)}, f32[256,128]{1,0:T(8,128)S(1)}, u32[]{:S(2)}, u32[]{:S(2)}) collective-permute-start(f32[256,128]{1,0:T(8,128)S(1)} %get-tuple-element.62), channel_id=1, source_target_pairs={{0,8},{4,12},{8,0},{12,4},{16,24},{20,28},{24,16},{28,20},{1,9},{5... | collective-permute-start | bytes 393224 | tf_op jit(solution)/shard_map/ppermute | solution.py:309
  36.1 1.8 %collective-permute-start.5 = (f32[256,128]{1,0:T(8,128)S(1)}, f32[256,128]{1,0:T(8,128)S(1)}, u32[]{:S(2)}, u32[]{:S(2)}) collective-permute-start(f32[256,128]{1,0:T(8,128)S(1)} %get-tuple-element.61), channel_id=1, source_target_pairs={{0,4},{4,0},{8,12},{12,8},{16,20},{20,16},{24,28},{28,24},{1,5},{5... | collective-permute-start | bytes 393224 | tf_op jit(solution)/shard_map/ppermute | solution.py:309
  38.2 2.9 %collective-permute-done.7 = f32[256,128]{1,0:T(8,128)S(1)} collective-permute-done((f32[256,128]{1,0:T(8,128)S(1)}, f32[256,128]{1,0:T(8,128)S(1)}, u32[]{:S(2)}, u32[]{:S(2)}) %collective-permute-start.7) | collective-permute-done | bytes 131104 | tf_op jit(solution)/shard_map/ppermute | solution.py:309
  41.1 0.8 %collective-permute-done.6 = f32[256,128]{1,0:T(8,128)S(1)} collective-permute-done((f32[256,128]{1,0:T(8,128)S(1)}, f32[256,128]{1,0:T(8,128)S(1)}, u32[]{:S(2)}, u32[]{:S(2)}) %collective-permute-start.6) | collective-permute-done | bytes 131104 | tf_op jit(solution)/shard_map/ppermute | solution.py:309
  41.9 1.2 %collective-permute-done.5 = f32[256,128]{1,0:T(8,128)S(1)} collective-permute-done((f32[256,128]{1,0:T(8,128)S(1)}, f32[256,128]{1,0:T(8,128)S(1)}, u32[]{:S(2)}, u32[]{:S(2)}) %collective-permute-start.5) | collective-permute-done | bytes 131104 | tf_op jit(solution)/shard_map/ppermute | solution.py:309
  43.9 1.4 %collective-permute-start.13 = (f32[256,128]{1,0:T(8,128)S(1)}, f32[256,128]{1,0:T(8,128)S(1)}, u32[]{:S(2)}, u32[]{:S(2)}) collective-permute-start(f32[256,128]{1,0:T(8,128)S(1)} %get-tuple-element.68), channel_id=1, source_target_pairs={{0,2},{1,3},{2,0},{3,1},{4,6},{5,7},{6,4},{7,5},{8,10},{9,11},{10,... | collective-permute-start | bytes 393224 | tf_op jit(solution)/shard_map/ppermute | solution.py:309
  45.7 5.5 %collective-permute-done.8 = f32[256,128]{1,0:T(8,128)S(1)} collective-permute-done((f32[256,128]{1,0:T(8,128)S(1)}, f32[256,128]{1,0:T(8,128)S(1)}, u32[]{:S(2)}, u32[]{:S(2)}) %collective-permute-start.8) | collective-permute-done | bytes 131104 | tf_op jit(solution)/shard_map/ppermute | solution.py:309
  51.3 0.9 %collective-permute-start.9 = (f32[256,128]{1,0:T(8,128)S(1)}, f32[256,128]{1,0:T(8,128)S(1)}, u32[]{:S(2)}, u32[]{:S(2)}) collective-permute-start(f32[256,128]{1,0:T(8,128)S(1)} %add.27.refs_0_), channel_id=1, source_target_pairs={{0,4},{4,0},{8,12},{12,8},{16,20},{20,16},{24,28},{28,24},{1,5},{5... | collective-permute-start | bytes 393224 | tf_op jit(solution)/shard_map/ppermute | solution.py:309
  52.2 2.6 %collective-permute-start.11 = (f32[256,128]{1,0:T(8,128)S(1)}, f32[256,128]{1,0:T(8,128)S(1)}, u32[]{:S(2)}, u32[]{:S(2)}) collective-permute-start(f32[256,128]{1,0:T(8,128)S(1)} %add.27.refs_0_), channel_id=1, source_target_pairs={{0,12},{4,8},{8,4},{12,0},{16,28},{20,24},{24,20},{28,16},{1,13},{... | collective-permute-start | bytes 393224 | tf_op jit(solution)/shard_map/ppermute | solution.py:309
  54.8 2.0 %collective-permute-done.9.refs_1_ = f32[256,128]{1,0:T(8,128)S(1)} collective-permute-done((f32[256,128]{1,0:T(8,128)S(1)}, f32[256,128]{1,0:T(8,128)S(1)}, u32[]{:S(2)}, u32[]{:S(2)}) %collective-permute-start.9) | collective-permute-done | bytes 131104 | tf_op jit(solution)/shard_map/ppermute | solution.py:309
  56.8 1.4 %collective-permute-done.10.refs_2_ = f32[256,128]{1,0:T(8,128)S(1)} collective-permute-done((f32[256,128]{1,0:T(8,128)S(1)}, f32[256,128]{1,0:T(8,128)S(1)}, u32[]{:S(2)}, u32[]{:S(2)}) %collective-permute-start.10) | collective-permute-done | bytes 131104 | tf_op jit(solution)/shard_map/ppermute | solution.py:309
  58.2 2.5 %collective-permute-done.11.refs_3_ = f32[256,128]{1,0:T(8,128)S(1)} collective-permute-done((f32[256,128]{1,0:T(8,128)S(1)}, f32[256,128]{1,0:T(8,128)S(1)}, u32[]{:S(2)}, u32[]{:S(2)}) %collective-permute-start.11) | collective-permute-done | bytes 131104 | tf_op jit(solution)/shard_map/ppermute | solution.py:309
  60.7 0.9 %shard_map.91 = (f32[1024,128]{1,0:T(8,128)}, f32[256,128]{1,0:T(8,128)}) custom-call(f32[256,128]{1,0:T(8,128)S(1)} %add.27.refs_0_, f32[256,128]{1,0:T(8,128)S(1)} %collective-permute-done.9.refs_1_, f32[256,128]{1,0:T(8,128)S(1)} %collective-permute-done.10.refs_2_, f32[256,128]{1,0:T(8,128)S(1)} %collective-permute-done.11.refs_3_, ...), custom_call_target="tpu_custom_call" | custom-call | tf_op jit(solution)/shard_map/pallas_call | solution.py:440
  (28 shorter events, 5.4 us)
Async XLA Ops:
  2.3 1.8 %collective-permute-start = (f32[64,512]{1,0:T(8,128)S(1)}, f32[64,512]{1,0:T(8,128)S(1)}, u32[]{:S(2)}, u32[]{:S(2)}) collective-permute-start(f32[64,512]{1,0:T(8,128)S(1)} %get-tuple-element.42), channel_id=1, source_target_pairs={{0,1},{1,0},{2,3},{3,2},{4,5},{5,4},{6,7},{7,6},{8,9},{9,8},{10,11... | collective-permute-start | bytes 393224 | tf_op jit(solution)/shard_map/ppermute | solution.py:309
  4.2 7.2 %collective-permute-start.1 = (f32[64,512]{1,0:T(8,128)S(1)}, f32[64,512]{1,0:T(8,128)S(1)}, u32[]{:S(2)}, u32[]{:S(2)}) collective-permute-start(f32[64,512]{1,0:T(8,128)S(1)} %add.21.mine_ref), channel_id=1, source_target_pairs={{0,2},{1,3},{2,0},{3,1},{4,6},{5,7},{6,4},{7,5},{8,10},{9,11},{10,... | collective-permute-start | bytes 393224 | tf_op jit(solution)/shard_map/ppermute | solution.py:309
  24.9 1.4 %collective-permute-start.2 = (f32[72,512]{1,0:T(8,128)S(1)}, f32[72,512]{1,0:T(8,128)S(1)}, u32[]{:S(2)}, u32[]{:S(2)}) collective-permute-start(f32[72,512]{1,0:T(8,128)S(1)} %get-tuple-element.49), channel_id=1, source_target_pairs={{0,1},{1,0},{2,3},{3,2},{4,5},{5,4},{6,7},{7,6},{8,9},{9,8},{10,11... | collective-permute-start | bytes 442376 | tf_op jit(solution)/shard_map/ppermute | solution.py:309
  26.4 5.6 %collective-permute-start.3 = (f32[64,512]{1,0:T(8,128)S(1)}, f32[64,512]{1,0:T(8,128)S(1)}, u32[]{:S(2)}, u32[]{:S(2)}) collective-permute-start(f32[64,512]{1,0:T(8,128)S(1)} %slice_add_fusion), channel_id=1, source_target_pairs={{0,2},{1,3},{2,0},{3,1},{4,6},{5,7},{6,4},{7,5},{8,10},{9,11},{10,... | collective-permute-start | bytes 393224 | tf_op jit(solution)/shard_map/ppermute | solution.py:309
  32.1 1.4 %collective-permute-start.4 = (f32[64,512]{1,0:T(8,128)S(1)}, f32[64,512]{1,0:T(8,128)S(1)}, u32[]{:S(2)}, u32[]{:S(2)}) collective-permute-start(f32[64,512]{1,0:T(8,128)S(1)} %subtract_multiply_fusion.g_ref), channel_id=1, source_target_pairs={{0,1},{1,0},{2,3},{3,2},{4,5},{5,4},{6,7},{7,6},{8,9},{9,8},{10,11... | collective-permute-start | bytes 393224 | tf_op jit(solution)/shard_map/ppermute | solution.py:309
  33.7 7.3 %collective-permute-start.7 = (f32[256,128]{1,0:T(8,128)S(1)}, f32[256,128]{1,0:T(8,128)S(1)}, u32[]{:S(2)}, u32[]{:S(2)}) collective-permute-start(f32[256,128]{1,0:T(8,128)S(1)} %get-tuple-element.63), channel_id=1, source_target_pairs={{0,12},{4,8},{8,4},{12,0},{16,28},{20,24},{24,20},{28,16},{1,13},{... | collective-permute-start | bytes 393224 | tf_op jit(solution)/shard_map/ppermute | solution.py:309
  34.7 7.1 %collective-permute-start.6 = (f32[256,128]{1,0:T(8,128)S(1)}, f32[256,128]{1,0:T(8,128)S(1)}, u32[]{:S(2)}, u32[]{:S(2)}) collective-permute-start(f32[256,128]{1,0:T(8,128)S(1)} %get-tuple-element.62), channel_id=1, source_target_pairs={{0,8},{4,12},{8,0},{12,4},{16,24},{20,28},{24,16},{28,20},{1,9},{5... | collective-permute-start | bytes 393224 | tf_op jit(solution)/shard_map/ppermute | solution.py:309
  36.1 6.9 %collective-permute-start.5 = (f32[256,128]{1,0:T(8,128)S(1)}, f32[256,128]{1,0:T(8,128)S(1)}, u32[]{:S(2)}, u32[]{:S(2)}) collective-permute-start(f32[256,128]{1,0:T(8,128)S(1)} %get-tuple-element.61), channel_id=1, source_target_pairs={{0,4},{4,0},{8,12},{12,8},{16,20},{20,16},{24,28},{28,24},{1,5},{5... | collective-permute-start | bytes 393224 | tf_op jit(solution)/shard_map/ppermute | solution.py:309
  43.1 8.2 %collective-permute-start.8 = (f32[256,128]{1,0:T(8,128)S(1)}, f32[256,128]{1,0:T(8,128)S(1)}, u32[]{:S(2)}, u32[]{:S(2)}) collective-permute-start(f32[256,128]{1,0:T(8,128)S(1)} %add_add_fusion), channel_id=1, source_target_pairs={{0,16},{4,20},{8,24},{12,28},{16,0},{20,4},{24,8},{28,12},{1,17},{... | collective-permute-start | bytes 393224 | tf_op jit(solution)/shard_map/ppermute | solution.py:309
  43.8 8.4 %collective-permute-start.12 = (f32[256,128]{1,0:T(8,128)S(1)}, f32[256,128]{1,0:T(8,128)S(1)}, u32[]{:S(2)}, u32[]{:S(2)}) collective-permute-start(f32[256,128]{1,0:T(8,128)S(1)} %get-tuple-element.67), channel_id=1, source_target_pairs={{0,1},{1,0},{2,3},{3,2},{4,5},{5,4},{6,7},{7,6},{8,9},{9,8},{10,11... | collective-permute-start | bytes 393224 | tf_op jit(solution)/shard_map/ppermute | solution.py:309
  43.9 10.9 %collective-permute-start.13 = (f32[256,128]{1,0:T(8,128)S(1)}, f32[256,128]{1,0:T(8,128)S(1)}, u32[]{:S(2)}, u32[]{:S(2)}) collective-permute-start(f32[256,128]{1,0:T(8,128)S(1)} %get-tuple-element.68), channel_id=1, source_target_pairs={{0,2},{1,3},{2,0},{3,1},{4,6},{5,7},{6,4},{7,5},{8,10},{9,11},{10,... | collective-permute-start | bytes 393224 | tf_op jit(solution)/shard_map/ppermute | solution.py:309
  45.3 9.5 %collective-permute-start.14 = (f32[256,128]{1,0:T(8,128)S(1)}, f32[256,128]{1,0:T(8,128)S(1)}, u32[]{:S(2)}, u32[]{:S(2)}) collective-permute-start(f32[256,128]{1,0:T(8,128)S(1)} %get-tuple-element.69), channel_id=1, source_target_pairs={{0,3},{1,2},{2,1},{3,0},{4,7},{5,6},{6,5},{7,4},{8,11},{9,10},{10,... | collective-permute-start | bytes 393224 | tf_op jit(solution)/shard_map/ppermute | solution.py:309
  51.3 5.5 %collective-permute-start.9 = (f32[256,128]{1,0:T(8,128)S(1)}, f32[256,128]{1,0:T(8,128)S(1)}, u32[]{:S(2)}, u32[]{:S(2)}) collective-permute-start(f32[256,128]{1,0:T(8,128)S(1)} %add.27.refs_0_), channel_id=1, source_target_pairs={{0,4},{4,0},{8,12},{12,8},{16,20},{20,16},{24,28},{28,24},{1,5},{5... | collective-permute-start | bytes 393224 | tf_op jit(solution)/shard_map/ppermute | solution.py:309
  52.2 6.0 %collective-permute-start.10 = (f32[256,128]{1,0:T(8,128)S(1)}, f32[256,128]{1,0:T(8,128)S(1)}, u32[]{:S(2)}, u32[]{:S(2)}) collective-permute-start(f32[256,128]{1,0:T(8,128)S(1)} %add.27.refs_0_), channel_id=1, source_target_pairs={{0,8},{4,12},{8,0},{12,4},{16,24},{20,28},{24,16},{28,20},{1,9},{5... | collective-permute-start | bytes 393224 | tf_op jit(solution)/shard_map/ppermute | solution.py:309
  52.2 8.5 %collective-permute-start.11 = (f32[256,128]{1,0:T(8,128)S(1)}, f32[256,128]{1,0:T(8,128)S(1)}, u32[]{:S(2)}, u32[]{:S(2)}) collective-permute-start(f32[256,128]{1,0:T(8,128)S(1)} %add.27.refs_0_), channel_id=1, source_target_pairs={{0,12},{4,8},{8,4},{12,0},{16,28},{20,24},{24,20},{28,16},{1,13},{... | collective-permute-start | bytes 393224 | tf_op jit(solution)/shard_map/ppermute | solution.py:309
